TPU v7x, 32 devices: a whole 2x2x4 slice. The times are simulated.
32 devices in a mesh: dp: 8 (over z, y), tensor: 4 (over x, core).
Axes of the slice: x: 2, y: 2, z: 4, core: 2. Of those that a mesh axis runs over, the one named last changes fastest.
Arguments:
- tokens: bfloat16 [32768, 1024], P(('dp', 'tensor')), may hold values from -6 to 6
- lengths: int32 [16], P('dp'), may hold values from 1 to 2048, as said below
- gain_first: float32 [1024], replicated, may hold values from 0.25 to 1.75
- shift_first: float32 [1024], replicated, may hold values from -3 to 3
- query_weight: bfloat16 [1024, 1024], P(None, 'tensor'), may hold values from -0.1875 to 0.1875
- key_weight: bfloat16 [1024, 1024], P(None, 'tensor'), may hold values from -0.1875 to 0.1875
- value_weight: bfloat16 [1024, 1024], P(None, 'tensor'), may hold values from -0.1875 to 0.1875
- output_weight: bfloat16 [1024, 1024], P('tensor'), may hold values from -3 to 3
- gain_second: float32 [1024], replicated, may hold values from 0.25 to 1.75
- shift_second: float32 [1024], replicated, may hold values from -3 to 3
- gate_weight: bfloat16 [1024, 4096], P(None, 'tensor'), may hold values from -0.1875 to 0.1875
- up_weight: bfloat16 [1024, 4096], P(None, 'tensor'), may hold values from -0.1875 to 0.1875
- down_weight: bfloat16 [4096, 1024], P('tensor'), may hold values from -0.09375 to 0.09375
- cotangent: bfloat16 [32768, 1024], P(('dp', 'tensor')), may hold values from -6 to 6
Outputs:
- output: bfloat16 [32768, 1024], P(('dp', 'tensor'))
- input_grad: bfloat16 [32768, 1024], P(('dp', 'tensor'))
- grad_query: float32 [1024, 1024], P(None, 'tensor')
- grad_key: float32 [1024, 1024], P(None, 'tensor')
- grad_value: float32 [1024, 1024], P(None, 'tensor')
- grad_output: float32 [1024, 1024], P('tensor')
- grad_gate: float32 [1024, 4096], P(None, 'tensor')
- grad_up: float32 [1024, 4096], P(None, 'tensor')
- grad_down: float32 [4096, 1024], P('tensor')
- grad_gain_first: float32 [1024], replicated
- grad_shift_first: float32 [1024], replicated
- grad_gain_second: float32 [1024], replicated
- grad_shift_second: float32 [1024], replicated
Inputs may be any that keep to these rules, and one draw needn't show every extreme that they name: `lengths`: real tokens of each window, from position 0; window 0 is full (2048); the last window holds at most 1024.
All inputs are finite; a program needn't handle non-finite values.
Results may differ from a plain program's by a relative error of at most 0.015.
Values may be sent and summed in bfloat16 or wider, within the bound.
No kernel may reach another device: no remote copies, remote signals or barrier semaphores. Data moves between devices by JAX's collectives and lax.ppermute only.
A program may use at most 256 MiB of HBM per device.

v0:
```python
import math

import jax
import jax.numpy as jnp
from jax import lax
from jax.sharding import PartitionSpec as P

HD = 64
LEN = 2048
QBLK = 512


EPSILON = 1e-05
MASKED = -1e30


def layer_stats(inputs, norm_gain, norm_shift):
    row_mean = jnp.mean(inputs, axis=-1, keepdims=True)
    centred = inputs - row_mean
    row_scale = lax.rsqrt(jnp.mean(centred * centred, axis=-1, keepdims=True) + EPSILON)
    standard = centred * row_scale
    return (standard * norm_gain + norm_shift, standard, row_scale)


def layer_back(upstream, norm_gain, standard, row_scale):
    scaled = upstream * norm_gain
    return row_scale * (
        scaled
        - jnp.mean(scaled, axis=-1, keepdims=True)
        - standard * jnp.mean(scaled * standard, axis=-1, keepdims=True)
    )


def rope_tables(length, head_width):
    position = jnp.arange(length, dtype=jnp.float32)
    inverse = 10000.0 ** (-2.0 * jnp.arange(head_width // 2, dtype=jnp.float32) / head_width)
    angles = position[:, None] * inverse[None, :]
    return (jnp.cos(angles), jnp.sin(angles))


def rotate(tensor, cosines, sines):
    half_width = tensor.shape[-1] // 2
    front_half = tensor[..., :half_width]
    back_half = tensor[..., half_width:]
    return jnp.concatenate(
        [front_half * cosines - back_half * sines, front_half * sines + back_half * cosines],
        axis=-1,
    )


def rotate_back(upstream, cosines, sines):
    half_width = upstream.shape[-1] // 2
    front_half = upstream[..., :half_width]
    back_half = upstream[..., half_width:]
    return jnp.concatenate(
        [front_half * cosines + back_half * sines, back_half * cosines - front_half * sines],
        axis=-1,
    )


def to_heads(matrix, windows, heads_dev):
    return (
        matrix.reshape(windows, LEN, heads_dev, HD)
        .transpose(0, 2, 1, 3)
        .reshape(windows * heads_dev, LEN, HD)
    )


def from_heads(stacked, windows, heads_dev):
    return (
        stacked.reshape(windows, heads_dev, LEN, HD)
        .transpose(0, 2, 1, 3)
        .reshape(windows * LEN, heads_dev * HD)
    )


def contract_rows(left, right):
    return lax.dot_general(
        left, right, (((0,), (0,)), ((), ())), preferred_element_type=jnp.float32
    )


def times_transposed(left, right):
    return lax.dot_general(
        left, right, (((1,), (1,)), ((), ())), preferred_element_type=jnp.float32
    )


def attend(pieces):
    query_item, key_item, value_item, length = pieces
    factor = 1.0 / math.sqrt(HD)
    key_valid = jnp.arange(LEN) < length

    def one_block(query_block):
        scores = times_transposed(query_block, key_item) * factor
        scores = jnp.where(key_valid[None, :], scores, MASKED)
        row_max = jnp.max(scores, axis=-1, keepdims=True)
        weights = jnp.exp(scores - row_max)
        totals = jnp.sum(weights, axis=-1, keepdims=True)
        probs = (weights / totals).astype(jnp.bfloat16)
        mixed = jnp.dot(probs, value_item, preferred_element_type=jnp.float32)
        return (mixed, (row_max + jnp.log(totals))[:, 0])

    mixed, log_totals = lax.map(one_block, query_item.reshape(LEN // QBLK, QBLK, HD))
    return (mixed.reshape(LEN, HD), log_totals.reshape(LEN))


def attend_back(pieces):
    query_item, key_item, value_item, upstream, log_totals, length = pieces
    factor = 1.0 / math.sqrt(HD)
    key_valid = jnp.arange(LEN) < length

    def one_block(carry, block):
        key_total, value_total = carry
        query_block, grad_block, total_block = block
        scores = times_transposed(query_block, key_item) * factor
        scores = jnp.where(key_valid[None, :], scores, MASKED)
        probs = jnp.exp(scores - total_block[:, None])
        grad_probs = times_transposed(grad_block, value_item)
        row_dot = jnp.sum(probs * grad_probs, axis=-1, keepdims=True)
        grad_scores = (probs * (grad_probs - row_dot)).astype(jnp.bfloat16)
        grad_query = jnp.dot(grad_scores, key_item, preferred_element_type=jnp.float32) * factor
        key_total = key_total + contract_rows(grad_scores, query_block) * factor
        value_total = value_total + contract_rows(probs.astype(jnp.bfloat16), grad_block)
        return ((key_total, value_total), grad_query)

    starting = jnp.zeros((LEN, HD), jnp.float32)
    blocks = LEN // QBLK
    (key_total, value_total), grad_query = lax.scan(
        one_block,
        (starting, starting),
        (
            query_item.reshape(blocks, QBLK, HD),
            upstream.reshape(blocks, QBLK, HD),
            log_totals.reshape(blocks, QBLK),
        ),
    )
    return (grad_query.reshape(LEN, HD), key_total, value_total)


def shards(
    tokens,
    lengths,
    gain_first,
    shift_first,
    query_weight,
    key_weight,
    value_weight,
    output_weight,
    gain_second,
    shift_second,
    gate_weight,
    up_weight,
    down_weight,
    cotangent,
):
    head_cols = query_weight.shape[1]
    heads_dev = head_cols // HD
    windows = lengths.shape[0]
    ff_dev = gate_weight.shape[1]
    cosines, sines = rope_tables(LEN, HD)
    weight_qkv = jnp.concatenate([query_weight, key_weight, value_weight], axis=1)
    weight_gu = jnp.concatenate([gate_weight, up_weight], axis=1)
    head_lengths = jnp.repeat(lengths, heads_dev)
    inputs = tokens.astype(jnp.float32)
    normed_one, standard_one, scale_one = layer_stats(inputs, gain_first, shift_first)
    low_one = normed_one.astype(jnp.bfloat16)
    full_one = lax.all_gather(low_one, "tensor", axis=0, tiled=True)
    qkv_rows = jnp.dot(full_one, weight_qkv, preferred_element_type=jnp.float32)
    queries = rotate(to_heads(qkv_rows[:, :head_cols], windows, heads_dev), cosines, sines).astype(
        jnp.bfloat16
    )
    keys = rotate(
        to_heads(qkv_rows[:, head_cols : 2 * head_cols], windows, heads_dev), cosines, sines
    ).astype(jnp.bfloat16)
    values = to_heads(qkv_rows[:, 2 * head_cols :], windows, heads_dev).astype(jnp.bfloat16)
    attended, log_totals = lax.map(attend, (queries, keys, values, head_lengths))
    mixed_rows = from_heads(attended, windows, heads_dev).astype(jnp.bfloat16)
    mixer_sum = lax.psum_scatter(
        jnp.dot(mixed_rows, output_weight, preferred_element_type=jnp.float32),
        "tensor",
        scatter_dimension=0,
        tiled=True,
    )
    hidden_one = inputs + mixer_sum
    normed_two, standard_two, scale_two = layer_stats(hidden_one, gain_second, shift_second)
    low_two = normed_two.astype(jnp.bfloat16)
    full_two = lax.all_gather(low_two, "tensor", axis=0, tiled=True)
    gu_rows = jnp.dot(full_two, weight_gu, preferred_element_type=jnp.float32)
    gate_pre = gu_rows[:, :ff_dev]
    up_pre = gu_rows[:, ff_dev:]
    sigmoid_gate = jax.nn.sigmoid(gate_pre)
    activated = gate_pre * sigmoid_gate
    inner = (activated * up_pre).astype(jnp.bfloat16)
    feed_sum = lax.psum_scatter(
        jnp.dot(inner, down_weight, preferred_element_type=jnp.float32).astype(jnp.bfloat16),
        "tensor",
        scatter_dimension=0,
        tiled=True,
    ).astype(jnp.float32)
    output = (hidden_one + feed_sum).astype(jnp.bfloat16)
    target = lax.all_gather(cotangent, "tensor", axis=0, tiled=True)
    grad_inner = times_transposed(target, down_weight)
    grad_down = contract_rows(inner, target)
    grad_upx = (grad_inner * activated).astype(jnp.bfloat16)
    grad_gatex = (
        grad_inner * up_pre * sigmoid_gate * (1.0 + gate_pre * (1.0 - sigmoid_gate))
    ).astype(jnp.bfloat16)
    grad_gu = jnp.concatenate([grad_gatex, grad_upx], axis=1)
    grad_two = lax.psum_scatter(
        times_transposed(grad_gu, weight_gu), "tensor", scatter_dimension=0, tiled=True
    )
    grad_gu_weight = contract_rows(full_two, grad_gu)
    grad_hidden = cotangent.astype(jnp.float32) + layer_back(
        grad_two, gain_second, standard_two, scale_two
    )
    gain_two_part = jnp.sum(grad_two * standard_two, axis=0)
    shift_two_part = jnp.sum(grad_two, axis=0)
    grad_branch = lax.all_gather(grad_hidden.astype(jnp.bfloat16), "tensor", axis=0, tiled=True)
    grad_output = contract_rows(mixed_rows, grad_branch)
    grad_mixed = times_transposed(grad_branch, output_weight).astype(jnp.bfloat16)
    grad_heads = to_heads(grad_mixed, windows, heads_dev)
    grad_queries, grad_keys, grad_values = lax.map(
        attend_back, (queries, keys, values, grad_heads, log_totals, head_lengths)
    )
    grad_qx = from_heads(rotate_back(grad_queries, cosines, sines), windows, heads_dev).astype(
        jnp.bfloat16
    )
    grad_kx = from_heads(rotate_back(grad_keys, cosines, sines), windows, heads_dev).astype(
        jnp.bfloat16
    )
    grad_vx = from_heads(grad_values, windows, heads_dev).astype(jnp.bfloat16)
    grad_qkv = jnp.concatenate([grad_qx, grad_kx, grad_vx], axis=1)
    grad_one = lax.psum_scatter(
        times_transposed(grad_qkv, weight_qkv), "tensor", scatter_dimension=0, tiled=True
    )
    grad_qkv_weight = contract_rows(full_one, grad_qkv)
    input_grad = (grad_hidden + layer_back(grad_one, gain_first, standard_one, scale_one)).astype(
        jnp.bfloat16
    )
    gain_one_part = jnp.sum(grad_one * standard_one, axis=0)
    shift_one_part = jnp.sum(grad_one, axis=0)
    norm_sums = lax.psum(
        (gain_one_part, shift_one_part, gain_two_part, shift_two_part), ("dp", "tensor")
    )
    weight_sums = (
        lax.psum(grad_qkv_weight[:, :head_cols].astype(jnp.bfloat16), "dp").astype(jnp.float32),
        lax.psum(grad_qkv_weight[:, head_cols : 2 * head_cols].astype(jnp.bfloat16), "dp").astype(
            jnp.float32
        ),
        lax.psum(grad_qkv_weight[:, 2 * head_cols :].astype(jnp.bfloat16), "dp").astype(
            jnp.float32
        ),
        lax.psum(grad_output.astype(jnp.bfloat16), "dp").astype(jnp.float32),
        lax.psum(grad_gu_weight[:, :ff_dev].astype(jnp.bfloat16), "dp").astype(jnp.float32),
        lax.psum(grad_gu_weight[:, ff_dev:].astype(jnp.bfloat16), "dp").astype(jnp.float32),
        lax.psum(grad_down.astype(jnp.bfloat16), "dp").astype(jnp.float32),
    )
    return (
        output,
        input_grad,
        weight_sums[0],
        weight_sums[1],
        weight_sums[2],
        weight_sums[3],
        weight_sums[4],
        weight_sums[5],
        weight_sums[6],
        norm_sums[0],
        norm_sums[1],
        norm_sums[2],
        norm_sums[3],
    )


def solution(mesh):
    return jax.shard_map(
        shards,
        mesh=mesh,
        in_specs=(
            P(("dp", "tensor"), None),
            P("dp"),
            P(),
            P(),
            P(None, "tensor"),
            P(None, "tensor"),
            P(None, "tensor"),
            P("tensor", None),
            P(),
            P(),
            P(None, "tensor"),
            P(None, "tensor"),
            P("tensor", None),
            P(("dp", "tensor"), None),
        ),
        out_specs=(
            P(("dp", "tensor"), None),
            P(("dp", "tensor"), None),
            P(None, "tensor"),
            P(None, "tensor"),
            P(None, "tensor"),
            P("tensor", None),
            P(None, "tensor"),
            P(None, "tensor"),
            P("tensor", None),
            P(),
            P(),
            P(),
            P(),
        ),
        check_vma=False,
    )
```

profile of v0, /device:TPU:0, one launch (start us, length us, event | category | flops | bytes accessed | tf_op | source)
XLA Modules:
  0.0 2065.5 jit_solution(4024489934945331752)
XLA Ops:
  19.5 56.2 %all-gather.5.cloned.1.call-done = bf16[4096,1024]{1,0:T(8,128)(2,1)} async-done(((bf16[1024,1024]{1,0:T(8,128)(2,1)}), bf16[4096,1024]{1,0:T(8,128)(2,1)}) %all-gather.5.cloned.1.call-update) | async-done | bytes 8388624 | tf_op jit(solution)/shard_map/all_gather | solution.py:168
  155.8 304.9 %while.55 = (s32[]{:T(128)}, bf16[8,2048,64]{2,1,0:T(8,128)(2,1)}, f32[8,2048]{1,0:T(8,128)}, bf16[8,2048,64]{2,1,0:T(8,128)(2,1)}, bf16[8,2048,64]{2,1,0:T(8,12...) while((s32[]{:T(128)}, bf16[8,2048,64]{2,1,0:T(8,128)(2,1)}, ...), condition=%wide.region_7.8_spmd, body=%wide.region_2.7_spmd.sunk | while | flops 281019904 | bytes 33354588 | solution.py:177
  197.6 31.7 %while.58 = (s32[]{:T(128)}, bf16[4,512,64]{1,2,0:T(8,128)(2,1)S(1)}, f32[4,512]{1,0:T(4,128)S(1)}, bf16[4,512,64]{2,1,0:T(8,128)(2,1)S(1)}, bf16[2048,64]{1,0:T...) while((s32[]{:T(128)}, bf16[4,512,64]{1,2,0:T(8,128)(2,1)S(1)}, ...), condition=%wide.region_6.6_spmd.clone, body=%wide.region_3.5_spmd.clone.sunk | while | flops 281019904 | bytes 30437512 | solution.py:104
  235.7 31.7 %while.58 = (s32[]{:T(128)}, bf16[4,512,64]{1,2,0:T(8,128)(2,1)S(1)}, f32[4,512]{1,0:T(4,128)S(1)}, bf16[4,512,64]{2,1,0:T(8,128)(2,1)S(1)}, bf16[2048,64]{1,0:T...) while((s32[]{:T(128)}, bf16[4,512,64]{1,2,0:T(8,128)(2,1)S(1)}, ...), condition=%wide.region_6.6_spmd.clone, body=%wide.region_3.5_spmd.clone.sunk | while | flops 281019904 | bytes 30437512 | solution.py:104
  273.8 31.7 %while.58 = (s32[]{:T(128)}, bf16[4,512,64]{1,2,0:T(8,128)(2,1)S(1)}, f32[4,512]{1,0:T(4,128)S(1)}, bf16[4,512,64]{2,1,0:T(8,128)(2,1)S(1)}, bf16[2048,64]{1,0:T...) while((s32[]{:T(128)}, bf16[4,512,64]{1,2,0:T(8,128)(2,1)S(1)}, ...), condition=%wide.region_6.6_spmd.clone, body=%wide.region_3.5_spmd.clone.sunk | while | flops 281019904 | bytes 30437512 | solution.py:104
  311.9 31.7 %while.58 = (s32[]{:T(128)}, bf16[4,512,64]{1,2,0:T(8,128)(2,1)S(1)}, f32[4,512]{1,0:T(4,128)S(1)}, bf16[4,512,64]{2,1,0:T(8,128)(2,1)S(1)}, bf16[2048,64]{1,0:T...) while((s32[]{:T(128)}, bf16[4,512,64]{1,2,0:T(8,128)(2,1)S(1)}, ...), condition=%wide.region_6.6_spmd.clone, body=%wide.region_3.5_spmd.clone.sunk | while | flops 281019904 | bytes 30437512 | solution.py:104
  350.1 31.7 %while.58 = (s32[]{:T(128)}, bf16[4,512,64]{1,2,0:T(8,128)(2,1)S(1)}, f32[4,512]{1,0:T(4,128)S(1)}, bf16[4,512,64]{2,1,0:T(8,128)(2,1)S(1)}, bf16[2048,64]{1,0:T...) while((s32[]{:T(128)}, bf16[4,512,64]{1,2,0:T(8,128)(2,1)S(1)}, ...), condition=%wide.region_6.6_spmd.clone, body=%wide.region_3.5_spmd.clone.sunk | while | flops 281019904 | bytes 30437512 | solution.py:104
  479.9 126.2 %reduce-scatter.5.cloned.1.call-done = f32[1024,1024]{1,0:T(8,128)} async-done(((f32[4096,1024]{1,0:T(8,128)}), f32[1024,1024]{1,0:T(8,128)}) %reduce-scatter.5.cloned.1.call-update) | async-done | bytes 4194320 | tf_op jit(solution)/shard_map/reduce_scatter | solution.py:179
  618.9 53.1 %all-gather.7.cloned.1.call-done = bf16[4096,1024]{1,0:T(8,128)(2,1)} async-done(((bf16[1024,1024]{1,0:T(8,128)(2,1)}), bf16[4096,1024]{1,0:T(8,128)(2,1)}) %all-gather.7.cloned.1.call-update) | async-done | bytes 8388624 | tf_op jit(solution)/shard_map/all_gather | solution.py:188
  697.7 34.1 %all-gather.9.cloned.1.call-done = bf16[4096,1024]{1,0:T(8,128)(2,1)} async-done(((bf16[1024,1024]{1,0:T(8,128)(2,1)}), bf16[4096,1024]{1,0:T(8,128)(2,1)}) %all-gather.9.cloned.1.call-update) | async-done | bytes 8388624 | tf_op jit(solution)/shard_map/all_gather | solution.py:202
  799.8 111.0 %reduce-scatter.9.cloned.1.call-done = f32[1024,1024]{1,0:T(8,128)} async-done(((f32[4096,1024]{1,0:T(8,128)}), f32[1024,1024]{1,0:T(8,128)}) %reduce-scatter.9.cloned.1.call-update) | async-done | bytes 4194320 | tf_op jit(solution)/shard_map/reduce_scatter | solution.py:210
  915.8 69.2 %reduce-scatter.7.cloned.1.call-done = bf16[1024,1024]{1,0:T(8,128)(2,1)} async-done(((bf16[4096,1024]{1,0:T(8,128)(2,1)}), bf16[1024,1024]{1,0:T(8,128)(2,1)}) %reduce-scatter.7.cloned.1.call-update) | async-done | bytes 2097168 | tf_op jit(solution)/shard_map/reduce_scatter | solution.py:195
  1067.0 507.6 %while.57 = (s32[]{:T(128)}, f32[8,2048,64]{1,2,0:T(8,128)}, f32[8,2048,64]{1,2,0:T(8,128)}, bf16[8,2048,64]{1,2,0:T(8,128)(2,1)}, bf16[8,2048,64]{2,1,0:T(8,128...) while((s32[]{:T(128)}, f32[8,2048,64]{1,2,0:T(8,128)}, ...), condition=%wide.region_19.20_spmd, body=%wide.region_15.19_spmd.sunk | while | flops 681215488 | bytes 76203976 | solution.py:223
  1075.4 50.6 %while.59 = (s32[]{:T(128)}, f32[2048,64]{0,1:T(8,128)}, f32[2048,64]{0,1:T(8,128)S(1)}, f32[4,512,64]{1,2,0:T(8,128)}, bf16[4,512,64]{2,1,0:T(8,128)(2,1)}, /*i...) while((s32[]{:T(128)}, f32[2048,64]{0,1:T(8,128)}, ...), condition=%wide.region_18.18_spmd.clone, body=%wide.region_16.17_spmd.clone.sunk | while | flops 681215488 | bytes 68829880 | solution.py:129
  1138.8 50.6 %while.59 = (s32[]{:T(128)}, f32[2048,64]{0,1:T(8,128)}, f32[2048,64]{0,1:T(8,128)S(1)}, f32[4,512,64]{1,2,0:T(8,128)}, bf16[4,512,64]{2,1,0:T(8,128)(2,1)}, /*i...) while((s32[]{:T(128)}, f32[2048,64]{0,1:T(8,128)}, ...), condition=%wide.region_18.18_spmd.clone, body=%wide.region_16.17_spmd.clone.sunk | while | flops 681215488 | bytes 68829880 | solution.py:129
  1202.2 50.6 %while.59 = (s32[]{:T(128)}, f32[2048,64]{0,1:T(8,128)}, f32[2048,64]{0,1:T(8,128)S(1)}, f32[4,512,64]{1,2,0:T(8,128)}, bf16[4,512,64]{2,1,0:T(8,128)(2,1)}, /*i...) while((s32[]{:T(128)}, f32[2048,64]{0,1:T(8,128)}, ...), condition=%wide.region_18.18_spmd.clone, body=%wide.region_16.17_spmd.clone.sunk | while | flops 681215488 | bytes 68829880 | solution.py:129
  1265.7 50.6 %while.59 = (s32[]{:T(128)}, f32[2048,64]{0,1:T(8,128)}, f32[2048,64]{0,1:T(8,128)S(1)}, f32[4,512,64]{1,2,0:T(8,128)}, bf16[4,512,64]{2,1,0:T(8,128)(2,1)}, /*i...) while((s32[]{:T(128)}, f32[2048,64]{0,1:T(8,128)}, ...), condition=%wide.region_18.18_spmd.clone, body=%wide.region_16.17_spmd.clone.sunk | while | flops 681215488 | bytes 68829880 | solution.py:129
  1329.1 50.6 %while.59 = (s32[]{:T(128)}, f32[2048,64]{0,1:T(8,128)}, f32[2048,64]{0,1:T(8,128)S(1)}, f32[4,512,64]{1,2,0:T(8,128)}, bf16[4,512,64]{2,1,0:T(8,128)(2,1)}, /*i...) while((s32[]{:T(128)}, f32[2048,64]{0,1:T(8,128)}, ...), condition=%wide.region_18.18_spmd.clone, body=%wide.region_16.17_spmd.clone.sunk | while | flops 681215488 | bytes 68829880 | solution.py:129
  1392.5 50.6 %while.59 = (s32[]{:T(128)}, f32[2048,64]{0,1:T(8,128)}, f32[2048,64]{0,1:T(8,128)S(1)}, f32[4,512,64]{1,2,0:T(8,128)}, bf16[4,512,64]{2,1,0:T(8,128)(2,1)}, /*i...) while((s32[]{:T(128)}, f32[2048,64]{0,1:T(8,128)}, ...), condition=%wide.region_18.18_spmd.clone, body=%wide.region_16.17_spmd.clone.sunk | while | flops 681215488 | bytes 68829880 | solution.py:129
  1455.9 50.6 %while.59 = (s32[]{:T(128)}, f32[2048,64]{0,1:T(8,128)}, f32[2048,64]{0,1:T(8,128)S(1)}, f32[4,512,64]{1,2,0:T(8,128)}, bf16[4,512,64]{2,1,0:T(8,128)(2,1)}, /*i...) while((s32[]{:T(128)}, f32[2048,64]{0,1:T(8,128)}, ...), condition=%wide.region_18.18_spmd.clone, body=%wide.region_16.17_spmd.clone.sunk | while | flops 681215488 | bytes 68829880 | solution.py:129
  1519.3 50.6 %while.59 = (s32[]{:T(128)}, f32[2048,64]{0,1:T(8,128)}, f32[2048,64]{0,1:T(8,128)S(1)}, f32[4,512,64]{1,2,0:T(8,128)}, bf16[4,512,64]{2,1,0:T(8,128)(2,1)}, /*i...) while((s32[]{:T(128)}, f32[2048,64]{0,1:T(8,128)}, ...), condition=%wide.region_18.18_spmd.clone, body=%wide.region_16.17_spmd.clone.sunk | while | flops 681215488 | bytes 68829880 | solution.py:129
  1619.5 262.1 %all-reduce.4.cloned.1.call-done = (bf16[1024,256]{1,0:T(8,128)(2,1)}, bf16[1024,256]{1,0:T(8,128)(2,1)}, bf16[1024,256]{1,0:T(8,128)(2,1)}, bf16[256,1024]{1,0:...) async-done(((bf16[1024,256]{1,0:T(8,128)(2,1)}, bf16[1024,256]{1,0:T(8,128)(2,1)}, bf16[1024,256]{1,0:T(8,128)(2,1)}, ...) | async-done | bytes 8388624 | tf_op jit(solution)/shard_map/psum | solution.py:247
  1895.5 113.7 %reduce-scatter.11.cloned.1.call-done = f32[1024,1024]{1,0:T(8,128)} async-done(((f32[4096,1024]{1,0:T(8,128)}), f32[1024,1024]{1,0:T(8,128)}) %reduce-scatter.11.cloned.1.call-update) | async-done | bytes 4194320 | tf_op jit(solution)/shard_map/reduce_scatter | solution.py:234
  2013.0 39.6 %all-reduce = (f32[1024]{0:T(1024)}, f32[1024]{0:T(1024)}, f32[1024]{0:T(1024)}, f32[1024]{0:T(1024)}) all-reduce(f32[1024]{0:T(1024)S(1)} %get-tuple-element.308, f32[1024]{0:T(1024)S(1)} %get-tuple-element.313, f32[1024]{0:T(1024)S(1)} %copy-done.35, f32[1024]{0:T(1024)S(1)} %copy-done.36), channel_id=1, replica_groups=mesh['dp'=8,'tensor'=4] {'dp','tensor'}, use_global_device_ids=true, to_apply=%region_31.32 | all-reduce | flops 4096 | bytes 32768 | tf_op jit(solution)/shard_map/psum | solution.py:243
  (1014 shorter events, 1276.7 us)
Async XLA Ops:
  7.2 724.6 %copy-start = (bf16[1024,1024]{1,0:T(8,128)(2,1)S(1)}, bf16[1024,1024]{1,0:T(8,128)(2,1)}, u32[]{:S(2)}) copy-start(bf16[1024,1024]{1,0:T(8,128)(2,1)} %param.34) | copy-start | bytes 6291460
  7.2 68.5 %all-gather.5.cloned.1.call-start = ((), (), s32[]{:S(2)}) async-start(), calls=%async_computation.4 | async-start | bytes 10485760 | tf_op jit(solution)/shard_map/all_gather | solution.py:168
  14.5 591.6 %reduce-scatter.5.cloned.1.call-start = ((), (), s32[]{:S(2)}) async-start(), calls=%async_computation.5 | async-start | bytes 20971520 | tf_op jit(solution)/shard_map/reduce_scatter | solution.py:179
  19.4 107.4 %copy-start.12 = (f32[2048,32]{0,1:T(8,128)}, f32[2048,32]{0,1:T(8,128)S(1)}, u32[]{:S(2)}) copy-start(f32[2048,32]{0,1:T(8,128)S(1)} %get-tuple-element.428) | copy-start | bytes 786436
  19.5 107.4 %copy-start.14 = (f32[2048,32]{0,1:T(8,128)}, f32[2048,32]{0,1:T(8,128)S(1)}, u32[]{:S(2)}) copy-start(f32[2048,32]{0,1:T(8,128)S(1)} %get-tuple-element.429) | copy-start | bytes 786436
  460.7 9.7 copy-start.40
  460.7 11.0 copy-start.20
  479.8 192.1 %all-gather.7.cloned.1.call-start = ((), (), s32[]{:S(2)}) async-start(), calls=%async_computation.6 | async-start | bytes 10485760 | tf_op jit(solution)/shard_map/all_gather | solution.py:188
  613.5 118.3 %all-gather.9.cloned.1.call-start = ((), (), s32[]{:S(2)}) async-start(), calls=%async_computation.8 | async-start | bytes 10485760 | tf_op jit(solution)/shard_map/all_gather | solution.py:202
  614.1 296.7 %reduce-scatter.9.cloned.1.call-start = ((), (), s32[]{:S(2)}) async-start(), calls=%async_computation.9 | async-start | bytes 20971520 | tf_op jit(solution)/shard_map/reduce_scatter | solution.py:210
  784.5 200.5 %reduce-scatter.7.cloned.1.call-start = ((), (), s32[]{:S(2)}) async-start(), calls=%async_computation.7 | async-start | bytes 10485760 | tf_op jit(solution)/shard_map/reduce_scatter | solution.py:195
  799.8 185.2 %copy-start.9 = (bf16[1024,1024]{1,0:T(8,128)(2,1)S(1)}, bf16[1024,1024]{1,0:T(8,128)(2,1)}, u32[]{:S(2)}) copy-start(bf16[1024,1024]{1,0:T(8,128)(2,1)} %param.35) | copy-start | bytes 6291460
  799.8 250.5 %all-gather.11.cloned.1.call-start = ((), (), s32[]{:S(2)}) async-start(), calls=%async_computation.10 | async-start | bytes 10485760 | tf_op jit(solution)/shard_map/all_gather | solution.py:219
  991.9 889.8 %all-reduce.4.cloned.1.call-start = ((), (), s32[]{:S(2)}) async-start(), calls=%async_computation.12 | async-start | bytes 16777216 | tf_op jit(solution)/shard_map/psum | solution.py:247
  1018.2 32.1 %copy-start.21 = (bf16[256,1024]{1,0:T(8,128)(2,1)S(1)}, bf16[256,1024]{1,0:T(8,128)(2,1)}, u32[]{:S(2)}) copy-start(bf16[256,1024]{1,0:T(8,128)(2,1)} %param.29) | copy-start | bytes 1572868
  1067.0 507.6 %copy-start.13 = (f32[2048,32]{0,1:T(8,128)S(1)}, f32[2048,32]{0,1:T(8,128)}, u32[]{:S(2)}) copy-start(f32[2048,32]{0,1:T(8,128)} %copy-done.12) | copy-start | bytes 786436
  1591.9 8.2 copy-start.11
  1606.6 402.6 %reduce-scatter.11.cloned.1.call-start = ((), (), s32[]{:S(2)}) async-start(), calls=%async_computation.11 | async-start | bytes 20971520 | tf_op jit(solution)/shard_map/reduce_scatter | solution.py:234
  1891.2 118.0 %copy-start.7 = (bf16[1024,1024]{1,0:T(8,128)(2,1)S(1)}, bf16[1024,1024]{1,0:T(8,128)(2,1)}, u32[]{:S(2)}) copy-start(bf16[1024,1024]{1,0:T(8,128)(2,1)} %param.22) | copy-start | bytes 6291460
  1891.2 118.0 %copy-start.29 = (f32[1024]{0:T(1024)S(1)}, f32[1024]{0:T(1024)}, u32[]{:S(2)}) copy-start(f32[1024]{0:T(1024)} %copy-done.28) | copy-start | bytes 12292
  1891.2 118.0 %copy-start.31 = (f32[1024]{0:T(1024)S(1)}, f32[1024]{0:T(1024)}, u32[]{:S(2)}) copy-start(f32[1024]{0:T(1024)} %copy-done.30) | copy-start | bytes 12292
  1891.2 118.0 %copy-start.34 = (f32[1024]{0:T(1024)S(1)}, f32[1024]{0:T(1024)}, u32[]{:S(2)}) copy-start(f32[1024]{0:T(1024)} %param.24) | copy-start | bytes 12292
  1894.4 118.6 %copy-start.35 = (f32[1024]{0:T(1024)S(1)}, f32[1024]{0:T(1024)}, u32[]{:S(2)}) copy-start(f32[1024]{0:T(1024)} %get-tuple-element.306) | copy-start | bytes 12292
  1894.4 118.6 %copy-start.36 = (f32[1024]{0:T(1024)S(1)}, f32[1024]{0:T(1024)}, u32[]{:S(2)}) copy-start(f32[1024]{0:T(1024)} %get-tuple-element.312) | copy-start | bytes 12292
  (122 other events, 349.8 us)
Sparse Core Ops, SparseCore 0:
  14.7 60.9 all-gather.4
  480.0 126.1 reduce-scatter.4
  613.7 58.2 all-gather.6
  673.5 58.2 all-gather.8
  784.6 126.0 reduce-scatter.8
  913.2 71.7 reduce-scatter.6
  992.0 58.2 all-gather.10
  1606.7 274.8 all-reduce.3
  1884.4 124.7 reduce-scatter.10
where the time goes:
time: 2080 us; the launch traced here: 2070 us
  waiting for transfers between devices  844 us (41%)
  matrix products  626 us (30%)
  local copies, waits for them, and re-layouts  395 us (19%)
  other arithmetic  143 us (7%)
  blocking collectives  39.6 us (2%)
    psum x1, waiting for transfers between devices, shards(): lax.psum(grad_qkv_weight[:, :head_cols].astype(jnp.bfloat16), 'dp')  262 us
    dot_general x100, matrix products, times_transposed(): lax.dot_general(left, right, (((1,), (1,)), ((), ())), preferred_element_...  229 us
    dot_general x68, matrix products, contract_rows(): lax.dot_general(left, right, (((0,), (0,)), ((), ())), preferred_element_...  180 us
    reduce_scatter x1, waiting for transfers between devices, shards(): lax.psum_scatter(jnp.dot(mixed_rows, output_weight, preferred_element_typ...  126 us
    while x200, local copies, waits for them, and re-layouts  125 us
    reduce_scatter x1, waiting for transfers between devices, shards(): lax.psum_scatter(times_transposed(grad_qkv, weight_qkv), 'tensor', scatte...  114 us
    dot_general x32, matrix products, one_block(): mixed = jnp.dot(probs, value_item, preferred_element_type=jnp.float32)  112 us
    reduce_scatter x1, waiting for transfers between devices, shards(): lax.psum_scatter(times_transposed(grad_gu, weight_gu), 'tensor', scatter_...  111 us
  transfers between devices with their start and end apart: 9, of which 9 were waited for; matrix products, arithmetic and copies ran while one was open for 6% of the time, Pallas kernels for 0%

commit v1 on v0

v1 whole, which is shorter than its diff:
```python
import functools
import math

import jax
import jax.numpy as jnp
from jax import lax
from jax.experimental import pallas as pl
from jax.experimental.pallas import tpu as pltpu
from jax.sharding import PartitionSpec as P

HD = 64
LEN = 2048
EPSILON = 1e-05
MASKED = -1e30
LANES = 128
LOG2E = math.log2(math.e)
BF16 = jnp.bfloat16
F32 = jnp.float32
MIB = 1 << 20
COST_SHARE = 0.1
PIECES = 4


def contract(left, right, left_dim, right_dim):
    return lax.dot_general(
        left, right, (((left_dim,), (right_dim,)), ((), ())), preferred_element_type=F32
    )


def cost(flops, moved, transcendentals=0):
    return pl.CostEstimate(
        flops=int(flops * COST_SHARE),
        bytes_accessed=int(moved * COST_SHARE),
        transcendentals=int(transcendentals * COST_SHARE),
    )


def swap_halves(value):
    columns = value.shape[1]
    lane = lax.broadcasted_iota(jnp.int32, value.shape, 1)
    return jnp.where(
        lane % HD < HD // 2,
        pltpu.roll(value, columns - HD // 2, 1),
        pltpu.roll(value, HD // 2, 1),
    )


def project_kernel(rows_ref, weight_ref, cos_ref, sin_ref, q_ref, k_ref, v_ref):
    columns = q_ref.shape[1]
    product = contract(rows_ref[...], weight_ref[...], 1, 0)
    cosines = jnp.concatenate([cos_ref[...]] * (columns // LANES), axis=1)
    sines = jnp.concatenate([sin_ref[...]] * (columns // LANES), axis=1)
    for part, out_ref in ((0, q_ref), (1, k_ref)):
        value = product[:, part * columns : (part + 1) * columns]
        out_ref[...] = (value * cosines + swap_halves(value) * sines).astype(BF16)
    v_ref[...] = product[:, 2 * columns :].astype(BF16)


def project(rows, weight, cosines, sines, block=512):
    count, width = rows.shape
    columns = weight.shape[1] // 3
    table = pl.BlockSpec((block, LANES), lambda i: (i, 0))
    out = pl.BlockSpec((block, columns), lambda i: (i, 0))
    return pl.pallas_call(
        project_kernel,
        grid=(count // block,),
        in_specs=[
            pl.BlockSpec((block, width), lambda i: (i, 0)),
            pl.BlockSpec(weight.shape, lambda i: (0, 0)),
            table,
            table,
        ],
        out_specs=[out, out, out],
        out_shape=[jax.ShapeDtypeStruct((count, columns), BF16)] * 3,
        cost_estimate=cost(2 * count * width * 3 * columns, 2 * (count * width + width * 3 * columns + count * 3 * columns), 0),
        compiler_params=pltpu.CompilerParams(vmem_limit_bytes=40 * MIB),
        name="project_rope",
    )(rows, weight, cosines, sines)


def masked_keys(place_ref, key_ref, masked_ref):
    count = key_ref.shape[0]
    lane = lax.broadcasted_iota(jnp.int32, (count, LANES), 1)
    row = lax.broadcasted_iota(jnp.int32, (count, LANES), 0) + place_ref[1]
    position = jnp.where(row >= count, row - count, row)
    bias = jnp.where(position >= place_ref[0], MASKED, 0.0).astype(BF16)
    nothing = jnp.zeros_like(bias)
    key = key_ref[...]
    masked_ref[0] = jnp.where(lane < HD, key, jnp.where(lane == HD, bias, nothing))
    masked_ref[1] = jnp.where(lane >= HD, key, jnp.where(lane == 0, bias, nothing))


def masked_queries(query):
    lane = lax.broadcasted_iota(jnp.int32, query.shape, 1)
    scaled = query * jnp.asarray(1.0 / math.sqrt(HD), BF16)
    one = jnp.ones_like(query)
    nothing = jnp.zeros_like(query)
    return (
        scaled,
        jnp.where(lane < HD, scaled, jnp.where(lane == HD, one, nothing)),
        jnp.where(lane >= HD, scaled, jnp.where(lane == 0, one, nothing)),
    )


def attend_kernel(place_ref, q_ref, k_ref, v_ref, out_ref, log_ref, keys, values_t, *, chunk):
    count = k_ref.shape[0]

    @pl.when(pl.program_id(1) == 0)
    def _():
        masked_keys(place_ref, k_ref, keys)
        values_t[...] = v_ref[...].T

    queries = masked_queries(q_ref[...])[1:]
    mixed, logs = [], []
    for head in range(2):
        scores = [
            contract(keys[head, start : start + chunk, :], queries[head], 1, 1)
            for start in range(0, count, chunk)
        ]
        top = functools.reduce(
            jnp.maximum, [jnp.max(block, axis=0, keepdims=True) for block in scores]
        )
        total = 0.0
        summed = 0.0
        for index, block in enumerate(scores):
            weights = jnp.exp2((block - top) * LOG2E)
            total = total + jnp.sum(weights, axis=0, keepdims=True)
            value = values_t[
                head * HD : (head + 1) * HD, index * chunk : (index + 1) * chunk
            ]
            summed = summed + contract(value, weights.astype(BF16), 1, 0)
        mixed.append(summed / total)
        logs.append(top * LOG2E + jnp.log2(total))
    out_ref[...] = jnp.concatenate(mixed, axis=0).T.astype(BF16)
    log_ref[0] = jnp.concatenate(logs + [jnp.zeros((6, q_ref.shape[0]), F32)], axis=0)


def attend(place, queries, keys, values, block=1024, chunk=512):
    count, columns = queries.shape
    pairs = columns // LANES
    whole = pl.BlockSpec((count, LANES), lambda p, i, _: (0, p))
    rows = pl.BlockSpec((block, LANES), lambda p, i, _: (i, p))
    return pl.pallas_call(
        functools.partial(attend_kernel, chunk=chunk),
        grid_spec=pltpu.PrefetchScalarGridSpec(
            num_scalar_prefetch=1,
            grid=(pairs, count // block),
            in_specs=[rows, whole, whole],
            out_specs=[rows, pl.BlockSpec((1, 8, block), lambda p, i, _: (p, 0, i))],
            scratch_shapes=[
                pltpu.VMEM((2, count, LANES), BF16),
                pltpu.VMEM((LANES, count), BF16),
            ],
        ),
        out_shape=[
            jax.ShapeDtypeStruct((count, columns), BF16),
            jax.ShapeDtypeStruct((pairs, 8, count), F32),
        ],
        cost_estimate=cost(16 * count * count * columns, 8 * count * columns, count * count * columns // HD),
        compiler_params=pltpu.CompilerParams(vmem_limit_bytes=56 * MIB),
        name="attention_forward",
    )(place, queries, keys, values)


def attend_back_kernel(
    place_ref,
    q_ref,
    k_ref,
    v_ref,
    out_ref,
    up_ref,
    log_ref,
    cos_row_ref,
    sin_row_ref,
    cos_ref,
    sin_ref,
    *rest,
    chunk,
):
    grad_ref, keys, grad_keys_t, grad_values_t = rest[-4:]
    count = k_ref.shape[0]
    step = pl.program_id(1)

    @pl.when(step == 0)
    def _():
        masked_keys(place_ref, k_ref, keys)
        grad_keys_t[...] = jnp.zeros_like(grad_keys_t)
        grad_values_t[...] = jnp.zeros_like(grad_values_t)

    scaled, *queries = masked_queries(q_ref[...])
    upstream = up_ref[...]
    lane = lax.broadcasted_iota(jnp.int32, upstream.shape, 1)
    nothing = jnp.zeros_like(upstream)
    products = upstream.astype(F32) * out_ref[...].astype(F32)
    scaled_t = scaled.T
    upstream_t = upstream.T
    logs = log_ref[0].T
    grad_queries = []
    for head in range(2):
        mine = (lane < HD) == (head == 0)
        own_upstream = jnp.where(mine, upstream, nothing)
        row_dot = jnp.sum(jnp.where(mine, products, 0.0), axis=1, keepdims=True)
        log_total = logs[:, head : head + 1]
        heads = slice(head * HD, (head + 1) * HD)
        grad_query = 0.0
        for start in range(0, count, chunk):
            span = slice(start, start + chunk)
            scores = contract(queries[head], keys[head, span, :], 1, 1)
            probs = jnp.exp2(scores * LOG2E - log_total)
            grad_probs = contract(own_upstream, v_ref[span, :], 1, 1)
            grad_scores = (probs * (grad_probs - row_dot)).astype(BF16)
            grad_values_t[heads, span] += contract(
                upstream_t[heads, :], probs.astype(BF16), 1, 0
            )
            grad_keys_t[heads, span] += contract(scaled_t[heads, :], grad_scores, 1, 0)
            grad_query = grad_query + contract(grad_scores, k_ref[span, :], 1, 0)
        grad_queries.append(grad_query)
    grad_query = jnp.where(lane < HD, *grad_queries) * (1.0 / math.sqrt(HD))
    block = grad_query.shape[0]
    grad_ref[0, pl.ds(pl.multiple_of(step * block, block), block), :] = (
        grad_query * cos_row_ref[...] - swap_halves(grad_query) * sin_row_ref[...]
    ).astype(BF16)

    @pl.when(step == pl.num_programs(1) - 1)
    def _():
        grad_key = grad_keys_t[...].T
        grad_ref[1] = (
            grad_key * cos_ref[...] - swap_halves(grad_key) * sin_ref[...]
        ).astype(BF16)
        grad_ref[2] = grad_values_t[...].T.astype(BF16)


def attend_back(
    place, queries, keys, values, mixed, upstream, logs, cosines, sines, pair, grads, block=512, chunk=512
):
    count, columns = queries.shape
    whole = pl.BlockSpec((count, LANES), lambda p, i, _: (0, pair))
    rows = pl.BlockSpec((block, LANES), lambda p, i, _: (i, pair))
    table = pl.BlockSpec((count, LANES), lambda p, i, _: (0, 0))
    table_rows = pl.BlockSpec((block, LANES), lambda p, i, _: (i, 0))
    held = [] if grads is None else [grads]
    return pl.pallas_call(
        functools.partial(attend_back_kernel, chunk=chunk),
        grid_spec=pltpu.PrefetchScalarGridSpec(
            num_scalar_prefetch=1,
            grid=(1, count // block),
            in_specs=[
                rows,
                whole,
                whole,
                rows,
                rows,
                pl.BlockSpec((1, 8, block), lambda p, i, _: (pair, 0, i)),
                table_rows,
                table_rows,
                table,
                table,
            ]
            + [pl.BlockSpec(memory_space=pl.ANY)] * len(held),
            out_specs=pl.BlockSpec((3, count, LANES), lambda p, i, _: (0, 0, pair)),
            scratch_shapes=[
                pltpu.VMEM((2, count, LANES), BF16),
                pltpu.VMEM((LANES, count), F32),
                pltpu.VMEM((LANES, count), F32),
            ],
        ),
        out_shape=jax.ShapeDtypeStruct((3, count, columns), BF16),
        input_output_aliases={11: 0} if held else {},
        cost_estimate=cost(28 * count * count * LANES, 16 * count * LANES, count * count * 2),
        compiler_params=pltpu.CompilerParams(vmem_limit_bytes=60 * MIB),
        name="attention_backward",
    )(place, queries, keys, values, mixed, upstream, logs, cosines, sines, cosines, sines, *held)


def feed_kernel(
    rows_ref,
    target_ref,
    gate_ref,
    up_ref,
    down_ref,
    inner_ref,
    grad_gate_ref,
    grad_up_ref,
    weight_gate_ref,
    weight_up_ref,
    weight_down_ref,
    rows_t,
    target_t,
    *,
    chunk,
):
    @pl.when(pl.program_id(0) == 0)
    def _():
        rows_t[...] = rows_ref[...].T
        target_t[...] = target_ref[...].T

    for start in range(0, rows_ref.shape[0], chunk):
        span = slice(start, start + chunk)
        gate = contract(rows_ref[span, :], gate_ref[...], 1, 0)
        up = contract(rows_ref[span, :], up_ref[...], 1, 0)
        grad_inner = contract(target_ref[span, :], down_ref[...], 1, 1)
        share = jax.nn.sigmoid(gate)
        activated = gate * share
        inner_ref[span, :] = (activated * up).astype(BF16)
        grad_up_ref[span, :] = (grad_inner * activated).astype(BF16)
        grad_gate_ref[span, :] = (
            grad_inner * up * share * (1.0 + gate * (1.0 - share))
        ).astype(BF16)
    weight_gate_ref[...] = contract(rows_t[...], grad_gate_ref[...], 1, 0).astype(BF16)
    weight_up_ref[...] = contract(rows_t[...], grad_up_ref[...], 1, 0).astype(BF16)
    weight_down_ref[...] = contract(target_t[...], inner_ref[...], 1, 0).T.astype(BF16)


def feed(rows, target, gate_weight, up_weight, down_weight, block=256, chunk=512):
    count, width = rows.shape
    units = gate_weight.shape[1]
    block = min(block, units)
    whole = pl.BlockSpec((count, width), lambda i: (0, 0), pipeline_mode=pl.Buffered(1))
    across = pl.BlockSpec((width, block), lambda i: (0, i))
    down = pl.BlockSpec((block, width), lambda i: (i, 0))
    out = pl.BlockSpec((count, block), lambda i: (0, i))
    return pl.pallas_call(
        functools.partial(feed_kernel, chunk=chunk),
        grid=(units // block,),
        in_specs=[whole, whole, across, across, down],
        out_specs=[out, out, out, across, across, down],
        out_shape=[jax.ShapeDtypeStruct((count, units), BF16)] * 3
        + [jax.ShapeDtypeStruct((width, units), BF16)] * 2
        + [jax.ShapeDtypeStruct((units, width), BF16)],
        scratch_shapes=[pltpu.VMEM((width, count), BF16)] * 2,
        cost_estimate=cost(
            12 * count * width * units,
            4 * count * width + 12 * width * units + 6 * count * units,
            2 * count * units,
        ),
        compiler_params=pltpu.CompilerParams(vmem_limit_bytes=60 * MIB),
        name="feed_forward",
    )(rows, target, gate_weight, up_weight, down_weight)


def sum_kernel(*refs, dims):
    total = 0.0
    for index, dim in enumerate(dims):
        total = total + contract(refs[2 * index][...], refs[2 * index + 1][...], 1, dim)
    refs[-1][...] = total.astype(refs[-1].dtype)


def sum_products(terms, start, rows, dtype=F32, block=512):
    block = min(block, rows)
    first = start // block
    operands, specs, dims, flops, moved = [], [], [], 0, 0
    for left, plane, right, part, dim in terms:
        depth = left.shape[-1]
        if plane is None:
            specs.append(pl.BlockSpec((block, depth), lambda i: (first + i, 0)))
        else:
            specs.append(
                pl.BlockSpec((None, block, depth), lambda i, plane=plane: (plane, first + i, 0))
            )
        shape = right.shape if part is None else (right.shape[0], depth)
        column = 0 if part is None else part
        specs.append(pl.BlockSpec(shape, lambda i, column=column: (0, column)))
        operands += [left, right]
        dims.append(dim)
        width = shape[1 - dim]
        flops += 2 * rows * depth * width
        moved += 2 * rows * depth + 2 * depth * width
    return pl.pallas_call(
        functools.partial(sum_kernel, dims=tuple(dims)),
        grid=(rows // block,),
        in_specs=specs,
        out_specs=pl.BlockSpec((block, width), lambda i: (i, 0)),
        out_shape=jax.ShapeDtypeStruct((rows, width), dtype),
        cost_estimate=cost(flops, moved + 4 * rows * width),
        compiler_params=pltpu.CompilerParams(vmem_limit_bytes=58 * MIB),
        name="sum_products",
    )(*operands)


def outer_kernel(left_ref, right_ref, out_ref, left_t):
    @pl.when(pl.program_id(0) == 0)
    def _():
        left_t[...] = left_ref[...].T

    out_ref[...] = contract(left_t[...], right_ref[...], 1, 0).astype(BF16)


def outer(left, right, block):
    count, width = left.shape
    columns = right.shape[-1]
    if right.ndim == 3:
        steps = right.shape[0]
        block = columns
        spec = pl.BlockSpec((None, count, columns), lambda i: (i, 0, 0))
    else:
        steps = columns // block
        spec = pl.BlockSpec((count, block), lambda i: (0, i))
    return pl.pallas_call(
        outer_kernel,
        grid=(steps,),
        in_specs=[
            pl.BlockSpec((count, width), lambda i: (0, 0), pipeline_mode=pl.Buffered(1)),
            spec,
        ],
        out_specs=pl.BlockSpec((width, block), lambda i: (0, i)),
        out_shape=jax.ShapeDtypeStruct((width, steps * block), BF16),
        scratch_shapes=[pltpu.VMEM((width, count), BF16)],
        cost_estimate=cost(
            2 * count * width * steps * block,
            2 * count * (width + steps * block) + 2 * width * steps * block,
        ),
        compiler_params=pltpu.CompilerParams(vmem_limit_bytes=40 * MIB),
        name="outer_product",
    )(left, right)


def standardize(value):
    centred = value - jnp.mean(value, axis=-1, keepdims=True)
    scale = lax.rsqrt(jnp.mean(centred * centred, axis=-1, keepdims=True) + EPSILON)
    return centred * scale, scale


def norm_kernel(*refs, added):
    value = refs[0][...].astype(F32)
    for ref in refs[1 : 1 + added]:
        value = value + ref[...].astype(F32)
    gain_ref, shift_ref = refs[1 + added : 3 + added]
    standard, _ = standardize(value)
    if added:
        refs[-2][...] = value
    refs[-1][...] = (standard * gain_ref[...] + shift_ref[...]).astype(BF16)


def norm(base, terms, gain, shift, pieces=PIECES, block=256):
    count, width = base.shape
    rows = count // pieces
    block = min(block, rows)
    vector = pl.BlockSpec((1, width), lambda i: (0, 0))
    total, out = None, []
    for piece in range(pieces):
        first = piece * rows // block
        whole = pl.BlockSpec((block, width), lambda i, first=first: (first + i, 0))
        shapes = [jax.ShapeDtypeStruct((rows, width), BF16)]
        specs = [pl.BlockSpec((block, width), lambda i: (i, 0))]
        held = []
        if terms:
            shapes = [jax.ShapeDtypeStruct((count, width), F32)] + shapes
            specs = [whole] + specs
            held = [] if total is None else [total]
        results = pl.pallas_call(
            lambda *refs, held=len(held): norm_kernel(
                *refs[: 3 + len(terms)], *refs[3 + len(terms) + held :], added=len(terms)
            ),
            grid=(rows // block,),
            in_specs=[whole] * (1 + len(terms))
            + [vector, vector]
            + [pl.BlockSpec(memory_space=pl.ANY)] * len(held),
            out_specs=specs,
            out_shape=shapes,
            input_output_aliases={3 + len(terms): 0} if held else {},
            cost_estimate=cost(16 * rows * width, 8 * rows * width * len(shapes)),
            name="layer_norm",
        )(base, *terms, gain.reshape(1, width), shift.reshape(1, width), *held)
        out.append(results[-1])
        if terms:
            total = results[0]
    return total, out


def norm_back_kernel(*refs, added, low):
    base_ref, straight_ref, gain_ref = refs[:3]
    upstream = refs[3][...].astype(F32)
    for ref in refs[4 : 3 + added]:
        upstream = upstream + ref[...].astype(F32)
    outs = refs[3 + added :]
    standard, scale = standardize(base_ref[...].astype(F32))
    scaled = upstream * gain_ref[...]
    back = straight_ref[...].astype(F32) + scale * (
        scaled
        - jnp.mean(scaled, axis=-1, keepdims=True)
        - standard * jnp.mean(scaled * standard, axis=-1, keepdims=True)
    )
    outs[0][...] = back.astype(BF16)
    if not low:
        outs[1][...] = back
    sums = jnp.concatenate(
        [
            jnp.sum(upstream * standard, axis=0, keepdims=True),
            jnp.sum(upstream, axis=0, keepdims=True),
        ],
        axis=0,
    )

    @pl.when(pl.program_id(0) == 0)
    def _():
        outs[-1][...] = sums

    @pl.when(pl.program_id(0) > 0)
    def _():
        outs[-1][...] += sums


def norm_back(base, straight, gain, terms, low, pieces=PIECES, block=256):
    count, width = base.shape
    rows = count // pieces
    block = min(block, rows)
    total, out, found = None, [], []
    for piece in range(pieces):
        first = piece * rows // block
        whole = pl.BlockSpec((block, width), lambda i, first=first: (first + i, 0))
        shapes = [jax.ShapeDtypeStruct((rows, width), BF16)]
        specs = [pl.BlockSpec((block, width), lambda i: (i, 0))]
        held = []
        if not low:
            shapes.append(jax.ShapeDtypeStruct((count, width), F32))
            specs.append(whole)
            held = [] if total is None else [total]
        results = pl.pallas_call(
            lambda *refs, held=len(held): norm_back_kernel(
                *refs[: 3 + len(terms)],
                *refs[3 + len(terms) + held :],
                added=len(terms),
                low=low,
            ),
            grid=(rows // block,),
            in_specs=[whole, whole, pl.BlockSpec((1, width), lambda i: (0, 0))]
            + [whole] * len(terms)
            + [pl.BlockSpec(memory_space=pl.ANY)] * len(held),
            out_specs=specs + [pl.BlockSpec((2, width), lambda i: (0, 0))],
            out_shape=shapes + [jax.ShapeDtypeStruct((2, width), F32)],
            input_output_aliases={3 + len(terms): 1} if held else {},
            cost_estimate=cost(30 * rows * width, 16 * rows * width),
            name="layer_norm_backward",
        )(base, straight, gain.reshape(1, width), *terms, *held)
        out.append(results[0])
        found.append(results[-1])
        if not low:
            total = results[1]
    return out, total, sum(found)


def rope_tables(offset):
    position = (jnp.arange(LEN, dtype=jnp.int32) + offset) % LEN
    inverse = 10000.0 ** (-2.0 * jnp.arange(HD // 2, dtype=F32) / HD)
    angles = position.astype(F32)[:, None] * inverse[None, :]
    cosines, sines = jnp.cos(angles), jnp.sin(angles)
    return (
        jnp.concatenate([cosines] * 4, axis=1),
        jnp.concatenate([-sines, sines, -sines, sines], axis=1),
    )


def exchanges(axis, size):
    if size & (size - 1):
        return [lambda value: lax.psum(value, axis)]
    return [
        lambda value, pairs=[(i, i ^ (1 << bit)) for i in range(size)]: value
        + lax.ppermute(value, axis, pairs)
        for bit in range(size.bit_length() - 1)
    ]


def shards(
    dp_size,
    tensor_size,
    tokens,
    lengths,
    gain_first,
    shift_first,
    query_weight,
    key_weight,
    value_weight,
    output_weight,
    gain_second,
    shift_second,
    gate_weight,
    up_weight,
    down_weight,
    cotangent,
):
    windows = lengths.shape[0]
    span = tensor_size // windows
    held = tokens.shape[0]
    width = tokens.shape[1]
    head_cols = query_weight.shape[1]
    here = lax.axis_index("tensor")
    window, seat = here // span, here % span

    def from_seat(value, shift):
        pairs = [
            (w * span + (s + shift) % span, w * span + s)
            for w in range(windows)
            for s in range(span)
        ]
        return lax.ppermute(value, "tensor", pairs)

    def to_seat(value, shift):
        return from_seat(value, span - shift)

    def from_window(value, shift):
        pairs = [((t + shift * span) % tensor_size, t) for t in range(tensor_size)]
        return lax.ppermute(value, "tensor", pairs)

    def to_window(value, shift):
        return from_window(value, windows - shift)

    def gather_rows(value):
        return jnp.concatenate(
            value + [from_seat(piece, s) for s in range(1, span) for piece in value], axis=0
        )

    def scatter(partial):
        sent = [to_seat(partial(s * held, held), s) for s in range(1, span)]
        return [partial(0, held)] + sent

    def all_windows(value):
        return [value] + [from_window(value, shift) for shift in range(1, windows)]

    def spread_windows(values):
        group = lax.axis_index("dp")
        sizes = [value.shape[0] // dp_size for value in values]
        mine = jnp.concatenate(
            [
                lax.dynamic_slice_in_dim(value, group * size, size, axis=0).reshape(-1, width)
                for value, size in zip(values, sizes)
            ],
            axis=0,
        )
        return [mine], [from_window(mine, shift) for shift in range(1, windows)]

    def gather_spread(values, piece):
        gathered = lax.all_gather(piece, "dp", axis=0)
        out, start = [], 0
        for value in values:
            count = value.size // width // dp_size
            out.append(gathered[:, start : start + count].reshape(value.shape))
            start += count
        return out

    def after(value, *others):
        return lax.optimization_barrier((value, *others))[0]

    place = jnp.stack(
        [lax.dynamic_index_in_dim(lengths, window, keepdims=False), seat * held]
    ).astype(jnp.int32)
    cosines, sines = rope_tables(seat * held)

    members = [[s] for s in range(windows)] if head_cols % LANES == 0 else [list(range(windows))]
    feed_weights = [gate_weight, up_weight, down_weight]
    slices_sent, slices = spread_windows(feed_weights)
    _, normed_one = norm(after(tokens, *slices_sent), [], gain_first, shift_first)
    full_one = gather_rows(normed_one)
    qkv_own = jnp.concatenate([query_weight, key_weight, value_weight], axis=1)
    qkv_other = all_windows(after(qkv_own, *slices))[1:]
    qkv_shards = [qkv_own] + qkv_other
    def joined(parts, axis):
        return parts[0] if len(parts) == 1 else jnp.concatenate(parts, axis=axis)

    def part_of(value, part):
        return value[:, part * head_cols : (part + 1) * head_cols]

    qkv_weights = [
        qkv_shards[group[0]]
        if len(group) == 1
        else joined([part_of(qkv_shards[s], part) for part in range(3) for s in group], 1)
        for group in members
    ]
    target = gather_rows([cotangent])
    qkv, attended = [], []
    rows_one = full_one
    for weight in qkv_weights:
        parts = project(rows_one, weight, cosines, sines)
        if not qkv:
            slices = [after(piece, parts[0]) for piece in slices]
            feed_shards = [feed_weights]
            feed_shards += [gather_spread(feed_weights, piece) for piece in slices]
        waits = slices if not qkv else [target]
        qkv.append((after(parts[0], *waits), *parts[1:]))
        attended.append(attend(place, *qkv[-1]))
        if len(attended) == 1:
            sent = after(output_weight, attended[0][0])
            output_shards = [output_weight] + all_windows(sent)[1:]
        rows_one = after(full_one, attended[-1][0])

    out_weights = [joined([output_shards[s] for s in group], 0) for group in members]
    mixer_terms = [
        (mixed, None, weight, None, 0) for (mixed, _), weight in zip(attended, out_weights)
    ]
    hidden_one, normed_two = norm(
        tokens,
        scatter(lambda start, rows: sum_products(mixer_terms, start, rows)),
        gain_second,
        shift_second,
    )
    full_two = gather_rows(normed_two)

    flip = [(d, d ^ 1) for d in range(dp_size)]
    odd = lax.axis_index("dp") % 2

    def half(value, which):
        count = value.shape[0] // 2
        return lax.dynamic_slice_in_dim(value, which * count, count, axis=0)

    def total(pieces, which):
        return sum(half(piece, which).astype(F32) for piece in pieces).astype(BF16)

    def swap_half(pieces, *others):
        pieces = [after(piece, *others) for piece in pieces]
        mine, sent = total(pieces, odd), total(pieces, 1 - odd)
        return (mine, lax.ppermute(sent, "dp", flip)), [mine, sent]

    def add_half(halves, *others):
        mine, received = (after(value, *others) for value in halves)
        return (mine.astype(F32) + received.astype(F32)).astype(BF16)

    def sum_half(value, turn):
        groups = [list(range(0, dp_size, 2)), list(range(1, dp_size, 2))]
        if turn & 1:
            groups = groups[::-1]
        if turn & 2:
            groups = [group[::-1] for group in groups]
        return lax.psum(value, "dp", axis_index_groups=groups)

    def swap_sum(mine, *others):
        mine = after(mine, *others)
        return mine, lax.ppermute(mine, "dp", flip)

    def whole_sum(halves, *others):
        mine, received = (after(value, *others) for value in halves)
        first, second = jnp.where(odd == 0, mine, received), jnp.where(odd == 0, received, mine)
        return jnp.concatenate([first, second], axis=0).astype(F32)

    def send_to_owner(parts):
        return [to_window(parts[shift], shift) for shift in range(1, windows)]

    order = list(range(1, windows)) + [0]
    fed = {}
    rows_two = full_two
    for s in order:
        fed[s] = feed(rows_two, target, *feed_shards[s])
        rows_two = after(full_two, fed[s][0])
    down_pieces, up_pieces, gate_pieces = (
        send_to_owner({s: fed[s][k] for s in order}) + [fed[0][k]] for k in (5, 4, 3)
    )
    two_terms, feed_terms = [], []
    for s in order:
        gate, up, down = feed_shards[s]
        two_terms += [(fed[s][1], None, gate, None, 1), (fed[s][2], None, up, None, 1)]
        feed_terms.append((fed[s][0], None, down, None, 0))

    two_sent = [
        sum_products(two_terms, shift * held, held, BF16) for shift in range(1, span)
    ]
    down_half, marks = swap_half(down_pieces, *two_sent)
    two_terms = [(after(two_terms[0][0], *marks), *two_terms[0][1:])] + two_terms[1:]
    two_kept = sum_products(two_terms, 0, held)
    grad_branch_own, grad_hidden, norm_two = norm_back(
        hidden_one,
        cotangent,
        gain_second,
        [two_kept] + [to_seat(part, shift + 1) for shift, part in enumerate(two_sent)],
        False,
    )
    grad_branch = gather_rows(grad_branch_own)
    down_half = add_half(down_half, *grad_branch_own)
    down_sum = sum_half(down_half, 0)
    grad_branch = after(grad_branch, down_half)

    members = members[::-1]
    out_weights, qkv_weights = out_weights[::-1], qkv_weights[::-1]
    qkv, attended = qkv[::-1], attended[::-1]
    out_grads, grad_mixed = {}, []
    for group, weight, (mixed, _) in zip(members, out_weights, attended):
        grad_mixed.append(sum_products([(grad_branch, None, weight, None, 1)], 0, LEN, BF16))
        out_grad = outer(mixed, grad_branch, min(512, width))
        for spot, s in enumerate(group):
            out_grads[s] = out_grad[spot * head_cols : (spot + 1) * head_cols]
    out_pieces = send_to_owner(out_grads) + [out_grads[0]]

    def up_swap(last):
        sums["up"], waits = swap_half(up_pieces, *last)
        return waits

    def up_sum(last):
        value = add_half(sums["up"], *last)
        sums["up"] = sum_half(value, 1)
        sums["down"] = swap_sum(down_sum, *last)
        return [value, sums["down"][0]]

    def gate_swap(last):
        sums["gate"], waits = swap_half(gate_pieces, *last)
        sums["out"], more = swap_half(out_pieces, *last)
        sums["down"] = whole_sum(sums["down"], *last)
        return waits + more + [sums["down"]]

    def gate_sum(last):
        values = [add_half(sums["gate"], *last), add_half(sums["out"], *last)]
        sums["gate"], sums["out"] = sum_half(tuple(values), 2)
        sums["up"] = swap_sum(sums["up"], *last)
        return values + [sums["up"][0]]

    across, along = (exchanges(axis, size) for axis, size in (("tensor", tensor_size), ("dp", dp_size)))
    norm_steps = across + along[1:]
    sums = {}
    moves = [up_swap, up_sum, gate_swap, gate_sum]
    last = list(out_grads.values()) + grad_mixed
    grad_qkv, qkv_grads = [], {}
    for index, group in enumerate(members):
        mixed, logs = attended[index]
        count = len(group) * head_cols
        grads = None
        for pair in range(count // LANES):
            waits = moves.pop(0)(last) if moves else last
            if norm_steps:
                norm_two = norm_steps.pop(0)(after(norm_two, *last))
                waits = waits + [norm_two]
            grads = attend_back(
                place,
                *qkv[index],
                mixed,
                after(grad_mixed[index], *waits),
                logs,
                cosines,
                sines,
                pair,
                grads,
            )
            last = [grads]
        grad_qkv.append(grads)
        qkv_grad = outer(full_one, grads, count)
        last = [qkv_grad]
        for spot, s in enumerate(group):
            if len(group) == 1:
                qkv_grads[s] = qkv_grad
            else:
                qkv_grads[s] = joined(
                    [
                        lax.slice_in_dim(
                            qkv_grad,
                            part * count + spot * head_cols,
                            part * count + (spot + 1) * head_cols,
                            axis=1,
                        )
                        for part in range(3)
                    ],
                    1,
                )
    for move in moves:
        last = move(last)

    qkv_half, marks = swap_half(send_to_owner(qkv_grads) + [qkv_grads[0]])
    feed_terms[0] = (after(feed_terms[0][0], *marks), *feed_terms[0][1:])
    feed_sent = [sum_products(feed_terms, shift * held, held, BF16) for shift in range(1, span)]
    feed_terms[0] = (after(feed_terms[0][0], *feed_sent), *feed_terms[0][1:])
    feed_parts = [sum_products(feed_terms, 0, held)]
    feed_parts += [to_seat(part, shift + 1) for shift, part in enumerate(feed_sent)]
    qkv_half = add_half(qkv_half, sums["gate"], feed_parts[0])
    qkv_sum = sum_half(qkv_half, 3)
    one_terms = [
        (grad_qkv[index], part, weight, part, 1)
        for index, weight in enumerate(qkv_weights)
        for part in range(3)
    ]
    one_terms[0] = (after(one_terms[0][0], qkv_half), *one_terms[0][1:])
    one_parts = scatter(
        lambda start, rows: sum_products(one_terms, start, rows, BF16 if start else F32)
    )
    (input_grad,), _, norm_one = norm_back(tokens, grad_hidden, gain_first, one_parts, True, 1)
    output = (hidden_one + sum(feed_parts)).astype(BF16)
    grad_down = sums["down"]
    grad_up = whole_sum(sums["up"], input_grad)
    grad_gate = whole_sum(swap_sum(sums["gate"], one_parts[0]), input_grad)
    out_grad = whole_sum(swap_sum(sums["out"], one_parts[0]), input_grad)
    for step in across + along[1:]:
        norm_one = step(norm_one)
    for step in norm_steps:
        norm_two = step(norm_two)
    norms = along[0](jnp.concatenate([norm_one, norm_two], axis=0))
    qkv_grad = whole_sum(swap_sum(qkv_sum, input_grad))

    return (
        output,
        input_grad,
        *(part_of(qkv_grad, part) for part in range(3)),
        out_grad,
        grad_gate,
        grad_up,
        grad_down,
        norms[0],
        norms[1],
        norms[2],
        norms[3],
    )


def solution(mesh):
    rows = P(("dp", "tensor"), None)
    columns = P(None, "tensor")
    depth = P("tensor", None)
    return jax.shard_map(
        functools.partial(shards, mesh.shape["dp"], mesh.shape["tensor"]),
        mesh=mesh,
        in_specs=(
            rows,
            P("dp"),
            P(),
            P(),
            columns,
            columns,
            columns,
            depth,
            P(),
            P(),
            columns,
            columns,
            depth,
            rows,
        ),
        out_specs=(
            rows,
            rows,
            columns,
            columns,
            columns,
            depth,
            columns,
            columns,
            depth,
            P(),
            P(),
            P(),
            P(),
        ),
        check_vma=False,
    )
```

time: 2080 us -> 623 us (0.30)
  waiting for transfers between devices: 844 us -> 60 us
  matrix products: 626 us -> 0 us
  Pallas kernels: 0 us -> 390 us
  local copies, waits for them, and re-layouts: 395 us -> 61.2 us
  other arithmetic: 143 us -> 51.7 us
  blocking collectives: 39.6 us -> 0 us
  starting transfers between devices: 0.37 us -> 37.1 us
    dot_general x236 -> x0, matrix products: 626 us -> none  [the longest x100 229 us: times_transposed(): lax.dot_general(left, right, (((1,), (1,)), ((), ())), preferred_element_...]
    reduce_scatter x4 -> x0, waiting for transfers between devices: 420 us -> none  [the longest x1 126 us: shards(): lax.psum_scatter(jnp.dot(mixed_rows, output_weight, preferred_element_typ...]
    pallas_call x0 -> x37, Pallas kernels: none -> 390 us  [the longest x4 109 us: attend_back(): pl.pallas_call(functools.partial(attend_back_kernel, chunk=chunk), grid_s...]
    psum x1 -> x4, waiting for transfers between devices: 262 us -> 43.7 us  [sum_half(): return lax.psum(value, 'dp', axis_index_groups=groups)]
    all_gather x4 -> x1, waiting for transfers between devices: 161 us -> 0.01 us  [gather_spread(): gathered = lax.all_gather(piece, 'dp', axis=0)]
    while x218 -> x0, local copies, waits for them, and re-layouts: 148 us -> none
    dynamic_slice x80 -> x3, local copies, waits for them, and re-layouts: 55.7 us -> 2.63 us  [the longest x2 2.05 us: spread_windows(): lax.dynamic_slice_in_dim(value, group * size, size, axis=0)]
    reduce_sum x38 -> x0, other arithmetic: 46.8 us -> none  [the longest x32 29.8 us: one_block(): totals = jnp.sum(weights, axis=-1, keepdims=True)]
  transfers between devices with their start and end apart: 9 -> 49, of which waited for: 9 -> 14; matrix products, arithmetic and copies ran while one was open for 6% -> 13% of each run, Pallas kernels for 0% -> 58%
where the time goes in v1:
time: 623 us; the launch traced here: 614 us
  Pallas kernels  390 us (63%)
  local copies, waits for them, and re-layouts  61.2 us (10%)
  waiting for transfers between devices  60 us (10%)
  other arithmetic  51.7 us (8%)
  starting transfers between devices  37.1 us (6%)
  between operations  14.7 us (2%)
    pallas_call x4, Pallas kernels, attend_back(): pl.pallas_call(functools.partial(attend_back_kernel, chunk=chunk), grid_s...  109 us
    pallas_call x10, Pallas kernels, sum_products(): pl.pallas_call(functools.partial(sum_kernel, dims=tuple(dims)), grid=(row...  82.2 us
    pallas_call x2, Pallas kernels, feed(): pl.pallas_call(functools.partial(feed_kernel, chunk=chunk), grid=(units /...  71.4 us
    pallas_call x2, Pallas kernels, attend(): pl.pallas_call(functools.partial(attend_kernel, chunk=chunk), grid_spec=p...  57.1 us
    unnamed x118, local copies, waits for them, and re-layouts  46 us
    psum x4, waiting for transfers between devices, sum_half(): return lax.psum(value, 'dp', axis_index_groups=groups)  43.7 us
    pallas_call x5, Pallas kernels, norm_back(): pl.pallas_call(lambda *refs, held=len(held): norm_back_kernel(*refs[:3 +...  23.2 us
    pallas_call x8, Pallas kernels, norm(): pl.pallas_call(lambda *refs, held=len(held): norm_kernel(*refs[:3 + len(t...  21.3 us
  transfers between devices with their start and end apart: 49, of which 14 were waited for; matrix products, arithmetic and copies ran while one was open for 13% of the time, Pallas kernels for 58%

profile of v1, /device:TPU:0, one launch (start us, length us, event | category | flops | bytes accessed | tf_op | source)
XLA Modules:
  0.0 614.4 jit_solution(6299927193273517239)
XLA Ops:
  47.5 28.3 %attention_forward.2 = (bf16[2048,256]{1,0:T(8,128)(2,1)}, f32[2,8,2048]{2,1,0:T(8,128)}) custom-call(s32[2]{0:T(128)} %pad_add_fusion.place_ref, bf16[2048,256]{1,0:T(8,128)(2,1)} %copy-done.13, bf16[2048,256]{1,0:T(8,128)(2,1)} %copy-done.14, bf16[2048,256]{1,0:T(8,128)(2,1)} %copy-done.15), custom_call_target="tpu_custom_call" | custom-call | flops 1717986944 | bytes 419430 | tf_op jit(solution)/shard_map/attention_forward/pallas_call | solution.py:143
  83.2 6.2 %project_rope.3 = (bf16[2048,256]{1,0:T(8,128)(2,1)S(1)}, bf16[2048,256]{1,0:T(8,128)(2,1)S(1)}, bf16[2048,256]{1,0:T(8,128)(2,1)S(1)}) custom-call(bf16[2048,1024]{1,0:T(8,128)(2,1)S(1)} %copy-done.8, bf16[1024,768]{1,0:T(8,128)(2,1)} %collective-permute-done.5.weight_ref.refs_1_.refs_3_.refs_5_, f32[2048,128]{1,0:T(8,128)S(1)} %get-tuple-element.242.cos_ref.cos_row_ref, ...), custom_call_target="tpu_custom_call" | custom-call | flops 322122560 | bytes 891289 | tf_op jit(solution)/shard_map/project_rope/pallas_call | solution.py:64
  92.3 28.8 %attention_forward.3 = (bf16[2048,256]{1,0:T(8,128)(2,1)}, f32[2,8,2048]{2,1,0:T(8,128)}) custom-call(s32[2]{0:T(128)} %pad_add_fusion.place_ref, bf16[2048,256]{1,0:T(8,128)(2,1)} %copy-done.16, bf16[2048,256]{1,0:T(8,128)(2,1)} %copy-done.17, bf16[2048,256]{1,0:T(8,128)(2,1)} %copy-done.18), custom_call_target="tpu_custom_call" | custom-call | flops 1717986944 | bytes 419430 | tf_op jit(solution)/shard_map/attention_forward/pallas_call | solution.py:143
  154.6 5.7 fusion.7
  160.4 35.7 %feed_forward.2 = (bf16[2048,1024]{1,0:T(8,128)(2,1)}, bf16[2048,1024]{1,0:T(8,128)(2,1)}, bf16[2048,1024]{1,0:T(8,128)(2,1)}, bf16[1024,1024]{1,0:T(8,128)(2,1)...) custom-call(bf16[2048,1024]{1,0:T(8,128)(2,1)} %constant_dynamic-update-slice_fusion.13.rows_ref, ...), custom_call_target="tpu_custom_call" | custom-call | flops 2576980480 | bytes 3355443 | tf_op jit(solution)/shard_map/feed_forward/pallas_call | solution.py:322
  196.2 35.7 %feed_forward.3 = (bf16[2048,1024]{1,0:T(8,128)(2,1)}, bf16[2048,1024]{1,0:T(8,128)(2,1)}, bf16[2048,1024]{1,0:T(8,128)(2,1)}, bf16[1024,1024]{1,0:T(8,128)(2,1)...) custom-call(bf16[2048,1024]{1,0:T(8,128)(2,1)} %constant_dynamic-update-slice_fusion.13.rows_ref, ...), custom_call_target="tpu_custom_call" | custom-call | flops 2576980480 | bytes 3355443 | tf_op jit(solution)/shard_map/feed_forward/pallas_call | solution.py:322
  231.9 15.4 %sum_products.12 = bf16[1024,1024]{1,0:T(8,128)(2,1)} custom-call(bf16[2048,1024]{1,0:T(8,128)(2,1)} %get-tuple-element.142.refs_0_, bf16[1024,1024]{1,0:T(8,128)(2,1)} %bitcast.17, bf16[2048,1024]{1,0:T(8,128)(2,1)} %get-tuple-element.135.refs_2_, bf16[1024,1024]{1,0:T(8,128)(2,1)} %bitcast.14, bf16[2048,1024]{1,0:T(8,128)(2,1)} %get-tuple-element.137.refs_4_, ...), custom_call_target="tpu_custom_call" | custom-call | flops 858993472 | bytes 2097152 | tf_op jit(solution)/shard_map/sum_products/pallas_call | solution.py:368
  253.6 15.4 %sum_products.13.refs_3_ = f32[1024,1024]{1,0:T(8,128)} custom-call(bf16[2048,1024]{1,0:T(8,128)(2,1)} %get-tuple-element.142.refs_0_, bf16[1024,1024]{1,0:T(8,128)(2,1)} %bitcast.18, bf16[2048,1024]{1,0:T(8,128)(2,1)} %get-tuple-element.135.refs_2_, bf16[1024,1024]{1,0:T(8,128)(2,1)} %bitcast.15, bf16[2048,1024]{1,0:T(8,128)(2,1)} %get-tuple-element.137.refs_4_, ...), custom_call_target="tpu_custom_call" | custom-call | flops 858993472 | bytes 2097152 | tf_op jit(solution)/shard_map/sum_products/pallas_call | solution.py:368
  301.9 5.3 sum_products.15.up_ref
  313.5 5.2 sum_products.14.up_ref
  324.6 27.1 %attention_backward.4.rest_0_ = bf16[3,2048,256]{2,1,0:T(8,128)(2,1)} custom-call(s32[2]{0:T(128)} %pad_add_fusion.place_ref, bf16[2048,256]{1,0:T(8,128)(2,1)} %copy-done.16, bf16[2048,256]{1,0:T(8,128)(2,1)} %copy-done.17, bf16[2048,256]{1,0:T(8,128)(2,1)} %copy-done.18, bf16[2048,256]{1,0:T(8,128)(2,1)} %get-tuple-element.122.refs_2_.left_ref.out_ref, ...), custom_call_target="tpu_custom_call" | custom-call | flops 1503238528 | bytes 419430 | tf_op jit(solution)/shard_map/attention_backward/pallas_call | solution.py:242
  362.0 27.2 %attention_backward.5.right_ref.refs_0_.refs_2_.refs_4_ = bf16[3,2048,256]{2,1,0:T(8,128)(2,1)} custom-call(s32[2]{0:T(128)} %pad_add_fusion.place_ref, bf16[2048,256]{1,0:T(8,128)(2,1)} %copy-done.16, bf16[2048,256]{1,0:T(8,128)(2,1)} %copy-done.17, bf16[2048,256]{1,0:T(8,128)(2,1)} %copy-done.18, ...), custom_call_target="tpu_custom_call", output_to_operand_aliasing={{}: (11, {})} | custom-call | flops 1503238528 | bytes 419430 | tf_op jit(solution)/shard_map/attention_backward/pallas_call | solution.py:242
  393.3 5.1 outer_product.6
  412.2 27.6 %attention_backward.6.rest_0_ = bf16[3,2048,256]{2,1,0:T(8,128)(2,1)} custom-call(s32[2]{0:T(128)} %pad_add_fusion.place_ref, bf16[2048,256]{1,0:T(8,128)(2,1)} %copy-done.13, bf16[2048,256]{1,0:T(8,128)(2,1)} %copy-done.14, bf16[2048,256]{1,0:T(8,128)(2,1)} %copy-done.15, bf16[2048,256]{1,0:T(8,128)(2,1)} %get-tuple-element.115.refs_0_.left_ref.out_ref, ...), custom_call_target="tpu_custom_call" | custom-call | flops 1503238528 | bytes 419430 | tf_op jit(solution)/shard_map/attention_backward/pallas_call | solution.py:242
  445.2 9.8 %all-reduce.8.cloned.1.call-done = bf16[512,1024]{1,0:T(8,128)(2,1)} async-done(((bf16[512,1024]{1,0:T(8,128)(2,1)}), bf16[512,1024]{1,0:T(8,128)(2,1)}) %all-reduce.8.cloned.1.call-update) | async-done | bytes 1048592 | tf_op jit(solution)/shard_map/psum | solution.py:722
  455.1 27.1 %attention_backward.7.right_ref.refs_6_.refs_8_.refs_10_ = bf16[3,2048,256]{2,1,0:T(8,128)(2,1)} custom-call(s32[2]{0:T(128)} %pad_add_fusion.place_ref, bf16[2048,256]{1,0:T(8,128)(2,1)} %copy-done.13, bf16[2048,256]{1,0:T(8,128)(2,1)} %copy-done.14, bf16[2048,256]{1,0:T(8,128)(2,1)} %copy-done.15, ...), custom_call_target="tpu_custom_call", output_to_operand_aliasing={{}: (11, {})} | custom-call | flops 1503238528 | bytes 419430 | tf_op jit(solution)/shard_map/attention_backward/pallas_call | solution.py:242
  486.4 5.1 outer_product.7
  495.6 8.6 %sum_products.16 = bf16[1024,1024]{1,0:T(8,128)(2,1)} custom-call(bf16[2048,1024]{1,0:T(8,128)(2,1)} %get-tuple-element.189.refs_0_, bf16[1024,1024]{1,0:T(8,128)(2,1)} %bitcast.20, bf16[2048,1024]{1,0:T(8,128)(2,1)} %get-tuple-element.188.refs_2_, bf16[1024,1024]{1,0:T(8,128)(2,1)} %refs_3_.3), custom_call_target="tpu_custom_call" | custom-call | flops 429496736 | bytes 1258291 | tf_op jit(solution)/shard_map/sum_products/pallas_call | solution.py:368
  504.2 8.9 %sum_products.17 = f32[1024,1024]{1,0:T(8,128)} custom-call(bf16[2048,1024]{1,0:T(8,128)(2,1)} %get-tuple-element.189.refs_0_, bf16[1024,1024]{1,0:T(8,128)(2,1)} %bitcast.21, bf16[2048,1024]{1,0:T(8,128)(2,1)} %get-tuple-element.188.refs_2_, bf16[1024,1024]{1,0:T(8,128)(2,1)} %refs_3_.3), custom_call_target="tpu_custom_call" | custom-call | flops 429496736 | bytes 1258291 | tf_op jit(solution)/shard_map/sum_products/pallas_call | solution.py:368
  518.8 7.4 %sum_products.19 = bf16[1024,1024]{1,0:T(8,128)(2,1)} custom-call(bf16[3,2048,256]{2,1,0:T(8,128)(2,1)} %attention_backward.5.right_ref.refs_0_.refs_2_.refs_4_, bf16[1024,768]{1,0:T(8,128)(2,1)} %collective-permute-done.5.weight_ref.refs_1_.refs_3_.refs_5_, bf16[3,2048,256]{2,1,0:T(8,128)(2,1)} %attention_backward.5.right_ref.refs_0_.refs_2_.refs_4_, ...), custom_call_target="tpu_custom_call" | custom-call | flops 322122560 | bytes 1048576 | tf_op jit(solution)/shard_map/sum_products/pallas_call | solution.py:368
  526.3 7.6 %sum_products.18.refs_3_ = f32[1024,1024]{1,0:T(8,128)} custom-call(bf16[3,2048,256]{2,1,0:T(8,128)(2,1)} %attention_backward.5.right_ref.refs_0_.refs_2_.refs_4_, bf16[1024,768]{1,0:T(8,128)(2,1)} %collective-permute-done.5.weight_ref.refs_1_.refs_3_.refs_5_, bf16[3,2048,256]{2,1,0:T(8,128)(2,1)} %attention_backward.5.right_ref.refs_0_.refs_2_.refs_4_, ...), custom_call_target="tpu_custom_call" | custom-call | flops 322122560 | bytes 1048576 | tf_op jit(solution)/shard_map/sum_products/pallas_call | solution.py:368
  537.4 6.0 add_convert_fusion
  543.5 7.8 %layer_norm_backward.9 = (bf16[1024,1024]{1,0:T(8,128)(2,1)}, f32[2,1024]{1,0:T(2,128)}) custom-call(bf16[1024,1024]{1,0:T(8,128)(2,1)} %refs_0_.13, f32[1024,1024]{1,0:T(8,128)} %get-tuple-element.190.refs_1_, f32[1,1024]{1,0:T(1,128)} %bitcast.35, f32[1024,1024]{1,0:T(8,128)} %sum_products.18.refs_3_, bf16[1024,1024]{1,0:T(8,128)(2,1)} %collective-permute-done.34.refs_4_), custom_call_target="tpu_custom_call" | custom-call | flops 3145728 | bytes 1677721 | tf_op jit(solution)/shard_map/layer_norm_backward/pallas_call | solution.py:518
  551.3 28.0 %all-reduce.10.cloned.1.call-done = bf16[512,768]{1,0:T(8,128)(2,1)} async-done(((bf16[512,768]{1,0:T(8,128)(2,1)}), bf16[512,768]{1,0:T(8,128)(2,1)}) %all-reduce.10.cloned.1.call-update) | async-done | bytes 786448 | tf_op jit(solution)/shard_map/psum | solution.py:722
  (283 shorter events, 214.4 us)
Async XLA Ops:
  7.2 147.5 %all-gather.3.cloned.1.call-start = ((), (), s32[]{:S(2)}) async-start(), calls=%async_computation.3 | async-start | bytes 7077888 | tf_op jit(solution)/shard_map/all_gather | solution.py:632
  10.2 34.9 %collective-permute-start.4 = (bf16[384,1024]{1,0:T(8,128)(2,1)}, bf16[384,1024]{1,0:T(8,128)(2,1)}, u32[]{:S(2)}, u32[]{:S(2)}) collective-permute-start(bf16[384,1024]{1,0:T(8,128)(2,1)} %pad_maximum_fusion.2), channel_id=1, source_target_pairs={{2,0},{3,1},{0,2},{1,3},{6,4},{7,5},{4,6},{5,7},{10,8},{11,9},{8,1... | collective-permute-start | bytes 2359304 | tf_op jit(solution)/shard_map/ppermute | solution.py:602
  45.2 308.9 %all-reduce.6.cloned.1.call-start = ((), (), s32[]{:S(2)}) async-start(), calls=%async_computation | async-start | bytes 2097152 | tf_op jit(solution)/shard_map/psum | solution.py:722
  45.5 32.6 %collective-permute-start.6 = (bf16[1024,1024]{1,0:T(8,128)(2,1)}, bf16[1024,1024]{1,0:T(8,128)(2,1)}, u32[]{:S(2)}, u32[]{:S(2)}) collective-permute-start(bf16[1024,1024]{1,0:T(8,128)(2,1)} %refs_1_.12), channel_id=1, source_target_pairs={{1,0},{0,1},{3,2},{2,3},{5,4},{4,5},{7,6},{6,7},{9,8},{8,9},{11,10... | collective-permute-start | bytes 6291464 | tf_op jit(solution)/shard_map/ppermute | solution.py:595
  45.6 37.5 %collective-permute-start.5 = (bf16[1024,768]{1,0:T(8,128)(2,1)}, bf16[1024,768]{1,0:T(8,128)(2,1)}, u32[]{:S(2)}, u32[]{:S(2)}) collective-permute-start(bf16[1024,768]{1,0:T(8,128)(2,1)} %copy-done.4), channel_id=1, source_target_pairs={{2,0},{3,1},{0,2},{1,3},{6,4},{7,5},{4,6},{5,7},{10,8},{11,9},{8,1... | collective-permute-start | bytes 4718600 | tf_op jit(solution)/shard_map/ppermute | solution.py:602
  75.9 45.3 %collective-permute-start.7 = (bf16[256,1024]{1,0:T(8,128)(2,1)S(1)}, bf16[256,1024]{1,0:T(8,128)(2,1)S(1)}, u32[]{:S(2)}, u32[]{:S(2)}) collective-permute-start(bf16[256,1024]{1,0:T(8,128)(2,1)S(1)} %copy-done.24), channel_id=1, source_target_pairs={{2,0},{3,1},{0,2},{1,3},{6,4},{7,5},{4,6},{5,7},{10,8},{11,9},{8,1... | collective-permute-start | bytes 1572872 | tf_op jit(solution)/shard_map/ppermute | solution.py:602
  196.1 53.3 %collective-permute-start.13 = (bf16[1024,1024]{1,0:T(8,128)(2,1)}, bf16[1024,1024]{1,0:T(8,128)(2,1)}, u32[]{:S(2)}, u32[]{:S(2)}) collective-permute-start(bf16[1024,1024]{1,0:T(8,128)(2,1)} %get-tuple-element.134), channel_id=1, source_target_pairs={{2,0},{3,1},{0,2},{1,3},{6,4},{7,5},{4,6},{5,7},{10,8},{11,9},{8,1... | collective-permute-start | bytes 6291464 | tf_op jit(solution)/shard_map/ppermute | solution.py:602
  247.5 71.2 %collective-permute-start.20 = (bf16[1024,1024]{1,0:T(8,128)(2,1)}, bf16[1024,1024]{1,0:T(8,128)(2,1)}, u32[]{:S(2)}, u32[]{:S(2)}) collective-permute-start(bf16[1024,1024]{1,0:T(8,128)(2,1)} %get-tuple-element.153), channel_id=1, source_target_pairs={{2,0},{3,1},{0,2},{1,3},{6,4},{7,5},{4,6},{5,7},{10,8},{11,9},{8,1... | collective-permute-start | bytes 6291464 | tf_op jit(solution)/shard_map/ppermute | solution.py:602
  274.3 26.0 %collective-permute-start.19 = (bf16[512,1024]{1,0:T(8,128)(2,1)}, bf16[512,1024]{1,0:T(8,128)(2,1)S(1)}, u32[]{:S(2)}, u32[]{:S(2)}) collective-permute-start(bf16[512,1024]{1,0:T(8,128)(2,1)} %get-tuple-element.214), channel_id=1, source_target_pairs={{0,4},{4,0},{8,12},{12,8},{16,20},{20,16},{24,28},{28,24},{1,5},{5... | collective-permute-start | bytes 3145736 | tf_op jit(solution)/shard_map/ppermute | solution.py:710
  296.3 102.1 %collective-permute-start.25 = (bf16[1024,1024]{1,0:T(8,128)(2,1)}, bf16[1024,1024]{1,0:T(8,128)(2,1)}, u32[]{:S(2)}, u32[]{:S(2)}) collective-permute-start(bf16[1024,1024]{1,0:T(8,128)(2,1)} %get-tuple-element.169), channel_id=1, source_target_pairs={{2,0},{3,1},{0,2},{1,3},{6,4},{7,5},{4,6},{5,7},{10,8},{11,9},{8,1... | collective-permute-start | bytes 6291464 | tf_op jit(solution)/shard_map/ppermute | solution.py:602
  301.8 153.2 %all-reduce.8.cloned.1.call-start = ((), (), s32[]{:S(2)}) async-start(), calls=%async_computation.1 | async-start | bytes 2097152 | tf_op jit(solution)/shard_map/psum | solution.py:722
  322.3 37.1 %collective-permute-start.22 = (bf16[512,1024]{1,0:T(8,128)(2,1)}, bf16[512,1024]{1,0:T(8,128)(2,1)}, u32[]{:S(2)}, u32[]{:S(2)}) collective-permute-start(bf16[512,1024]{1,0:T(8,128)(2,1)} %get-tuple-element.213), channel_id=1, source_target_pairs={{0,4},{4,0},{8,12},{12,8},{16,20},{20,16},{24,28},{28,24},{1,5},{5... | collective-permute-start | bytes 3145736 | tf_op jit(solution)/shard_map/ppermute | solution.py:710
  354.1 54.0 %collective-permute-start.27 = (bf16[512,1024]{1,0:T(8,128)(2,1)}, bf16[512,1024]{1,0:T(8,128)(2,1)}, u32[]{:S(2)}, u32[]{:S(2)}) collective-permute-start(bf16[512,1024]{1,0:T(8,128)(2,1)} %all-reduce.6.cloned.1.call-done), channel_id=1, source_target_pairs={{0,4},{4,0},{8,12},{12,8},{16,20},{20,16},{24,28},{28,24},{1,5},{5... | collective-permute-start | bytes 3145736 | tf_op jit(solution)/shard_map/ppermute | solution.py:726
  357.1 47.4 %collective-permute-start.26 = (bf16[256,1024]{1,0:T(8,128)(2,1)S(1)}, bf16[256,1024]{1,0:T(8,128)(2,1)S(1)}, u32[]{:S(2)}, u32[]{:S(2)}) collective-permute-start(bf16[256,1024]{1,0:T(8,128)(2,1)S(1)} %copy-done.20), channel_id=1, source_target_pairs={{2,0},{3,1},{0,2},{1,3},{6,4},{7,5},{4,6},{5,7},{10,8},{11,9},{8,1... | collective-permute-start | bytes 1572872 | tf_op jit(solution)/shard_map/ppermute | solution.py:602
  402.3 37.5 %collective-permute-start.29 = (bf16[512,1024]{1,0:T(8,128)(2,1)}, bf16[512,1024]{1,0:T(8,128)(2,1)}, u32[]{:S(2)}, u32[]{:S(2)}) collective-permute-start(bf16[512,1024]{1,0:T(8,128)(2,1)} %get-tuple-element.211), channel_id=1, source_target_pairs={{0,4},{4,0},{8,12},{12,8},{16,20},{20,16},{24,28},{28,24},{1,5},{5... | collective-permute-start | bytes 3145736 | tf_op jit(solution)/shard_map/ppermute | solution.py:710
  402.9 113.7 %all-reduce.12.cloned.1.call-start = ((), (), s32[]{:S(2)}) async-start(), calls=%async_computation.4 | async-start | bytes 2621440 | tf_op jit(solution)/shard_map/psum | solution.py:722
  402.9 88.5 %collective-permute-start.24 = (bf16[1024,768]{1,0:T(8,128)(2,1)S(1)}, bf16[1024,768]{1,0:T(8,128)(2,1)}, u32[]{:S(2)}, u32[]{:S(2)}) collective-permute-start(bf16[1024,768]{1,0:T(8,128)(2,1)S(1)} %outer_product.6), channel_id=1, source_target_pairs={{2,0},{3,1},{0,2},{1,3},{6,4},{7,5},{4,6},{5,7},{10,8},{11,9},{8,1... | collective-permute-start | bytes 4718600 | tf_op jit(solution)/shard_map/ppermute | solution.py:602
  406.0 33.8 %collective-permute-start.30 = (bf16[128,1024]{1,0:T(8,128)(2,1)S(1)}, bf16[128,1024]{1,0:T(8,128)(2,1)S(1)}, u32[]{:S(2)}, u32[]{:S(2)}) collective-permute-start(bf16[128,1024]{1,0:T(8,128)(2,1)S(1)} %get-tuple-element.229), channel_id=1, source_target_pairs={{0,4},{4,0},{8,12},{12,8},{16,20},{20,16},{24,28},{28,24},{1,5},{5... | collective-permute-start | bytes 786440 | tf_op jit(solution)/shard_map/ppermute | solution.py:710
  455.1 124.3 %all-reduce.10.cloned.1.call-start = ((), (), s32[]{:S(2)}) async-start(), calls=%async_computation.2 | async-start | bytes 1572864 | tf_op jit(solution)/shard_map/psum | solution.py:722
  504.1 33.3 %collective-permute-start.32 = (bf16[1024,1024]{1,0:T(8,128)(2,1)}, bf16[1024,1024]{1,0:T(8,128)(2,1)S(1)}, u32[]{:S(2)}, u32[]{:S(2)}) collective-permute-start(bf16[1024,1024]{1,0:T(8,128)(2,1)} %sum_products.16), channel_id=1, source_target_pairs={{1,0},{0,1},{3,2},{2,3},{5,4},{4,5},{7,6},{6,7},{9,8},{8,9},{11,10... | collective-permute-start | bytes 6291464 | tf_op jit(solution)/shard_map/ppermute | solution.py:595
  533.8 47.0 %collective-permute-start.37 = (bf16[512,1024]{1,0:T(8,128)(2,1)}, bf16[512,1024]{1,0:T(8,128)(2,1)}, u32[]{:S(2)}, u32[]{:S(2)}) collective-permute-start(bf16[512,1024]{1,0:T(8,128)(2,1)} %get-tuple-element.200), channel_id=1, source_target_pairs={{0,4},{4,0},{8,12},{12,8},{16,20},{20,16},{24,28},{28,24},{1,5},{5... | collective-permute-start | bytes 3145736 | tf_op jit(solution)/shard_map/ppermute | solution.py:726
  535.3 47.3 %collective-permute-start.38 = (bf16[512,1024]{1,0:T(8,128)(2,1)}, bf16[512,1024]{1,0:T(8,128)(2,1)}, u32[]{:S(2)}, u32[]{:S(2)}) collective-permute-start(bf16[512,1024]{1,0:T(8,128)(2,1)} %all-reduce.8.cloned.1.call-done), channel_id=1, source_target_pairs={{0,4},{4,0},{8,12},{12,8},{16,20},{20,16},{24,28},{28,24},{1,5},{5... | collective-permute-start | bytes 3145736 | tf_op jit(solution)/shard_map/ppermute | solution.py:726
  535.9 52.2 %collective-permute-start.36 = (bf16[128,1024]{1,0:T(8,128)(2,1)S(1)}, bf16[128,1024]{1,0:T(8,128)(2,1)S(1)}, u32[]{:S(2)}, u32[]{:S(2)}) collective-permute-start(bf16[128,1024]{1,0:T(8,128)(2,1)S(1)} %copy-done.40), channel_id=1, source_target_pairs={{0,4},{4,0},{8,12},{12,8},{16,20},{20,16},{24,28},{28,24},{1,5},{5... | collective-permute-start | bytes 786440 | tf_op jit(solution)/shard_map/ppermute | solution.py:726
  579.4 26.1 %collective-permute-start.35 = (bf16[512,768]{1,0:T(8,128)(2,1)}, bf16[512,768]{1,0:T(8,128)(2,1)S(1)}, u32[]{:S(2)}, u32[]{:S(2)}) collective-permute-start(bf16[512,768]{1,0:T(8,128)(2,1)} %all-reduce.10.cloned.1.call-done), channel_id=1, source_target_pairs={{0,4},{4,0},{8,12},{12,8},{16,20},{20,16},{24,28},{28,24},{1,5},{5... | collective-permute-start | bytes 2359304 | tf_op jit(solution)/shard_map/ppermute | solution.py:726
  (72 other events, 653.6 us)
Sparse Core Ops, SparseCore 0:
  45.3 99.3 all-gather.2
  301.9 52.1 all-reduce.5
  403.0 51.9 all-reduce.7
  457.3 59.2 all-reduce.11
  536.0 43.3 all-reduce.9

commit v2 on v1

--- a/solution.py
+++ b/solution.py
@@ -18,7 +18,7 @@
 F32 = jnp.float32
 MIB = 1 << 20
 COST_SHARE = 0.1
-PIECES = 4
+PIECES = 2
 
 
 def contract(left, right, left_dim, right_dim):
@@ -45,9 +45,49 @@
     )
 
 
-def project_kernel(rows_ref, weight_ref, cos_ref, sin_ref, q_ref, k_ref, v_ref):
+def fetch(pieces, rows, sems):
+    copies, start = [], 0
+    for index, piece in enumerate(pieces):
+        count = piece.shape[0]
+        copies.append(
+            pltpu.make_async_copy(piece, rows.at[pl.ds(start, count), :], sems.at[index])
+        )
+        start += count
+    for copy in copies:
+        copy.start()
+    return copies
+
+
+def room(pieces):
+    count = sum(piece.shape[0] for piece in pieces)
+    return [
+        pltpu.VMEM((count, pieces[0].shape[1]), BF16),
+        pltpu.SemaphoreType.DMA((len(pieces),)),
+    ]
+
+
+def unpacked(ref):
+    value = ref[...]
+    return value.reshape(-1, value.shape[-1]) if value.ndim == 3 else value
+
+
+def packed(weight):
+    return isinstance(weight, tuple)
+
+
+def project_kernel(*refs, count):
+    pieces = refs[:count]
+    weight_ref, cos_ref, sin_ref, q_ref, k_ref, v_ref, rows, sems = refs[count:]
     columns = q_ref.shape[1]
-    product = contract(rows_ref[...], weight_ref[...], 1, 0)
+    block = q_ref.shape[0]
+
+    @pl.when(pl.program_id(0) == 0)
+    def _():
+        for copy in fetch(pieces, rows, sems):
+            copy.wait()
+
+    start = pl.multiple_of(pl.program_id(0) * block, block)
+    product = contract(rows[pl.ds(start, block), :], weight_ref[...], 1, 0)
     cosines = jnp.concatenate([cos_ref[...]] * (columns // LANES), axis=1)
     sines = jnp.concatenate([sin_ref[...]] * (columns // LANES), axis=1)
     for part, out_ref in ((0, q_ref), (1, k_ref)):
@@ -56,26 +96,27 @@
     v_ref[...] = product[:, 2 * columns :].astype(BF16)
 
 
-def project(rows, weight, cosines, sines, block=512):
-    count, width = rows.shape
+def project(pieces, weight, cosines, sines, block=512):
+    width = weight.shape[0]
     columns = weight.shape[1] // 3
+    count = sum(piece.shape[0] for piece in pieces)
     table = pl.BlockSpec((block, LANES), lambda i: (i, 0))
     out = pl.BlockSpec((block, columns), lambda i: (i, 0))
     return pl.pallas_call(
-        project_kernel,
+        functools.partial(project_kernel, count=len(pieces)),
         grid=(count // block,),
-        in_specs=[
-            pl.BlockSpec((block, width), lambda i: (i, 0)),
-            pl.BlockSpec(weight.shape, lambda i: (0, 0)),
-            table,
-            table,
-        ],
+        in_specs=[pl.BlockSpec(memory_space=pl.ANY)] * len(pieces)
+        + [pl.BlockSpec(weight.shape, lambda i: (0, 0)), table, table],
         out_specs=[out, out, out],
         out_shape=[jax.ShapeDtypeStruct((count, columns), BF16)] * 3,
-        cost_estimate=cost(2 * count * width * 3 * columns, 2 * (count * width + width * 3 * columns + count * 3 * columns), 0),
+        scratch_shapes=room(pieces),
+        cost_estimate=cost(
+            2 * count * width * 3 * columns,
+            2 * (count * width + width * 3 * columns + count * 3 * columns),
+        ),
         compiler_params=pltpu.CompilerParams(vmem_limit_bytes=40 * MIB),
         name="project_rope",
-    )(rows, weight, cosines, sines)
+    )(*pieces, weight, cosines, sines)
 
 
 def masked_keys(place_ref, key_ref, masked_ref):
@@ -272,33 +313,27 @@
     )(place, queries, keys, values, mixed, upstream, logs, cosines, sines, cosines, sines, *held)
 
 
-def feed_kernel(
-    rows_ref,
-    target_ref,
-    gate_ref,
-    up_ref,
-    down_ref,
-    inner_ref,
-    grad_gate_ref,
-    grad_up_ref,
-    weight_gate_ref,
-    weight_up_ref,
-    weight_down_ref,
-    rows_t,
-    target_t,
-    *,
-    chunk,
-):
+def feed_kernel(*refs, counts, chunk):
+    row_pieces, target_pieces = refs[: counts[0]], refs[counts[0] : sum(counts)]
+    refs = refs[sum(counts) :]
+    gate_ref, up_ref, down_ref, inner_ref, grad_gate_ref, grad_up_ref = refs[:6]
+    weight_gate_ref, weight_up_ref, weight_down_ref = refs[6:9]
+    rows, row_sems, target, target_sems, rows_t, target_t = refs[9:]
+
     @pl.when(pl.program_id(0) == 0)
     def _():
-        rows_t[...] = rows_ref[...].T
-        target_t[...] = target_ref[...].T
-
-    for start in range(0, rows_ref.shape[0], chunk):
+        copies = fetch(row_pieces, rows, row_sems) + fetch(target_pieces, target, target_sems)
+        for copy in copies:
+            copy.wait()
+        rows_t[...] = rows[...].T
+        target_t[...] = target[...].T
+
+    gate_weight, up_weight, down_weight = unpacked(gate_ref), unpacked(up_ref), unpacked(down_ref)
+    for start in range(0, rows.shape[0], chunk):
         span = slice(start, start + chunk)
-        gate = contract(rows_ref[span, :], gate_ref[...], 1, 0)
-        up = contract(rows_ref[span, :], up_ref[...], 1, 0)
-        grad_inner = contract(target_ref[span, :], down_ref[...], 1, 1)
+        gate = contract(rows[span, :], gate_weight, 1, 0)
+        up = contract(rows[span, :], up_weight, 1, 0)
+        grad_inner = contract(target[span, :], down_weight, 1, 1)
         share = jax.nn.sigmoid(gate)
         activated = gate * share
         inner_ref[span, :] = (activated * up).astype(BF16)
@@ -311,23 +346,37 @@
     weight_down_ref[...] = contract(target_t[...], inner_ref[...], 1, 0).T.astype(BF16)
 
 
-def feed(rows, target, gate_weight, up_weight, down_weight, block=256, chunk=512):
-    count, width = rows.shape
-    units = gate_weight.shape[1]
+def feed(rows, target, weights, block=256, chunk=512):
+    count = sum(piece.shape[0] for piece in rows)
+    width = rows[0].shape[1]
+    across_spec = lambda units: pl.BlockSpec((width, min(block, units)), lambda i: (0, i))
+    down_spec = lambda units: pl.BlockSpec((min(block, units), width), lambda i: (i, 0))
+    if packed(weights[0]):
+        units = width
+        replicas, deep = weights[0][0].shape[0], width // weights[0][0].shape[0]
+        specs = [
+            pl.BlockSpec((replicas, deep, block), lambda i, plane=weights[k][1]: (0, plane, i))
+            for k in range(2)
+        ] + [
+            pl.BlockSpec(
+                (block // deep, deep, width), lambda i, plane=weights[2][1]: (i, plane, 0)
+            )
+        ]
+        weights = [weight for weight, _ in weights]
+    else:
+        units = weights[0].shape[1]
+        specs = [across_spec(units)] * 2 + [down_spec(units)]
     block = min(block, units)
-    whole = pl.BlockSpec((count, width), lambda i: (0, 0), pipeline_mode=pl.Buffered(1))
-    across = pl.BlockSpec((width, block), lambda i: (0, i))
-    down = pl.BlockSpec((block, width), lambda i: (i, 0))
     out = pl.BlockSpec((count, block), lambda i: (0, i))
     return pl.pallas_call(
-        functools.partial(feed_kernel, chunk=chunk),
+        functools.partial(feed_kernel, counts=(len(rows), len(target)), chunk=chunk),
         grid=(units // block,),
-        in_specs=[whole, whole, across, across, down],
-        out_specs=[out, out, out, across, across, down],
+        in_specs=[pl.BlockSpec(memory_space=pl.ANY)] * (len(rows) + len(target)) + specs,
+        out_specs=[out, out, out] + [across_spec(units)] * 2 + [down_spec(units)],
         out_shape=[jax.ShapeDtypeStruct((count, units), BF16)] * 3
         + [jax.ShapeDtypeStruct((width, units), BF16)] * 2
         + [jax.ShapeDtypeStruct((units, width), BF16)],
-        scratch_shapes=[pltpu.VMEM((width, count), BF16)] * 2,
+        scratch_shapes=room(rows) + room(target) + [pltpu.VMEM((width, count), BF16)] * 2,
         cost_estimate=cost(
             12 * count * width * units,
             4 * count * width + 12 * width * units + 6 * count * units,
@@ -335,13 +384,13 @@
         ),
         compiler_params=pltpu.CompilerParams(vmem_limit_bytes=60 * MIB),
         name="feed_forward",
-    )(rows, target, gate_weight, up_weight, down_weight)
+    )(*rows, *target, *weights)
 
 
 def sum_kernel(*refs, dims):
     total = 0.0
     for index, dim in enumerate(dims):
-        total = total + contract(refs[2 * index][...], refs[2 * index + 1][...], 1, dim)
+        total = total + contract(refs[2 * index][...], unpacked(refs[2 * index + 1]), 1, dim)
     refs[-1][...] = total.astype(refs[-1].dtype)
 
 
@@ -357,9 +406,19 @@
             specs.append(
                 pl.BlockSpec((None, block, depth), lambda i, plane=plane: (plane, first + i, 0))
             )
-        shape = right.shape if part is None else (right.shape[0], depth)
-        column = 0 if part is None else part
-        specs.append(pl.BlockSpec(shape, lambda i, column=column: (0, column)))
+        if packed(right):
+            right, plane = right
+            replicas, deep = right.shape[0], right.shape[2] // right.shape[0]
+            shape = (right.shape[2], right.shape[2])
+            specs.append(
+                pl.BlockSpec(
+                    (replicas, deep, right.shape[2]), lambda i, plane=plane: (0, plane, 0)
+                )
+            )
+        else:
+            shape = right.shape if part is None else (right.shape[0], depth)
+            column = 0 if part is None else part
+            specs.append(pl.BlockSpec(shape, lambda i, column=column: (0, column)))
         operands += [left, right]
         dims.append(dim)
         width = shape[1 - dim]
@@ -377,41 +436,70 @@
     )(*operands)
 
 
-def outer_kernel(left_ref, right_ref, out_ref, left_t):
+def outer_kernel(*refs, count):
+    right_ref, out_ref, left, sems, left_t = refs[count:]
+
     @pl.when(pl.program_id(0) == 0)
     def _():
-        left_t[...] = left_ref[...].T
+        for copy in fetch(refs[:count], left, sems):
+            copy.wait()
+        left_t[...] = left[...].T
 
     out_ref[...] = contract(left_t[...], right_ref[...], 1, 0).astype(BF16)
 
 
-def outer(left, right, block):
-    count, width = left.shape
-    columns = right.shape[-1]
-    if right.ndim == 3:
-        steps = right.shape[0]
-        block = columns
-        spec = pl.BlockSpec((None, count, columns), lambda i: (i, 0, 0))
-    else:
-        steps = columns // block
-        spec = pl.BlockSpec((count, block), lambda i: (0, i))
+def outer(pieces, right):
+    width = pieces[0].shape[1]
+    planes, count, columns = right.shape
     return pl.pallas_call(
-        outer_kernel,
-        grid=(steps,),
-        in_specs=[
-            pl.BlockSpec((count, width), lambda i: (0, 0), pipeline_mode=pl.Buffered(1)),
-            spec,
-        ],
-        out_specs=pl.BlockSpec((width, block), lambda i: (0, i)),
-        out_shape=jax.ShapeDtypeStruct((width, steps * block), BF16),
-        scratch_shapes=[pltpu.VMEM((width, count), BF16)],
+        functools.partial(outer_kernel, count=len(pieces)),
+        grid=(planes,),
+        in_specs=[pl.BlockSpec(memory_space=pl.ANY)] * len(pieces)
+        + [pl.BlockSpec((None, count, columns), lambda i: (i, 0, 0))],
+        out_specs=pl.BlockSpec((width, columns), lambda i: (0, i)),
+        out_shape=jax.ShapeDtypeStruct((width, planes * columns), BF16),
+        scratch_shapes=room(pieces) + [pltpu.VMEM((width, count), BF16)],
         cost_estimate=cost(
-            2 * count * width * steps * block,
-            2 * count * (width + steps * block) + 2 * width * steps * block,
+            2 * count * width * planes * columns,
+            2 * count * (width + planes * columns) + 2 * width * planes * columns,
         ),
         compiler_params=pltpu.CompilerParams(vmem_limit_bytes=40 * MIB),
         name="outer_product",
-    )(left, right)
+    )(*pieces, right)
+
+
+def branch_kernel(*refs, count, groups, chunk):
+    weights = refs[count : count + groups]
+    mixed = refs[count + groups : count + 2 * groups]
+    outs = refs[count + 2 * groups : count + 4 * groups]
+    rows, sems = refs[count + 4 * groups :]
+    for copy in fetch(refs[:count], rows, sems):
+        copy.wait()
+    for index in range(groups):
+        outs[groups + index][...] = contract(mixed[index][...].T, rows[...], 1, 0).astype(BF16)
+        for start in range(0, rows.shape[0], chunk):
+            span = slice(start, start + chunk)
+            outs[index][span, :] = contract(rows[span, :], weights[index][...], 1, 1).astype(BF16)
+
+
+def branch_back(pieces, weights, mixed, chunk=512):
+    count = sum(piece.shape[0] for piece in pieces)
+    width = pieces[0].shape[1]
+    groups = len(weights)
+    vmem = pl.BlockSpec(memory_space=pltpu.VMEM)
+    columns = [weight.shape[0] for weight in weights]
+    results = pl.pallas_call(
+        functools.partial(branch_kernel, count=len(pieces), groups=groups, chunk=chunk),
+        in_specs=[pl.BlockSpec(memory_space=pl.ANY)] * len(pieces) + [vmem] * (2 * groups),
+        out_specs=[vmem] * (2 * groups),
+        out_shape=[jax.ShapeDtypeStruct((count, size), BF16) for size in columns]
+        + [jax.ShapeDtypeStruct((size, width), BF16) for size in columns],
+        scratch_shapes=room(pieces),
+        cost_estimate=cost(4 * count * width * sum(columns), 6 * count * width),
+        compiler_params=pltpu.CompilerParams(vmem_limit_bytes=48 * MIB),
+        name="branch_backward",
+    )(*pieces, *weights, *mixed)
+    return results[:groups], results[groups:]
 
 
 def standardize(value):
@@ -605,9 +693,7 @@
         return from_window(value, windows - shift)
 
     def gather_rows(value):
-        return jnp.concatenate(
-            value + [from_seat(piece, s) for s in range(1, span) for piece in value], axis=0
-        )
+        return value + [from_seat(piece, s) for s in range(1, span) for piece in value]
 
     def scatter(partial):
         sent = [to_seat(partial(s * held, held), s) for s in range(1, span)]
@@ -630,6 +716,8 @@
 
     def gather_spread(values, piece):
         gathered = lax.all_gather(piece, "dp", axis=0)
+        if all(value.shape == (width, width) for value in values):
+            return [(gathered, plane) for plane in range(len(values))]
         out, start = [], 0
         for value in values:
             count = value.size // width // dp_size
@@ -639,6 +727,9 @@
 
     def after(value, *others):
         return lax.optimization_barrier((value, *others))[0]
+
+    def pieces_after(pieces, *others):
+        return [after(pieces[0], *others)] + pieces[1:]
 
     place = jnp.stack(
         [lax.dynamic_index_in_dim(lengths, window, keepdims=False), seat * held]
@@ -674,13 +765,13 @@
             slices = [after(piece, parts[0]) for piece in slices]
             feed_shards = [feed_weights]
             feed_shards += [gather_spread(feed_weights, piece) for piece in slices]
-        waits = slices if not qkv else [target]
+        waits = slices if not qkv else target
         qkv.append((after(parts[0], *waits), *parts[1:]))
         attended.append(attend(place, *qkv[-1]))
         if len(attended) == 1:
             sent = after(output_weight, attended[0][0])
             output_shards = [output_weight] + all_windows(sent)[1:]
-        rows_one = after(full_one, attended[-1][0])
+        rows_one = pieces_after(full_one, attended[-1][0])
 
     out_weights = [joined([output_shards[s] for s in group], 0) for group in members]
     mixer_terms = [
@@ -737,8 +828,8 @@
     fed = {}
     rows_two = full_two
     for s in order:
-        fed[s] = feed(rows_two, target, *feed_shards[s])
-        rows_two = after(full_two, fed[s][0])
+        fed[s] = feed(rows_two, target, feed_shards[s])
+        rows_two = pieces_after(full_two, fed[s][0])
     down_pieces, up_pieces, gate_pieces = (
         send_to_owner({s: fed[s][k] for s in order}) + [fed[0][k]] for k in (5, 4, 3)
     )
@@ -764,17 +855,17 @@
     grad_branch = gather_rows(grad_branch_own)
     down_half = add_half(down_half, *grad_branch_own)
     down_sum = sum_half(down_half, 0)
-    grad_branch = after(grad_branch, down_half)
+    grad_branch = pieces_after(grad_branch, down_half)
 
     members = members[::-1]
     out_weights, qkv_weights = out_weights[::-1], qkv_weights[::-1]
     qkv, attended = qkv[::-1], attended[::-1]
-    out_grads, grad_mixed = {}, []
-    for group, weight, (mixed, _) in zip(members, out_weights, attended):
-        grad_mixed.append(sum_products([(grad_branch, None, weight, None, 1)], 0, LEN, BF16))
-        out_grad = outer(mixed, grad_branch, min(512, width))
-        for spot, s in enumerate(group):
-            out_grads[s] = out_grad[spot * head_cols : (spot + 1) * head_cols]
+    grad_mixed, found = branch_back(grad_branch, out_weights, [mixed for mixed, _ in attended])
+    out_grads = {
+        s: out_grad[spot * head_cols : (spot + 1) * head_cols]
+        for group, out_grad in zip(members, found)
+        for spot, s in enumerate(group)
+    }
     out_pieces = send_to_owner(out_grads) + [out_grads[0]]
 
     def up_swap(last):
@@ -803,7 +894,7 @@
     norm_steps = across + along[1:]
     sums = {}
     moves = [up_swap, up_sum, gate_swap, gate_sum]
-    last = list(out_grads.values()) + grad_mixed
+    last = list(grad_mixed)
     grad_qkv, qkv_grads = [], {}
     for index, group in enumerate(members):
         mixed, logs = attended[index]
@@ -827,7 +918,7 @@
             )
             last = [grads]
         grad_qkv.append(grads)
-        qkv_grad = outer(full_one, grads, count)
+        qkv_grad = outer(full_one, grads)
         last = [qkv_grad]
         for spot, s in enumerate(group):
             if len(group) == 1:
@@ -849,13 +940,17 @@
         last = move(last)
 
     qkv_half, marks = swap_half(send_to_owner(qkv_grads) + [qkv_grads[0]])
-    feed_terms[0] = (after(feed_terms[0][0], *marks), *feed_terms[0][1:])
+    grad_down = sums["down"]
+    grad_up = whole_sum(sums["up"], *marks)
+    feed_terms[0] = (after(feed_terms[0][0], grad_up), *feed_terms[0][1:])
     feed_sent = [sum_products(feed_terms, shift * held, held, BF16) for shift in range(1, span)]
     feed_terms[0] = (after(feed_terms[0][0], *feed_sent), *feed_terms[0][1:])
     feed_parts = [sum_products(feed_terms, 0, held)]
     feed_parts += [to_seat(part, shift + 1) for shift, part in enumerate(feed_sent)]
     qkv_half = add_half(qkv_half, sums["gate"], feed_parts[0])
     qkv_sum = sum_half(qkv_half, 3)
+    gate_halves = swap_sum(sums["gate"], qkv_half)
+    out_halves = swap_sum(sums["out"], qkv_half)
     one_terms = [
         (grad_qkv[index], part, weight, part, 1)
         for index, weight in enumerate(qkv_weights)
@@ -865,12 +960,14 @@
     one_parts = scatter(
         lambda start, rows: sum_products(one_terms, start, rows, BF16 if start else F32)
     )
+    output = (hidden_one + sum(feed_parts)).astype(BF16)
+    qkv_halves = swap_sum(qkv_sum, one_parts[0], output)
+    one_parts[0] = after(one_parts[0], qkv_halves[0])
     (input_grad,), _, norm_one = norm_back(tokens, grad_hidden, gain_first, one_parts, True, 1)
-    output = (hidden_one + sum(feed_parts)).astype(BF16)
-    grad_down = sums["down"]
-    grad_up = whole_sum(sums["up"], input_grad)
-    grad_gate = whole_sum(swap_sum(sums["gate"], one_parts[0]), input_grad)
-    out_grad = whole_sum(swap_sum(sums["out"], one_parts[0]), input_grad)
+    grad_gate = whole_sum(gate_halves, qkv_halves[0])
+    out_grad = whole_sum(out_halves, qkv_halves[0])
+    qkv_grad = whole_sum(qkv_halves, input_grad)
+
     for step in across + along[1:]:
         norm_one = step(norm_one)
     for step in norm_steps:

time: 623 us -> 575 us (0.923)
  local copies, waits for them, and re-layouts: 61.2 us -> 18.1 us
  Pallas kernels: 390 us -> 378 us
  waiting for transfers between devices: 60 us -> 67.2 us
    unnamed x118 -> x96, local copies, waits for them, and re-layouts: 46 us -> 13.1 us
    pallas_call x8 -> x7, Pallas kernels: 96.8 us -> 110 us  [the longest x2 73.4 us: feed(): pl.pallas_call(functools.partial(feed_kernel, counts=(len(rows), len(targ...]
    pallas_call x10 -> x8, Pallas kernels: 82.2 us -> 71.2 us  [sum_products(): pl.pallas_call(functools.partial(sum_kernel, dims=tuple(dims)), grid=(row...]
    pallas_call x8 -> x4, Pallas kernels: 21.3 us -> 13 us  [norm(): pl.pallas_call(lambda *refs, held=len(held): norm_kernel(*refs[:3 + len(t...]
    psum x4, waiting for transfers between devices: 43.7 us -> 36.1 us  [sum_half(): return lax.psum(value, 'dp', axis_index_groups=groups)]
    ppermute x8, waiting for transfers between devices: 1.22 us -> 7.48 us  [from_window(): return lax.ppermute(value, 'tensor', pairs)]
    ppermute x9, waiting for transfers between devices: 7.73 us -> 14 us  [exchanges(): lax.ppermute(value, axis, pairs)]
    pallas_call x5 -> x3, Pallas kernels: 23.2 us -> 17.6 us  [norm_back(): pl.pallas_call(lambda *refs, held=len(held): norm_back_kernel(*refs[:3 +...]
  transfers between devices with their start and end apart: 49 -> 43, of which waited for: 14 -> 12; matrix products, arithmetic and copies ran while one was open for 13% -> 10% of each run, Pallas kernels for 58% -> 60%
where the time goes in v2:
time: 575 us; the launch traced here: 568 us
  Pallas kernels  378 us (66%)
  waiting for transfers between devices  67.2 us (12%)
  other arithmetic  54 us (9%)
  starting transfers between devices  36.4 us (6%)
  local copies, waits for them, and re-layouts  18.1 us (3%)
  between operations  14.7 us (3%)
    pallas_call x4, Pallas kernels, attend_back(): pl.pallas_call(functools.partial(attend_back_kernel, chunk=chunk), grid_s...  109 us
    pallas_call x2, Pallas kernels, feed(): pl.pallas_call(functools.partial(feed_kernel, counts=(len(rows), len(targ...  73.4 us
    pallas_call x8, Pallas kernels, sum_products(): pl.pallas_call(functools.partial(sum_kernel, dims=tuple(dims)), grid=(row...  71.2 us
    pallas_call x2, Pallas kernels, attend(): pl.pallas_call(functools.partial(attend_kernel, chunk=chunk), grid_spec=p...  57 us
    psum x4, waiting for transfers between devices, sum_half(): return lax.psum(value, 'dp', axis_index_groups=groups)  36.1 us
    pallas_call x3, Pallas kernels, norm_back(): pl.pallas_call(lambda *refs, held=len(held): norm_back_kernel(*refs[:3 +...  17.6 us
    convert_element_type x5, other arithmetic, total(): sum((half(piece, which).astype(F32) for piece in pieces)).astype(BF16)  16.2 us
    pallas_call x2, Pallas kernels, project(): pl.pallas_call(functools.partial(project_kernel, count=len(pieces)), grid...  14.8 us
  transfers between devices with their start and end apart: 43, of which 12 were waited for; matrix products, arithmetic and copies ran while one was open for 10% of the time, Pallas kernels for 60%

profile of v2, /device:TPU:0, one launch (start us, length us, event | category | flops | bytes accessed | tf_op | source)
XLA Modules:
  0.0 568.3 jit_solution(8540511931785230665)
XLA Ops:
  25.0 6.9 %project_rope.2 = (bf16[2048,256]{1,0:T(8,128)(2,1)S(1)}, bf16[2048,256]{1,0:T(8,128)(2,1)S(1)}, bf16[2048,256]{1,0:T(8,128)(2,1)S(1)}) custom-call(bf16[512,1024]{1,0:T(8,128)(2,1)S(1)} %copy-done.6, bf16[512,1024]{1,0:T(8,128)(2,1)S(1)} %copy-done.7, bf16[512,1024]{1,0:T(8,128)(2,1)} %collective-permute-done.refs_2_, ...), custom_call_target="tpu_custom_call" | custom-call | flops 322122560 | bytes 891289 | tf_op jit(solution)/shard_map/project_rope/pallas_call | solution.py:105
  37.4 28.5 %attention_forward.2 = (bf16[2048,256]{1,0:T(8,128)(2,1)}, f32[2,8,2048]{2,1,0:T(8,128)}) custom-call(s32[2]{0:T(128)} %pad_add_fusion.place_ref, bf16[2048,256]{1,0:T(8,128)(2,1)} %copy-done.14, bf16[2048,256]{1,0:T(8,128)(2,1)} %copy-done.15, bf16[2048,256]{1,0:T(8,128)(2,1)} %copy-done.16), custom_call_target="tpu_custom_call" | custom-call | flops 1717986944 | bytes 419430 | tf_op jit(solution)/shard_map/attention_forward/pallas_call | solution.py:184
  73.1 7.9 %project_rope.3 = (bf16[2048,256]{1,0:T(8,128)(2,1)S(1)}, bf16[2048,256]{1,0:T(8,128)(2,1)S(1)}, bf16[2048,256]{1,0:T(8,128)(2,1)S(1)}) custom-call(bf16[512,1024]{1,0:T(8,128)(2,1)S(1)} %copy-done.6, bf16[512,1024]{1,0:T(8,128)(2,1)S(1)} %copy-done.8, bf16[512,1024]{1,0:T(8,128)(2,1)} %collective-permute-done.refs_2_, ...), custom_call_target="tpu_custom_call" | custom-call | flops 322122560 | bytes 891289 | tf_op jit(solution)/shard_map/project_rope/pallas_call | solution.py:105
  84.0 28.5 %attention_forward.3 = (bf16[2048,256]{1,0:T(8,128)(2,1)}, f32[2,8,2048]{2,1,0:T(8,128)}) custom-call(s32[2]{0:T(128)} %pad_add_fusion.place_ref, bf16[2048,256]{1,0:T(8,128)(2,1)} %copy-done.17, bf16[2048,256]{1,0:T(8,128)(2,1)} %copy-done.18, bf16[2048,256]{1,0:T(8,128)(2,1)} %copy-done.19), custom_call_target="tpu_custom_call" | custom-call | flops 1717986944 | bytes 419430 | tf_op jit(solution)/shard_map/attention_forward/pallas_call | solution.py:184
  136.4 36.7 %feed_forward.2 = (bf16[2048,1024]{1,0:T(8,128)(2,1)}, bf16[2048,1024]{1,0:T(8,128)(2,1)}, bf16[2048,1024]{1,0:T(8,128)(2,1)}, bf16[1024,1024]{1,0:T(8,128)(2,1)...) custom-call(bf16[512,1024]{1,0:T(8,128)(2,1)} %get-tuple-element.129.refs_0_, ...), custom_call_target="tpu_custom_call" | custom-call | flops 2576980480 | bytes 3355443 | tf_op jit(solution)/shard_map/feed_forward/pallas_call | solution.py:371
  173.3 36.7 %feed_forward.3 = (bf16[2048,1024]{1,0:T(8,128)(2,1)}, bf16[2048,1024]{1,0:T(8,128)(2,1)}, bf16[2048,1024]{1,0:T(8,128)(2,1)}, bf16[1024,1024]{1,0:T(8,128)(2,1)...) custom-call(bf16[512,1024]{1,0:T(8,128)(2,1)} %get-tuple-element.129.refs_0_, ...), custom_call_target="tpu_custom_call" | custom-call | flops 2576980480 | bytes 3355443 | tf_op jit(solution)/shard_map/feed_forward/pallas_call | solution.py:371
  210.0 15.2 %sum_products.10 = bf16[1024,1024]{1,0:T(8,128)(2,1)} custom-call(bf16[2048,1024]{1,0:T(8,128)(2,1)} %get-tuple-element.135.refs_0_, bf16[8,384,1024]{2,1,0:T(8,128)(2,1)} %bitcast.13, bf16[2048,1024]{1,0:T(8,128)(2,1)} %get-tuple-element.128.refs_2_, bf16[8,384,1024]{2,1,0:T(8,128)(2,1)} %bitcast.14, bf16[2048,1024]{1,0:T(8,128)(2,1)} %get-tuple-element.130.refs_4_, ...), custom_call_target="tpu_custom_call" | custom-call | flops 858993472 | bytes 2097152 | tf_op jit(solution)/shard_map/sum_products/pallas_call | solution.py:427
  233.4 15.1 %sum_products.11.refs_3_ = f32[1024,1024]{1,0:T(8,128)} custom-call(bf16[2048,1024]{1,0:T(8,128)(2,1)} %get-tuple-element.135.refs_0_, bf16[8,384,1024]{2,1,0:T(8,128)(2,1)} %bitcast.15, bf16[2048,1024]{1,0:T(8,128)(2,1)} %get-tuple-element.128.refs_2_, bf16[8,384,1024]{2,1,0:T(8,128)(2,1)} %bitcast.16, bf16[2048,1024]{1,0:T(8,128)(2,1)} %get-tuple-element.130.refs_4_, ...), custom_call_target="tpu_custom_call" | custom-call | flops 858993472 | bytes 2097152 | tf_op jit(solution)/shard_map/sum_products/pallas_call | solution.py:427
  263.7 8.3 %branch_backward.1 = (bf16[2048,256]{1,0:T(8,128)(2,1)S(1)}, bf16[2048,256]{1,0:T(8,128)(2,1)S(1)}, bf16[256,1024]{1,0:T(8,128)(2,1)S(1)}, bf16[256,1024]{1,0:T(8,128)(2,1)S(1)}) custom-call(bf16[512,1024]{1,0:T(8,128)(2,1)S(1)} %copy-done.23, bf16[512,1024]{1,0:T(8,128)(2,1)} %get-tuple-element.138.refs_1_, ...), custom_call_target="tpu_custom_call" | custom-call | flops 429496736 | bytes 1258291 | tf_op jit(solution)/shard_map/branch_backward/pallas_call | solution.py:491
  280.9 27.1 %attention_backward.4.rest_0_ = bf16[3,2048,256]{2,1,0:T(8,128)(2,1)} custom-call(s32[2]{0:T(128)} %pad_add_fusion.place_ref, bf16[2048,256]{1,0:T(8,128)(2,1)} %copy-done.17, bf16[2048,256]{1,0:T(8,128)(2,1)} %copy-done.18, bf16[2048,256]{1,0:T(8,128)(2,1)} %copy-done.19, bf16[2048,256]{1,0:T(8,128)(2,1)} %get-tuple-element.118.refs_2_.refs_6_.out_ref, ...), custom_call_target="tpu_custom_call" | custom-call | flops 1503238528 | bytes 419430 | tf_op jit(solution)/shard_map/attention_backward/pallas_call | solution.py:283
  308.0 7.7 %all-reduce.8.cloned.1.call-done = bf16[512,1024]{1,0:T(8,128)(2,1)} async-done(((bf16[512,1024]{1,0:T(8,128)(2,1)}), bf16[512,1024]{1,0:T(8,128)(2,1)}) %all-reduce.8.cloned.1.call-update) | async-done | bytes 1048592 | tf_op jit(solution)/shard_map/psum | solution.py:813
  323.7 27.6 %attention_backward.5.refs_4_.refs_0_.refs_2_ = bf16[3,2048,256]{2,1,0:T(8,128)(2,1)} custom-call(s32[2]{0:T(128)} %pad_add_fusion.place_ref, bf16[2048,256]{1,0:T(8,128)(2,1)} %copy-done.17, bf16[2048,256]{1,0:T(8,128)(2,1)} %copy-done.18, bf16[2048,256]{1,0:T(8,128)(2,1)} %copy-done.19, ...), custom_call_target="tpu_custom_call", output_to_operand_aliasing={{}: (11, {})} | custom-call | flops 1503238528 | bytes 419430 | tf_op jit(solution)/shard_map/attention_backward/pallas_call | solution.py:283
  353.2 6.9 %outer_product.2 = bf16[1024,768]{1,0:T(8,128)(2,1)S(1)} custom-call(bf16[512,1024]{1,0:T(8,128)(2,1)S(1)} %copy-done.6, bf16[512,1024]{1,0:T(8,128)(2,1)S(1)} %copy-done.9, bf16[512,1024]{1,0:T(8,128)(2,1)} %collective-permute-done.refs_2_, bf16[512,1024]{1,0:T(8,128)(2,1)} %collective-permute-done.1.refs_3_, bf16[3,2048,256]{2,1,0:T(8,128)(2,1)S(1)} %copy-done.1), custom_call_target="tpu_custom_call" | custom-call | flops 322122560 | bytes 891289 | tf_op jit(solution)/shard_map/outer_product/pallas_call | solution.py:454
  375.3 27.1 %attention_backward.6.rest_0_ = bf16[3,2048,256]{2,1,0:T(8,128)(2,1)} custom-call(s32[2]{0:T(128)} %pad_add_fusion.place_ref, bf16[2048,256]{1,0:T(8,128)(2,1)} %copy-done.14, bf16[2048,256]{1,0:T(8,128)(2,1)} %copy-done.15, bf16[2048,256]{1,0:T(8,128)(2,1)} %copy-done.16, bf16[2048,256]{1,0:T(8,128)(2,1)} %get-tuple-element.111.refs_0_.refs_7_.out_ref, ...), custom_call_target="tpu_custom_call" | custom-call | flops 1503238528 | bytes 419430 | tf_op jit(solution)/shard_map/attention_backward/pallas_call | solution.py:283
  409.9 27.1 %attention_backward.7.refs_4_.refs_6_.refs_8_.refs_10_ = bf16[3,2048,256]{2,1,0:T(8,128)(2,1)} custom-call(s32[2]{0:T(128)} %pad_add_fusion.place_ref, bf16[2048,256]{1,0:T(8,128)(2,1)} %copy-done.14, bf16[2048,256]{1,0:T(8,128)(2,1)} %copy-done.15, bf16[2048,256]{1,0:T(8,128)(2,1)} %copy-done.16, ...), custom_call_target="tpu_custom_call", output_to_operand_aliasing={{}: (11, {})} | custom-call | flops 1503238528 | bytes 419430 | tf_op jit(solution)/shard_map/attention_backward/pallas_call | solution.py:283
  438.9 6.8 %outer_product.3 = bf16[1024,768]{1,0:T(8,128)(2,1)S(1)} custom-call(bf16[512,1024]{1,0:T(8,128)(2,1)S(1)} %copy-done.6, bf16[512,1024]{1,0:T(8,128)(2,1)S(1)} %copy-done.9, bf16[512,1024]{1,0:T(8,128)(2,1)} %collective-permute-done.refs_2_, bf16[512,1024]{1,0:T(8,128)(2,1)} %collective-permute-done.1.refs_3_, bf16[3,2048,256]{2,1,0:T(8,128)(2,1)S(1)} %copy-done), custom_call_target="tpu_custom_call" | custom-call | flops 322122560 | bytes 891289 | tf_op jit(solution)/shard_map/outer_product/pallas_call | solution.py:454
  452.0 8.6 %sum_products.12 = bf16[1024,1024]{1,0:T(8,128)(2,1)} custom-call(bf16[2048,1024]{1,0:T(8,128)(2,1)} %get-tuple-element.181.refs_0_, bf16[8,384,1024]{2,1,0:T(8,128)(2,1)} %bitcast.17, bf16[2048,1024]{1,0:T(8,128)(2,1)} %get-tuple-element.180.refs_2_, bf16[1024,1024]{1,0:T(8,128)(2,1)} %refs_3_.3), custom_call_target="tpu_custom_call" | custom-call | flops 429496736 | bytes 1258291 | tf_op jit(solution)/shard_map/sum_products/pallas_call | solution.py:427
  460.5 9.1 %sum_products.13 = f32[1024,1024]{1,0:T(8,128)} custom-call(bf16[2048,1024]{1,0:T(8,128)(2,1)} %get-tuple-element.181.refs_0_, bf16[8,384,1024]{2,1,0:T(8,128)(2,1)} %bitcast.18, bf16[2048,1024]{1,0:T(8,128)(2,1)} %get-tuple-element.180.refs_2_, bf16[1024,1024]{1,0:T(8,128)(2,1)} %refs_3_.3), custom_call_target="tpu_custom_call" | custom-call | flops 429496736 | bytes 1258291 | tf_op jit(solution)/shard_map/sum_products/pallas_call | solution.py:427
  470.7 7.3 %sum_products.15 = bf16[1024,1024]{1,0:T(8,128)(2,1)} custom-call(bf16[3,2048,256]{2,1,0:T(8,128)(2,1)} %attention_backward.5.refs_4_.refs_0_.refs_2_, bf16[1024,768]{1,0:T(8,128)(2,1)} %collective-permute-done.3.refs_4_.refs_1_.refs_3_.refs_5_, bf16[3,2048,256]{2,1,0:T(8,128)(2,1)} %attention_backward.5.refs_4_.refs_0_.refs_2_, ...), custom_call_target="tpu_custom_call" | custom-call | flops 322122560 | bytes 1048576 | tf_op jit(solution)/shard_map/sum_products/pallas_call | solution.py:427
  480.1 7.7 %sum_products.14.refs_3_ = f32[1024,1024]{1,0:T(8,128)} custom-call(bf16[3,2048,256]{2,1,0:T(8,128)(2,1)} %attention_backward.5.refs_4_.refs_0_.refs_2_, bf16[1024,768]{1,0:T(8,128)(2,1)} %collective-permute-done.3.refs_4_.refs_1_.refs_3_.refs_5_, bf16[3,2048,256]{2,1,0:T(8,128)(2,1)} %attention_backward.5.refs_4_.refs_0_.refs_2_, ...), custom_call_target="tpu_custom_call" | custom-call | flops 322122560 | bytes 1048576 | tf_op jit(solution)/shard_map/sum_products/pallas_call | solution.py:427
  487.9 5.5 add_convert_fusion
  493.3 28.4 %all-reduce.10.cloned.1.call-done = bf16[512,768]{1,0:T(8,128)(2,1)} async-done(((bf16[512,768]{1,0:T(8,128)(2,1)}), bf16[512,768]{1,0:T(8,128)(2,1)}) %all-reduce.10.cloned.1.call-update) | async-done | bytes 786448 | tf_op jit(solution)/shard_map/psum | solution.py:813
  521.7 7.9 %layer_norm_backward.5 = (bf16[1024,1024]{1,0:T(8,128)(2,1)}, f32[2,1024]{1,0:T(2,128)}) custom-call(bf16[1024,1024]{1,0:T(8,128)(2,1)} %refs_0_.7, f32[1024,1024]{1,0:T(8,128)} %get-tuple-element.182.refs_1_, f32[1,1024]{1,0:T(1,128)} %bitcast.25, f32[1024,1024]{1,0:T(8,128)} %sum_products.14.refs_3_, bf16[1024,1024]{1,0:T(8,128)(2,1)} %collective-permute-done.29.refs_4_), custom_call_target="tpu_custom_call" | custom-call | flops 3145728 | bytes 1677721 | tf_op jit(solution)/shard_map/layer_norm_backward/pallas_call | solution.py:606
  549.3 9.6 %collective-permute-done.37 = f32[4,1024]{1,0:T(4,128)S(1)} collective-permute-done((f32[4,1024]{1,0:T(4,128)S(1)}, f32[4,1024]{1,0:T(4,128)S(1)}, u32[]{:S(2)}, u32[]{:S(2)}) %collective-permute-start.37) | collective-permute-done | bytes 16416 | tf_op jit(solution)/shard_map/ppermute | solution.py:646
  (235 shorter events, 155.5 us)
Async XLA Ops:
  7.2 128.3 %all-gather.3.cloned.1.call-start = ((), (), s32[]{:S(2)}) async-start(), calls=%async_computation.3 | async-start | bytes 7077888 | tf_op jit(solution)/shard_map/all_gather | solution.py:718
  10.2 24.5 %collective-permute-start.2 = (bf16[384,1024]{1,0:T(8,128)(2,1)}, bf16[384,1024]{1,0:T(8,128)(2,1)}, u32[]{:S(2)}, u32[]{:S(2)}) collective-permute-start(bf16[384,1024]{1,0:T(8,128)(2,1)} %pad_maximum_fusion.2), channel_id=1, source_target_pairs={{2,0},{3,1},{0,2},{1,3},{6,4},{7,5},{4,6},{5,7},{10,8},{11,9},{8,1... | collective-permute-start | bytes 2359304 | tf_op jit(solution)/shard_map/ppermute | solution.py:690
  34.8 281.0 %all-reduce.8.cloned.1.call-start = ((), (), s32[]{:S(2)}) async-start(), calls=%async_computation.1 | async-start | bytes 2097152 | tf_op jit(solution)/shard_map/psum | solution.py:813
  35.4 48.6 %collective-permute-start.4 = (bf16[1024,1024]{1,0:T(8,128)(2,1)}, bf16[1024,1024]{1,0:T(8,128)(2,1)}, u32[]{:S(2)}, u32[]{:S(2)}) collective-permute-start(bf16[1024,1024]{1,0:T(8,128)(2,1)} %refs_1_.7), channel_id=1, source_target_pairs={{1,0},{0,1},{3,2},{2,3},{5,4},{4,5},{7,6},{6,7},{9,8},{8,9},{11,10... | collective-permute-start | bytes 6291464 | tf_op jit(solution)/shard_map/ppermute | solution.py:683
  35.6 37.5 %collective-permute-start.3 = (bf16[1024,768]{1,0:T(8,128)(2,1)}, bf16[1024,768]{1,0:T(8,128)(2,1)}, u32[]{:S(2)}, u32[]{:S(2)}) collective-permute-start(bf16[1024,768]{1,0:T(8,128)(2,1)} %copy-done.4), channel_id=1, source_target_pairs={{2,0},{3,1},{0,2},{1,3},{6,4},{7,5},{4,6},{5,7},{10,8},{11,9},{8,1... | collective-permute-start | bytes 4718600 | tf_op jit(solution)/shard_map/ppermute | solution.py:690
  65.9 46.5 %collective-permute-start.5 = (bf16[256,1024]{1,0:T(8,128)(2,1)S(1)}, bf16[256,1024]{1,0:T(8,128)(2,1)S(1)}, u32[]{:S(2)}, u32[]{:S(2)}) collective-permute-start(bf16[256,1024]{1,0:T(8,128)(2,1)S(1)} %copy-done.10), channel_id=1, source_target_pairs={{2,0},{3,1},{0,2},{1,3},{6,4},{7,5},{4,6},{5,7},{10,8},{11,9},{8,1... | collective-permute-start | bytes 1572872 | tf_op jit(solution)/shard_map/ppermute | solution.py:690
  173.1 54.2 %collective-permute-start.10 = (bf16[1024,1024]{1,0:T(8,128)(2,1)}, bf16[1024,1024]{1,0:T(8,128)(2,1)}, u32[]{:S(2)}, u32[]{:S(2)}) collective-permute-start(bf16[1024,1024]{1,0:T(8,128)(2,1)} %get-tuple-element.127), channel_id=1, source_target_pairs={{2,0},{3,1},{0,2},{1,3},{6,4},{7,5},{4,6},{5,7},{10,8},{11,9},{8,1... | collective-permute-start | bytes 6291464 | tf_op jit(solution)/shard_map/ppermute | solution.py:690
  225.2 23.3 %collective-permute-start.11 = (bf16[1024,1024]{1,0:T(8,128)(2,1)}, bf16[1024,1024]{1,0:T(8,128)(2,1)S(1)}, u32[]{:S(2)}, u32[]{:S(2)}) collective-permute-start(bf16[1024,1024]{1,0:T(8,128)(2,1)} %sum_products.10), channel_id=1, source_target_pairs={{1,0},{0,1},{3,2},{2,3},{5,4},{4,5},{7,6},{6,7},{9,8},{8,9},{11,10... | collective-permute-start | bytes 6291464 | tf_op jit(solution)/shard_map/ppermute | solution.py:683
  225.6 48.8 %collective-permute-start.9 = (bf16[1024,1024]{1,0:T(8,128)(2,1)}, bf16[1024,1024]{1,0:T(8,128)(2,1)}, u32[]{:S(2)}, u32[]{:S(2)}) collective-permute-start(bf16[1024,1024]{1,0:T(8,128)(2,1)} %get-tuple-element.125), channel_id=1, source_target_pairs={{2,0},{3,1},{0,2},{1,3},{6,4},{7,5},{4,6},{5,7},{10,8},{11,9},{8,1... | collective-permute-start | bytes 6291464 | tf_op jit(solution)/shard_map/ppermute | solution.py:690
  231.8 28.7 %collective-permute-start.12 = (bf16[512,1024]{1,0:T(8,128)(2,1)}, bf16[512,1024]{1,0:T(8,128)(2,1)}, u32[]{:S(2)}, u32[]{:S(2)}) collective-permute-start(bf16[512,1024]{1,0:T(8,128)(2,1)} %get-tuple-element.203), channel_id=1, source_target_pairs={{0,4},{4,0},{8,12},{12,8},{16,20},{20,16},{24,28},{28,24},{1,5},{5... | collective-permute-start | bytes 3145736 | tf_op jit(solution)/shard_map/ppermute | solution.py:801
  260.0 100.2 %collective-permute-start.17 = (bf16[1024,1024]{1,0:T(8,128)(2,1)}, bf16[1024,1024]{1,0:T(8,128)(2,1)}, u32[]{:S(2)}, u32[]{:S(2)}) collective-permute-start(bf16[1024,1024]{1,0:T(8,128)(2,1)} %get-tuple-element.154), channel_id=1, source_target_pairs={{2,0},{3,1},{0,2},{1,3},{6,4},{7,5},{4,6},{5,7},{10,8},{11,9},{8,1... | collective-permute-start | bytes 6291464 | tf_op jit(solution)/shard_map/ppermute | solution.py:690
  263.6 138.8 %all-reduce.6.cloned.1.call-start = ((), (), s32[]{:S(2)}) async-start(), calls=%async_computation | async-start | bytes 2097152 | tf_op jit(solution)/shard_map/psum | solution.py:813
  277.9 43.1 %collective-permute-start.16 = (bf16[512,1024]{1,0:T(8,128)(2,1)}, bf16[512,1024]{1,0:T(8,128)(2,1)}, u32[]{:S(2)}, u32[]{:S(2)}) collective-permute-start(bf16[512,1024]{1,0:T(8,128)(2,1)} %get-tuple-element.202), channel_id=1, source_target_pairs={{0,4},{4,0},{8,12},{12,8},{16,20},{20,16},{24,28},{28,24},{1,5},{5... | collective-permute-start | bytes 3145736 | tf_op jit(solution)/shard_map/ppermute | solution.py:801
  315.8 55.7 %collective-permute-start.20 = (bf16[512,1024]{1,0:T(8,128)(2,1)}, bf16[512,1024]{1,0:T(8,128)(2,1)}, u32[]{:S(2)}, u32[]{:S(2)}) collective-permute-start(bf16[512,1024]{1,0:T(8,128)(2,1)} %all-reduce.8.cloned.1.call-done), channel_id=1, source_target_pairs={{0,4},{4,0},{8,12},{12,8},{16,20},{20,16},{24,28},{28,24},{1,5},{5... | collective-permute-start | bytes 3145736 | tf_op jit(solution)/shard_map/ppermute | solution.py:817
  318.7 47.9 %collective-permute-start.19 = (bf16[256,1024]{1,0:T(8,128)(2,1)S(1)}, bf16[256,1024]{1,0:T(8,128)(2,1)}, u32[]{:S(2)}, u32[]{:S(2)}) collective-permute-start(bf16[256,1024]{1,0:T(8,128)(2,1)S(1)} %copy-done.27), channel_id=1, source_target_pairs={{2,0},{3,1},{0,2},{1,3},{6,4},{7,5},{4,6},{5,7},{10,8},{11,9},{8,1... | collective-permute-start | bytes 1572872 | tf_op jit(solution)/shard_map/ppermute | solution.py:690
  323.6 146.1 %all-reduce.12.cloned.1.call-start = ((), (), s32[]{:S(2)}) async-start(), calls=%async_computation.4 | async-start | bytes 2621440 | tf_op jit(solution)/shard_map/psum | solution.py:813
  364.6 38.8 %collective-permute-start.23 = (bf16[512,1024]{1,0:T(8,128)(2,1)}, bf16[512,1024]{1,0:T(8,128)(2,1)}, u32[]{:S(2)}, u32[]{:S(2)}) collective-permute-start(bf16[512,1024]{1,0:T(8,128)(2,1)} %get-tuple-element.199), channel_id=1, source_target_pairs={{0,4},{4,0},{8,12},{12,8},{16,20},{20,16},{24,28},{28,24},{1,5},{5... | collective-permute-start | bytes 3145736 | tf_op jit(solution)/shard_map/ppermute | solution.py:801
  365.2 80.6 %collective-permute-start.22 = (bf16[1024,768]{1,0:T(8,128)(2,1)}, bf16[1024,768]{1,0:T(8,128)(2,1)}, u32[]{:S(2)}, u32[]{:S(2)}) collective-permute-start(bf16[1024,768]{1,0:T(8,128)(2,1)} %copy-done.22), channel_id=1, source_target_pairs={{2,0},{3,1},{0,2},{1,3},{6,4},{7,5},{4,6},{5,7},{10,8},{11,9},{8,1... | collective-permute-start | bytes 4718600 | tf_op jit(solution)/shard_map/ppermute | solution.py:690
  370.0 33.4 %collective-permute-start.24 = (bf16[128,1024]{1,0:T(8,128)(2,1)}, bf16[128,1024]{1,0:T(8,128)(2,1)}, u32[]{:S(2)}, u32[]{:S(2)}) collective-permute-start(bf16[128,1024]{1,0:T(8,128)(2,1)} %get-tuple-element.218), channel_id=1, source_target_pairs={{0,4},{4,0},{8,12},{12,8},{16,20},{20,16},{24,28},{28,24},{1,5},{5... | collective-permute-start | bytes 786440 | tf_op jit(solution)/shard_map/ppermute | solution.py:801
  402.4 45.8 %collective-permute-start.26 = (bf16[512,1024]{1,0:T(8,128)(2,1)}, bf16[512,1024]{1,0:T(8,128)(2,1)}, u32[]{:S(2)}, u32[]{:S(2)}) collective-permute-start(bf16[512,1024]{1,0:T(8,128)(2,1)} %all-reduce.6.cloned.1.call-done), channel_id=1, source_target_pairs={{0,4},{4,0},{8,12},{12,8},{16,20},{20,16},{24,28},{28,24},{1,5},{5... | collective-permute-start | bytes 3145736 | tf_op jit(solution)/shard_map/ppermute | solution.py:817
  409.8 111.9 %all-reduce.10.cloned.1.call-start = ((), (), s32[]{:S(2)}) async-start(), calls=%async_computation.2 | async-start | bytes 1572864 | tf_op jit(solution)/shard_map/psum | solution.py:813
  460.5 27.3 %collective-permute-start.27 = (bf16[1024,1024]{1,0:T(8,128)(2,1)}, bf16[1024,1024]{1,0:T(8,128)(2,1)}, u32[]{:S(2)}, u32[]{:S(2)}) collective-permute-start(bf16[1024,1024]{1,0:T(8,128)(2,1)} %sum_products.12), channel_id=1, source_target_pairs={{1,0},{0,1},{3,2},{2,3},{5,4},{4,5},{7,6},{6,7},{9,8},{8,9},{11,10... | collective-permute-start | bytes 6291464 | tf_op jit(solution)/shard_map/ppermute | solution.py:683
  478.0 43.7 %collective-permute-start.29 = (bf16[1024,1024]{1,0:T(8,128)(2,1)}, bf16[1024,1024]{1,0:T(8,128)(2,1)}, u32[]{:S(2)}, u32[]{:S(2)}) collective-permute-start(bf16[1024,1024]{1,0:T(8,128)(2,1)} %sum_products.15), channel_id=1, source_target_pairs={{1,0},{0,1},{3,2},{2,3},{5,4},{4,5},{7,6},{6,7},{9,8},{8,9},{11,10... | collective-permute-start | bytes 6291464 | tf_op jit(solution)/shard_map/ppermute | solution.py:683
  478.5 52.7 %collective-permute-start.32 = (bf16[512,1024]{1,0:T(8,128)(2,1)S(1)}, bf16[512,1024]{1,0:T(8,128)(2,1)}, u32[]{:S(2)}, u32[]{:S(2)}) collective-permute-start(bf16[512,1024]{1,0:T(8,128)(2,1)S(1)} %copy-done.37), channel_id=1, source_target_pairs={{0,4},{4,0},{8,12},{12,8},{16,20},{20,16},{24,28},{28,24},{1,5},{5... | collective-permute-start | bytes 3145736 | tf_op jit(solution)/shard_map/ppermute | solution.py:817
  (66 other events, 571.0 us)
Sparse Core Ops, SparseCore 0:
  34.9 99.3 all-gather.2
  263.7 52.0 all-reduce.7
  323.7 51.5 all-reduce.5
  410.0 58.1 all-reduce.11
  480.2 41.4 all-reduce.9

commit v3 on v2

--- a/solution.py
+++ b/solution.py
@@ -387,49 +387,80 @@
     )(*rows, *target, *weights)
 
 
-def sum_kernel(*refs, dims):
-    total = 0.0
+def sum_kernel(*refs, places, dims, start, chunk):
+    terms = len(dims)
+    operands, out_ref = refs[: 2 * terms], refs[2 * terms]
+    buffers = refs[2 * terms + 1 : 4 * terms + 1]
+    total, result, sems, out_sems = refs[4 * terms + 1 :]
+    rows = total.shape[0]
+    copies = []
+    for index, (ref, place) in enumerate(zip(operands, places)):
+        copy = pltpu.make_async_copy(ref.at[place], buffers[index], sems.at[index])
+        copy.start()
+        copies.append(copy)
+    sent = []
     for index, dim in enumerate(dims):
-        total = total + contract(refs[2 * index][...], unpacked(refs[2 * index + 1]), 1, dim)
-    refs[-1][...] = total.astype(refs[-1].dtype)
-
-
-def sum_products(terms, start, rows, dtype=F32, block=512):
-    block = min(block, rows)
-    first = start // block
-    operands, specs, dims, flops, moved = [], [], [], 0, 0
+        copies[2 * index].wait()
+        copies[2 * index + 1].wait()
+        right = unpacked(buffers[2 * index + 1])
+        for first in range(0, rows, chunk):
+            span = slice(first, first + chunk)
+            product = contract(buffers[2 * index][span, :], right, 1, dim)
+            if index:
+                product = total[span, :] + product
+            if index + 1 < terms:
+                total[span, :] = product
+                continue
+            result[span, :] = product.astype(result.dtype)
+            copy = pltpu.make_async_copy(
+                result.at[pl.ds(first, chunk), :],
+                out_ref.at[pl.ds(first, chunk), :],
+                out_sems.at[first // chunk],
+            )
+            copy.start()
+            sent.append(copy)
+    for copy in sent:
+        copy.wait()
+
+
+def sum_products(terms, start, rows, dtype=F32, chunk=256):
+    chunk = min(chunk, rows)
+    operands, places, shapes, dims, flops, moved = [], [], [], [], 0, 0
     for left, plane, right, part, dim in terms:
         depth = left.shape[-1]
-        if plane is None:
-            specs.append(pl.BlockSpec((block, depth), lambda i: (first + i, 0)))
-        else:
-            specs.append(
-                pl.BlockSpec((None, block, depth), lambda i, plane=plane: (plane, first + i, 0))
-            )
+        span = pl.ds(start, rows)
+        places.append((span, slice(None)) if plane is None else (plane, span, slice(None)))
+        shapes.append((rows, depth))
         if packed(right):
             right, plane = right
-            replicas, deep = right.shape[0], right.shape[2] // right.shape[0]
-            shape = (right.shape[2], right.shape[2])
-            specs.append(
-                pl.BlockSpec(
-                    (replicas, deep, right.shape[2]), lambda i, plane=plane: (0, plane, 0)
-                )
-            )
+            width = right.shape[2]
+            deep = width // right.shape[0]
+            places.append((slice(None), pl.ds(plane * deep, deep), slice(None)))
+            shapes.append((right.shape[0], deep, width))
         else:
-            shape = right.shape if part is None else (right.shape[0], depth)
-            column = 0 if part is None else part
-            specs.append(pl.BlockSpec(shape, lambda i, column=column: (0, column)))
+            column = pl.ds(0, right.shape[1]) if part is None else pl.ds(part * depth, depth)
+            places.append((slice(None), column))
+            shapes.append((right.shape[0], column.size))
+            width = shapes[-1][1 - dim]
         operands += [left, right]
         dims.append(dim)
-        width = shape[1 - dim]
         flops += 2 * rows * depth * width
         moved += 2 * rows * depth + 2 * depth * width
+    anywhere = pl.BlockSpec(memory_space=pl.ANY)
     return pl.pallas_call(
-        functools.partial(sum_kernel, dims=tuple(dims)),
-        grid=(rows // block,),
-        in_specs=specs,
-        out_specs=pl.BlockSpec((block, width), lambda i: (i, 0)),
+        functools.partial(
+            sum_kernel, places=places, dims=tuple(dims), start=start, chunk=chunk
+        ),
+        in_specs=[anywhere] * len(operands),
+        out_specs=anywhere,
         out_shape=jax.ShapeDtypeStruct((rows, width), dtype),
+        scratch_shapes=[pltpu.VMEM(shape, BF16) for shape in shapes]
+        + [
+            pltpu.VMEM((rows, width), F32),
+            pltpu.VMEM((rows, width), dtype),
+            pltpu.SemaphoreType.DMA((len(operands),)),
+            pltpu.SemaphoreType.DMA((rows // chunk,)),
+        ],
         cost_estimate=cost(flops, moved + 4 * rows * width),
         compiler_params=pltpu.CompilerParams(vmem_limit_bytes=58 * MIB),
         name="sum_products",
@@ -628,14 +659,23 @@
 
 
 def rope_tables(offset):
-    position = (jnp.arange(LEN, dtype=jnp.int32) + offset) % LEN
-    inverse = 10000.0 ** (-2.0 * jnp.arange(HD // 2, dtype=F32) / HD)
-    angles = position.astype(F32)[:, None] * inverse[None, :]
-    cosines, sines = jnp.cos(angles), jnp.sin(angles)
-    return (
-        jnp.concatenate([cosines] * 4, axis=1),
-        jnp.concatenate([-sines, sines, -sines, sines], axis=1),
-    )
+    half = HD // 2
+    groups = LANES // half
+    count = LEN // groups
+    lane = jnp.arange(LANES, dtype=jnp.int32)
+    position = jnp.arange(count, dtype=jnp.int32)[:, None] + lane[None, :] // half * count
+    position = (position + offset) % LEN
+    inverse = 10000.0 ** (-2.0 * (lane % half).astype(F32) / HD)
+    angles = position.astype(F32) * inverse[None, :]
+    cosines, sines = lax.optimization_barrier((jnp.cos(angles), jnp.sin(angles)))
+
+    def rows(table, signs):
+        parts = [table[:, g * half : (g + 1) * half] for g in range(groups)]
+        return jnp.concatenate(
+            [jnp.concatenate([sign * part for sign in signs], axis=1) for part in parts], axis=0
+        )
+
+    return rows(cosines, (1, 1, 1, 1)), rows(sines, (-1, 1, -1, 1))
 
 
 def exchanges(axis, size):
@@ -875,25 +915,26 @@
     def up_sum(last):
         value = add_half(sums["up"], *last)
         sums["up"] = sum_half(value, 1)
+        sums["gate"], waits = swap_half(gate_pieces, value)
+        return [value] + waits
+
+    def gate_sum(last):
+        sums["gate"] = value = add_half(sums["gate"], *last)
+        sums["out"], waits = swap_half(out_pieces, *last)
         sums["down"] = swap_sum(down_sum, *last)
-        return [value, sums["down"][0]]
-
-    def gate_swap(last):
-        sums["gate"], waits = swap_half(gate_pieces, *last)
-        sums["out"], more = swap_half(out_pieces, *last)
+        return [value, sums["down"][0]] + waits
+
+    def down_whole(last):
         sums["down"] = whole_sum(sums["down"], *last)
-        return waits + more + [sums["down"]]
-
-    def gate_sum(last):
-        values = [add_half(sums["gate"], *last), add_half(sums["out"], *last)]
-        sums["gate"], sums["out"] = sum_half(tuple(values), 2)
+        value = add_half(sums["out"], *last)
+        sums["gate"], sums["out"] = sum_half((sums["gate"], value), 2)
         sums["up"] = swap_sum(sums["up"], *last)
-        return values + [sums["up"][0]]
+        return [sums["down"], value, sums["up"][0]]
 
     across, along = (exchanges(axis, size) for axis, size in (("tensor", tensor_size), ("dp", dp_size)))
     norm_steps = across + along[1:]
     sums = {}
-    moves = [up_swap, up_sum, gate_swap, gate_sum]
+    moves = [up_swap, up_sum, gate_sum, down_whole]
     last = list(grad_mixed)
     grad_qkv, qkv_grads = [], {}
     for index, group in enumerate(members):
@@ -940,41 +981,44 @@
         last = move(last)
 
     qkv_half, marks = swap_half(send_to_owner(qkv_grads) + [qkv_grads[0]])
-    grad_down = sums["down"]
     grad_up = whole_sum(sums["up"], *marks)
     feed_terms[0] = (after(feed_terms[0][0], grad_up), *feed_terms[0][1:])
-    feed_sent = [sum_products(feed_terms, shift * held, held, BF16) for shift in range(1, span)]
-    feed_terms[0] = (after(feed_terms[0][0], *feed_sent), *feed_terms[0][1:])
-    feed_parts = [sum_products(feed_terms, 0, held)]
-    feed_parts += [to_seat(part, shift + 1) for shift, part in enumerate(feed_sent)]
-    qkv_half = add_half(qkv_half, sums["gate"], feed_parts[0])
-    qkv_sum = sum_half(qkv_half, 3)
-    gate_halves = swap_sum(sums["gate"], qkv_half)
-    out_halves = swap_sum(sums["out"], qkv_half)
     one_terms = [
         (grad_qkv[index], part, weight, part, 1)
         for index, weight in enumerate(qkv_weights)
         for part in range(3)
     ]
-    one_terms[0] = (after(one_terms[0][0], qkv_half), *one_terms[0][1:])
-    one_parts = scatter(
-        lambda start, rows: sum_products(one_terms, start, rows, BF16 if start else F32)
-    )
+
+    def later(terms, *others):
+        return [(after(terms[0][0], *others), *terms[0][1:])] + terms[1:]
+
+    shifts = range(1, span)
+    feed_sent = [sum_products(feed_terms, shift * held, held, BF16) for shift in shifts]
+    qkv_half = add_half(qkv_half, *feed_sent)
+    gate_halves = swap_sum(sums["gate"], *feed_sent)
+    out_halves = swap_sum(sums["out"], *feed_sent)
+    qkv_sum = sum_half(after(qkv_half, gate_halves[0], out_halves[0]), 3)
+    one_terms = later(one_terms, qkv_half, gate_halves[0])
+    one_sent = [sum_products(one_terms, shift * held, held, BF16) for shift in shifts]
+    feed_parts = [sum_products(later(feed_terms, *one_sent), 0, held)]
+    one_parts = [sum_products(later(one_terms, feed_parts[0]), 0, held)]
+    feed_parts += [to_seat(part, shift) for shift, part in zip(shifts, feed_sent)]
+    one_parts += [to_seat(part, shift) for shift, part in zip(shifts, one_sent)]
     output = (hidden_one + sum(feed_parts)).astype(BF16)
-    qkv_halves = swap_sum(qkv_sum, one_parts[0], output)
-    one_parts[0] = after(one_parts[0], qkv_halves[0])
     (input_grad,), _, norm_one = norm_back(tokens, grad_hidden, gain_first, one_parts, True, 1)
+    for step in norm_steps:
+        norm_two = step(norm_two)
+    grad_down = sums["down"]
+    window = [input_grad, output]
+    qkv_halves = swap_sum(qkv_sum, *window)
+    norm_one = after(norm_one, qkv_halves[0])
+    for step in across + along[1:]:
+        norm_one = step(norm_one)
+    norms = along[0](jnp.concatenate([norm_one, norm_two], axis=0))
+    norm_one, norm_two = norms[:2], norms[2:]
     grad_gate = whole_sum(gate_halves, qkv_halves[0])
     out_grad = whole_sum(out_halves, qkv_halves[0])
-    qkv_grad = whole_sum(qkv_halves, input_grad)
-
-    for step in across + along[1:]:
-        norm_one = step(norm_one)
-    for step in norm_steps:
-        norm_two = step(norm_two)
-    norms = along[0](jnp.concatenate([norm_one, norm_two], axis=0))
-    qkv_grad = whole_sum(swap_sum(qkv_sum, input_grad))
-
+    qkv_grad = whole_sum(qkv_halves)
     return (
         output,
         input_grad,
@@ -983,10 +1027,10 @@
         grad_gate,
         grad_up,
         grad_down,
-        norms[0],
-        norms[1],
-        norms[2],
-        norms[3],
+        norm_one[0],
+        norm_one[1],
+        norm_two[0],
+        norm_two[1],
     )
 
 

time: 575 us -> 558 us (0.970)
  waiting for transfers between devices: 67.2 us -> 60.1 us
  Pallas kernels: 378 us -> 371 us
    psum x4, waiting for transfers between devices: 36.1 us -> 16.7 us  [sum_half(): return lax.psum(value, 'dp', axis_index_groups=groups)]
    ppermute x8, waiting for transfers between devices: 7.48 us -> 19 us  [from_window(): return lax.ppermute(value, 'tensor', pairs)]
    pallas_call x8, Pallas kernels: 71.2 us -> 63.3 us  [sum_products(): pl.pallas_call(functools.partial(sum_kernel, places=places, dims=tuple(di...]
    unnamed x96 -> x92, local copies, waits for them, and re-layouts: 13.1 us -> 15.2 us
  transfers between devices with their start and end apart: 43 -> 43, of which waited for: 12 -> 14; matrix products, arithmetic and copies ran while one was open for 10% -> 9% of each run, Pallas kernels for 60% -> 60%
where the time goes in v3:
time: 558 us; the launch traced here: 552 us
  Pallas kernels  371 us (66%)
  waiting for transfers between devices  60.1 us (11%)
  other arithmetic  50.5 us (9%)
  starting transfers between devices  36.3 us (7%)
  local copies, waits for them, and re-layouts  20.2 us (4%)
  between operations  14.8 us (3%)
    pallas_call x4, Pallas kernels, attend_back(): pl.pallas_call(functools.partial(attend_back_kernel, chunk=chunk), grid_s...  109 us
    pallas_call x2, Pallas kernels, feed(): pl.pallas_call(functools.partial(feed_kernel, counts=(len(rows), len(targ...  73.7 us
    pallas_call x8, Pallas kernels, sum_products(): pl.pallas_call(functools.partial(sum_kernel, places=places, dims=tuple(di...  63.3 us
    pallas_call x2, Pallas kernels, attend(): pl.pallas_call(functools.partial(attend_kernel, chunk=chunk), grid_spec=p...  57 us
    ppermute x8, waiting for transfers between devices, from_window(): return lax.ppermute(value, 'tensor', pairs)  19 us
    pallas_call x3, Pallas kernels, norm_back(): pl.pallas_call(lambda *refs, held=len(held): norm_back_kernel(*refs[:3 +...  17.8 us
    psum x4, waiting for transfers between devices, sum_half(): return lax.psum(value, 'dp', axis_index_groups=groups)  16.7 us
    convert_element_type x5, other arithmetic, total(): sum((half(piece, which).astype(F32) for piece in pieces)).astype(BF16)  16.2 us
  transfers between devices with their start and end apart: 43, of which 14 were waited for; matrix products, arithmetic and copies ran while one was open for 9% of the time, Pallas kernels for 60%

profile of v3, /device:TPU:0, one launch (start us, length us, event | category | flops | bytes accessed | tf_op | source)
XLA Modules:
  0.0 552.5 jit_solution(7130449284345004188)
XLA Ops:
  23.7 6.5 %project_rope.2 = (bf16[2048,256]{1,0:T(8,128)(2,1)S(1)}, bf16[2048,256]{1,0:T(8,128)(2,1)S(1)}, bf16[2048,256]{1,0:T(8,128)(2,1)S(1)}) custom-call(bf16[512,1024]{1,0:T(8,128)(2,1)S(1)} %copy-done.5, bf16[512,1024]{1,0:T(8,128)(2,1)S(1)} %copy-done.6, bf16[512,1024]{1,0:T(8,128)(2,1)} %collective-permute-done.refs_2_, ...), custom_call_target="tpu_custom_call" | custom-call | flops 322122560 | bytes 891289 | tf_op jit(solution)/shard_map/project_rope/pallas_call | solution.py:105
  35.8 28.5 %attention_forward.2 = (bf16[2048,256]{1,0:T(8,128)(2,1)}, f32[2,8,2048]{2,1,0:T(8,128)}) custom-call(s32[2]{0:T(128)} %pad_add_fusion.place_ref, bf16[2048,256]{1,0:T(8,128)(2,1)} %copy-done.13, bf16[2048,256]{1,0:T(8,128)(2,1)} %copy-done.14, bf16[2048,256]{1,0:T(8,128)(2,1)} %copy-done.15), custom_call_target="tpu_custom_call" | custom-call | flops 1717986944 | bytes 419430 | tf_op jit(solution)/shard_map/attention_forward/pallas_call | solution.py:184
  71.5 7.9 %project_rope.3 = (bf16[2048,256]{1,0:T(8,128)(2,1)S(1)}, bf16[2048,256]{1,0:T(8,128)(2,1)S(1)}, bf16[2048,256]{1,0:T(8,128)(2,1)S(1)}) custom-call(bf16[512,1024]{1,0:T(8,128)(2,1)S(1)} %copy-done.5, bf16[512,1024]{1,0:T(8,128)(2,1)S(1)} %copy-done.7, bf16[512,1024]{1,0:T(8,128)(2,1)} %collective-permute-done.refs_2_, ...), custom_call_target="tpu_custom_call" | custom-call | flops 322122560 | bytes 891289 | tf_op jit(solution)/shard_map/project_rope/pallas_call | solution.py:105
  82.3 28.5 %attention_forward.3 = (bf16[2048,256]{1,0:T(8,128)(2,1)}, f32[2,8,2048]{2,1,0:T(8,128)}) custom-call(s32[2]{0:T(128)} %pad_add_fusion.place_ref, bf16[2048,256]{1,0:T(8,128)(2,1)} %copy-done.16, bf16[2048,256]{1,0:T(8,128)(2,1)} %copy-done.17, bf16[2048,256]{1,0:T(8,128)(2,1)} %copy-done.18), custom_call_target="tpu_custom_call" | custom-call | flops 1717986944 | bytes 419430 | tf_op jit(solution)/shard_map/attention_forward/pallas_call | solution.py:184
  135.0 36.7 %feed_forward.2 = (bf16[2048,1024]{1,0:T(8,128)(2,1)}, bf16[2048,1024]{1,0:T(8,128)(2,1)}, bf16[2048,1024]{1,0:T(8,128)(2,1)}, bf16[1024,1024]{1,0:T(8,128)(2,1)...) custom-call(bf16[512,1024]{1,0:T(8,128)(2,1)} %get-tuple-element.134.refs_0_, ...), custom_call_target="tpu_custom_call" | custom-call | flops 2576980480 | bytes 3355443 | tf_op jit(solution)/shard_map/feed_forward/pallas_call | solution.py:371
  171.8 37.0 %feed_forward.3 = (bf16[2048,1024]{1,0:T(8,128)(2,1)}, bf16[2048,1024]{1,0:T(8,128)(2,1)}, bf16[2048,1024]{1,0:T(8,128)(2,1)}, bf16[1024,1024]{1,0:T(8,128)(2,1)...) custom-call(bf16[512,1024]{1,0:T(8,128)(2,1)} %get-tuple-element.134.refs_0_, ...), custom_call_target="tpu_custom_call" | custom-call | flops 2576980480 | bytes 3355443 | tf_op jit(solution)/shard_map/feed_forward/pallas_call | solution.py:371
  208.8 12.5 %sum_products.10 = bf16[1024,1024]{1,0:T(8,128)(2,1)} custom-call(bf16[2048,1024]{1,0:T(8,128)(2,1)} %get-tuple-element.140.refs_0_, bf16[8,384,1024]{2,1,0:T(8,128)(2,1)} %bitcast.13, bf16[2048,1024]{1,0:T(8,128)(2,1)} %get-tuple-element.133.refs_2_, bf16[8,384,1024]{2,1,0:T(8,128)(2,1)} %bitcast.14, bf16[2048,1024]{1,0:T(8,128)(2,1)} %get-tuple-element.135.refs_4_, ...), custom_call_target="tpu_custom_call" | custom-call | flops 858993472 | bytes 2097152 | tf_op jit(solution)/shard_map/sum_products/pallas_call | solution.py:450
  229.5 12.9 %sum_products.11.refs_3_ = f32[1024,1024]{1,0:T(8,128)} custom-call(bf16[2048,1024]{1,0:T(8,128)(2,1)} %get-tuple-element.140.refs_0_, bf16[8,384,1024]{2,1,0:T(8,128)(2,1)} %bitcast.15, bf16[2048,1024]{1,0:T(8,128)(2,1)} %get-tuple-element.133.refs_2_, bf16[8,384,1024]{2,1,0:T(8,128)(2,1)} %bitcast.16, bf16[2048,1024]{1,0:T(8,128)(2,1)} %get-tuple-element.135.refs_4_, ...), custom_call_target="tpu_custom_call" | custom-call | flops 858993472 | bytes 2097152 | tf_op jit(solution)/shard_map/sum_products/pallas_call | solution.py:450
  257.5 8.2 %branch_backward.1 = (bf16[2048,256]{1,0:T(8,128)(2,1)S(1)}, bf16[2048,256]{1,0:T(8,128)(2,1)S(1)}, bf16[256,1024]{1,0:T(8,128)(2,1)S(1)}, bf16[256,1024]{1,0:T(8,128)(2,1)S(1)}) custom-call(bf16[512,1024]{1,0:T(8,128)(2,1)S(1)} %copy-done.22, bf16[512,1024]{1,0:T(8,128)(2,1)} %get-tuple-element.143.refs_1_, ...), custom_call_target="tpu_custom_call" | custom-call | flops 429496736 | bytes 1258291 | tf_op jit(solution)/shard_map/branch_backward/pallas_call | solution.py:522
  277.2 27.3 %attention_backward.4.rest_0_ = bf16[3,2048,256]{2,1,0:T(8,128)(2,1)} custom-call(s32[2]{0:T(128)} %pad_add_fusion.place_ref, bf16[2048,256]{1,0:T(8,128)(2,1)} %copy-done.16, bf16[2048,256]{1,0:T(8,128)(2,1)} %copy-done.17, bf16[2048,256]{1,0:T(8,128)(2,1)} %copy-done.18, bf16[2048,256]{1,0:T(8,128)(2,1)} %get-tuple-element.123.refs_2_.refs_6_.out_ref, ...), custom_call_target="tpu_custom_call" | custom-call | flops 1503238528 | bytes 419430 | tf_op jit(solution)/shard_map/attention_backward/pallas_call | solution.py:283
  305.9 9.0 %collective-permute-done.17 = bf16[1024,1024]{1,0:T(8,128)(2,1)} collective-permute-done((bf16[1024,1024]{1,0:T(8,128)(2,1)}, bf16[1024,1024]{1,0:T(8,128)(2,1)}, u32[]{:S(2)}, u32[]{:S(2)}) %collective-permute-start.17) | collective-permute-done | bytes 2097184 | tf_op jit(solution)/shard_map/ppermute | solution.py:730
  325.1 27.4 %attention_backward.5.refs_4_.refs_0_.refs_2_ = bf16[3,2048,256]{2,1,0:T(8,128)(2,1)} custom-call(s32[2]{0:T(128)} %pad_add_fusion.place_ref, bf16[2048,256]{1,0:T(8,128)(2,1)} %copy-done.16, bf16[2048,256]{1,0:T(8,128)(2,1)} %copy-done.17, bf16[2048,256]{1,0:T(8,128)(2,1)} %copy-done.18, ...), custom_call_target="tpu_custom_call", output_to_operand_aliasing={{}: (11, {})} | custom-call | flops 1503238528 | bytes 419430 | tf_op jit(solution)/shard_map/attention_backward/pallas_call | solution.py:283
  354.4 6.8 %outer_product.2 = bf16[1024,768]{1,0:T(8,128)(2,1)S(1)} custom-call(bf16[512,1024]{1,0:T(8,128)(2,1)S(1)} %copy-done.5, bf16[512,1024]{1,0:T(8,128)(2,1)S(1)} %copy-done.8, bf16[512,1024]{1,0:T(8,128)(2,1)} %collective-permute-done.refs_2_, bf16[512,1024]{1,0:T(8,128)(2,1)} %collective-permute-done.1.refs_3_, bf16[3,2048,256]{2,1,0:T(8,128)(2,1)S(1)} %copy-done.1), custom_call_target="tpu_custom_call" | custom-call | flops 322122560 | bytes 891289 | tf_op jit(solution)/shard_map/outer_product/pallas_call | solution.py:485
  372.1 27.3 %attention_backward.6.rest_0_ = bf16[3,2048,256]{2,1,0:T(8,128)(2,1)} custom-call(s32[2]{0:T(128)} %pad_add_fusion.place_ref, bf16[2048,256]{1,0:T(8,128)(2,1)} %copy-done.13, bf16[2048,256]{1,0:T(8,128)(2,1)} %copy-done.14, bf16[2048,256]{1,0:T(8,128)(2,1)} %copy-done.15, bf16[2048,256]{1,0:T(8,128)(2,1)} %get-tuple-element.116.refs_0_.refs_7_.out_ref, ...), custom_call_target="tpu_custom_call" | custom-call | flops 1503238528 | bytes 419430 | tf_op jit(solution)/shard_map/attention_backward/pallas_call | solution.py:283
  408.1 27.5 %attention_backward.7.refs_4_.refs_6_.refs_8_.refs_10_ = bf16[3,2048,256]{2,1,0:T(8,128)(2,1)} custom-call(s32[2]{0:T(128)} %pad_add_fusion.place_ref, bf16[2048,256]{1,0:T(8,128)(2,1)} %copy-done.13, bf16[2048,256]{1,0:T(8,128)(2,1)} %copy-done.14, bf16[2048,256]{1,0:T(8,128)(2,1)} %copy-done.15, ...), custom_call_target="tpu_custom_call", output_to_operand_aliasing={{}: (11, {})} | custom-call | flops 1503238528 | bytes 419430 | tf_op jit(solution)/shard_map/attention_backward/pallas_call | solution.py:283
  437.5 7.0 %outer_product.3 = bf16[1024,768]{1,0:T(8,128)(2,1)S(1)} custom-call(bf16[512,1024]{1,0:T(8,128)(2,1)S(1)} %copy-done.5, bf16[512,1024]{1,0:T(8,128)(2,1)S(1)} %copy-done.8, bf16[512,1024]{1,0:T(8,128)(2,1)} %collective-permute-done.refs_2_, bf16[512,1024]{1,0:T(8,128)(2,1)} %collective-permute-done.1.refs_3_, bf16[3,2048,256]{2,1,0:T(8,128)(2,1)S(1)} %copy-done), custom_call_target="tpu_custom_call" | custom-call | flops 322122560 | bytes 891289 | tf_op jit(solution)/shard_map/outer_product/pallas_call | solution.py:485
  451.7 7.7 %sum_products.12 = bf16[1024,1024]{1,0:T(8,128)(2,1)} custom-call(bf16[2048,1024]{1,0:T(8,128)(2,1)} %get-tuple-element.190.refs_0_, bf16[8,384,1024]{2,1,0:T(8,128)(2,1)} %bitcast.17, bf16[2048,1024]{1,0:T(8,128)(2,1)} %get-tuple-element.185.refs_2_, bf16[1024,1024]{1,0:T(8,128)(2,1)} %refs_3_.3), custom_call_target="tpu_custom_call" | custom-call | flops 429496736 | bytes 1258291 | tf_op jit(solution)/shard_map/sum_products/pallas_call | solution.py:450
  466.7 6.5 %sum_products.13 = bf16[1024,1024]{1,0:T(8,128)(2,1)} custom-call(bf16[3,2048,256]{2,1,0:T(8,128)(2,1)} %attention_backward.5.refs_4_.refs_0_.refs_2_, bf16[1024,768]{1,0:T(8,128)(2,1)} %collective-permute-done.3.refs_4_.refs_1_.refs_3_.refs_5_, bf16[3,2048,256]{2,1,0:T(8,128)(2,1)} %attention_backward.5.refs_4_.refs_0_.refs_2_, ...), custom_call_target="tpu_custom_call" | custom-call | flops 322122560 | bytes 1048576 | tf_op jit(solution)/shard_map/sum_products/pallas_call | solution.py:450
  474.5 7.8 %sum_products.14 = f32[1024,1024]{1,0:T(8,128)} custom-call(bf16[2048,1024]{1,0:T(8,128)(2,1)} %get-tuple-element.190.refs_0_, bf16[8,384,1024]{2,1,0:T(8,128)(2,1)} %bitcast.18, bf16[2048,1024]{1,0:T(8,128)(2,1)} %get-tuple-element.185.refs_2_, bf16[1024,1024]{1,0:T(8,128)(2,1)} %refs_3_.3), custom_call_target="tpu_custom_call" | custom-call | flops 429496736 | bytes 1258291 | tf_op jit(solution)/shard_map/sum_products/pallas_call | solution.py:450
  482.3 7.5 %sum_products.15.refs_3_ = f32[1024,1024]{1,0:T(8,128)} custom-call(bf16[3,2048,256]{2,1,0:T(8,128)(2,1)} %attention_backward.5.refs_4_.refs_0_.refs_2_, bf16[1024,768]{1,0:T(8,128)(2,1)} %collective-permute-done.3.refs_4_.refs_1_.refs_3_.refs_5_, bf16[3,2048,256]{2,1,0:T(8,128)(2,1)} %attention_backward.5.refs_4_.refs_0_.refs_2_, ...), custom_call_target="tpu_custom_call" | custom-call | flops 322122560 | bytes 1048576 | tf_op jit(solution)/shard_map/sum_products/pallas_call | solution.py:450
  489.9 5.5 add_convert_fusion
  495.3 8.0 %layer_norm_backward.5 = (bf16[1024,1024]{1,0:T(8,128)(2,1)}, f32[2,1024]{1,0:T(2,128)}) custom-call(bf16[1024,1024]{1,0:T(8,128)(2,1)} %refs_0_.7, f32[1024,1024]{1,0:T(8,128)} %get-tuple-element.191.refs_1_, f32[1,1024]{1,0:T(1,128)} %bitcast.25, f32[1024,1024]{1,0:T(8,128)} %sum_products.15.refs_3_, bf16[1024,1024]{1,0:T(8,128)(2,1)} %collective-permute-done.29.refs_4_), custom_call_target="tpu_custom_call" | custom-call | flops 3145728 | bytes 1677721 | tf_op jit(solution)/shard_map/layer_norm_backward/pallas_call | solution.py:637
  503.3 13.7 %all-reduce.10.cloned.1.call-done = bf16[512,768]{1,0:T(8,128)(2,1)} async-done(((bf16[512,768]{1,0:T(8,128)(2,1)}), bf16[512,768]{1,0:T(8,128)(2,1)}) %all-reduce.10.cloned.1.call-update) | async-done | bytes 786448 | tf_op jit(solution)/shard_map/psum | solution.py:853
  537.1 5.9 %collective-permute-done.37 = f32[4,1024]{1,0:T(4,128)S(1)} collective-permute-done((f32[4,1024]{1,0:T(4,128)S(1)}, f32[4,1024]{1,0:T(4,128)S(1)}, u32[]{:S(2)}, u32[]{:S(2)}) %collective-permute-start.37) | collective-permute-done | bytes 16416 | tf_op jit(solution)/shard_map/ppermute | solution.py:686
  (233 shorter events, 164.1 us)
Async XLA Ops:
  7.2 126.8 %all-gather.3.cloned.1.call-start = ((), (), s32[]{:S(2)}) async-start(), calls=%async_computation.3 | async-start | bytes 7077888 | tf_op jit(solution)/shard_map/all_gather | solution.py:758
  10.2 22.9 %collective-permute-start.2 = (bf16[384,1024]{1,0:T(8,128)(2,1)}, bf16[384,1024]{1,0:T(8,128)(2,1)}, u32[]{:S(2)}, u32[]{:S(2)}) collective-permute-start(bf16[384,1024]{1,0:T(8,128)(2,1)} %pad_maximum_fusion), channel_id=1, source_target_pairs={{2,0},{3,1},{0,2},{1,3},{6,4},{7,5},{4,6},{5,7},{10,8},{11,9},{8,1... | collective-permute-start | bytes 2359304 | tf_op jit(solution)/shard_map/ppermute | solution.py:730
  33.2 329.2 %all-reduce.8.cloned.1.call-start = ((), (), s32[]{:S(2)}) async-start(), calls=%async_computation.1 | async-start | bytes 2097152 | tf_op jit(solution)/shard_map/psum | solution.py:853
  33.8 48.6 %collective-permute-start.4 = (bf16[1024,1024]{1,0:T(8,128)(2,1)}, bf16[1024,1024]{1,0:T(8,128)(2,1)}, u32[]{:S(2)}, u32[]{:S(2)}) collective-permute-start(bf16[1024,1024]{1,0:T(8,128)(2,1)} %refs_1_.7), channel_id=1, source_target_pairs={{1,0},{0,1},{3,2},{2,3},{5,4},{4,5},{7,6},{6,7},{9,8},{8,9},{11,10... | collective-permute-start | bytes 6291464 | tf_op jit(solution)/shard_map/ppermute | solution.py:723
  33.9 37.5 %collective-permute-start.3 = (bf16[1024,768]{1,0:T(8,128)(2,1)}, bf16[1024,768]{1,0:T(8,128)(2,1)}, u32[]{:S(2)}, u32[]{:S(2)}) collective-permute-start(bf16[1024,768]{1,0:T(8,128)(2,1)} %copy-done.4), channel_id=1, source_target_pairs={{2,0},{3,1},{0,2},{1,3},{6,4},{7,5},{4,6},{5,7},{10,8},{11,9},{8,1... | collective-permute-start | bytes 4718600 | tf_op jit(solution)/shard_map/ppermute | solution.py:730
  64.3 46.6 %collective-permute-start.5 = (bf16[256,1024]{1,0:T(8,128)(2,1)S(1)}, bf16[256,1024]{1,0:T(8,128)(2,1)S(1)}, u32[]{:S(2)}, u32[]{:S(2)}) collective-permute-start(bf16[256,1024]{1,0:T(8,128)(2,1)S(1)} %copy-done.9), channel_id=1, source_target_pairs={{2,0},{3,1},{0,2},{1,3},{6,4},{7,5},{4,6},{5,7},{10,8},{11,9},{8,1... | collective-permute-start | bytes 1572872 | tf_op jit(solution)/shard_map/ppermute | solution.py:730
  171.6 51.8 %collective-permute-start.10 = (bf16[1024,1024]{1,0:T(8,128)(2,1)}, bf16[1024,1024]{1,0:T(8,128)(2,1)}, u32[]{:S(2)}, u32[]{:S(2)}) collective-permute-start(bf16[1024,1024]{1,0:T(8,128)(2,1)} %get-tuple-element.132), channel_id=1, source_target_pairs={{2,0},{3,1},{0,2},{1,3},{6,4},{7,5},{4,6},{5,7},{10,8},{11,9},{8,1... | collective-permute-start | bytes 6291464 | tf_op jit(solution)/shard_map/ppermute | solution.py:730
  221.7 48.8 %collective-permute-start.9 = (bf16[1024,1024]{1,0:T(8,128)(2,1)}, bf16[1024,1024]{1,0:T(8,128)(2,1)}, u32[]{:S(2)}, u32[]{:S(2)}) collective-permute-start(bf16[1024,1024]{1,0:T(8,128)(2,1)} %get-tuple-element.130), channel_id=1, source_target_pairs={{2,0},{3,1},{0,2},{1,3},{6,4},{7,5},{4,6},{5,7},{10,8},{11,9},{8,1... | collective-permute-start | bytes 6291464 | tf_op jit(solution)/shard_map/ppermute | solution.py:730
  227.9 26.6 %collective-permute-start.12 = (bf16[512,1024]{1,0:T(8,128)(2,1)}, bf16[512,1024]{1,0:T(8,128)(2,1)}, u32[]{:S(2)}, u32[]{:S(2)}) collective-permute-start(bf16[512,1024]{1,0:T(8,128)(2,1)} %get-tuple-element.209), channel_id=1, source_target_pairs={{0,4},{4,0},{8,12},{12,8},{16,20},{20,16},{24,28},{28,24},{1,5},{5... | collective-permute-start | bytes 3145736 | tf_op jit(solution)/shard_map/ppermute | solution.py:841
  254.1 60.8 %collective-permute-start.17 = (bf16[1024,1024]{1,0:T(8,128)(2,1)}, bf16[1024,1024]{1,0:T(8,128)(2,1)}, u32[]{:S(2)}, u32[]{:S(2)}) collective-permute-start(bf16[1024,1024]{1,0:T(8,128)(2,1)} %get-tuple-element.159), channel_id=1, source_target_pairs={{2,0},{3,1},{0,2},{1,3},{6,4},{7,5},{4,6},{5,7},{10,8},{11,9},{8,1... | collective-permute-start | bytes 6291464 | tf_op jit(solution)/shard_map/ppermute | solution.py:730
  274.0 30.5 %collective-permute-start.16 = (bf16[512,1024]{1,0:T(8,128)(2,1)}, bf16[512,1024]{1,0:T(8,128)(2,1)S(1)}, u32[]{:S(2)}, u32[]{:S(2)}) collective-permute-start(bf16[512,1024]{1,0:T(8,128)(2,1)} %get-tuple-element.208), channel_id=1, source_target_pairs={{0,4},{4,0},{8,12},{12,8},{16,20},{20,16},{24,28},{28,24},{1,5},{5... | collective-permute-start | bytes 3145736 | tf_op jit(solution)/shard_map/ppermute | solution.py:841
  275.8 123.6 %all-reduce.6.cloned.1.call-start = ((), (), s32[]{:S(2)}) async-start(), calls=%async_computation | async-start | bytes 2097152 | tf_op jit(solution)/shard_map/psum | solution.py:853
  319.4 50.1 %collective-permute-start.19 = (bf16[512,1024]{1,0:T(8,128)(2,1)}, bf16[512,1024]{1,0:T(8,128)(2,1)}, u32[]{:S(2)}, u32[]{:S(2)}) collective-permute-start(bf16[512,1024]{1,0:T(8,128)(2,1)} %get-tuple-element.206), channel_id=1, source_target_pairs={{0,4},{4,0},{8,12},{12,8},{16,20},{20,16},{24,28},{28,24},{1,5},{5... | collective-permute-start | bytes 3145736 | tf_op jit(solution)/shard_map/ppermute | solution.py:841
  322.8 41.6 %collective-permute-start.20 = (bf16[256,1024]{1,0:T(8,128)(2,1)S(1)}, bf16[256,1024]{1,0:T(8,128)(2,1)}, u32[]{:S(2)}, u32[]{:S(2)}) collective-permute-start(bf16[256,1024]{1,0:T(8,128)(2,1)S(1)} %copy-done.26), channel_id=1, source_target_pairs={{2,0},{3,1},{0,2},{1,3},{6,4},{7,5},{4,6},{5,7},{10,8},{11,9},{8,1... | collective-permute-start | bytes 1572872 | tf_op jit(solution)/shard_map/ppermute | solution.py:730
  325.0 141.7 %all-reduce.12.cloned.1.call-start = ((), (), s32[]{:S(2)}) async-start(), calls=%async_computation.4 | async-start | bytes 2621440 | tf_op jit(solution)/shard_map/psum | solution.py:853
  362.4 37.1 %collective-permute-start.23 = (bf16[512,1024]{1,0:T(8,128)(2,1)}, bf16[512,1024]{1,0:T(8,128)(2,1)}, u32[]{:S(2)}, u32[]{:S(2)}) collective-permute-start(bf16[512,1024]{1,0:T(8,128)(2,1)} %all-reduce.8.cloned.1.call-done), channel_id=1, source_target_pairs={{0,4},{4,0},{8,12},{12,8},{16,20},{20,16},{24,28},{28,24},{1,5},{5... | collective-permute-start | bytes 3145736 | tf_op jit(solution)/shard_map/ppermute | solution.py:857
  362.6 81.9 %collective-permute-start.22 = (bf16[1024,768]{1,0:T(8,128)(2,1)}, bf16[1024,768]{1,0:T(8,128)(2,1)}, u32[]{:S(2)}, u32[]{:S(2)}) collective-permute-start(bf16[1024,768]{1,0:T(8,128)(2,1)} %copy-done.21), channel_id=1, source_target_pairs={{2,0},{3,1},{0,2},{1,3},{6,4},{7,5},{4,6},{5,7},{10,8},{11,9},{8,1... | collective-permute-start | bytes 4718600 | tf_op jit(solution)/shard_map/ppermute | solution.py:730
  367.9 31.5 %collective-permute-start.24 = (bf16[128,1024]{1,0:T(8,128)(2,1)}, bf16[128,1024]{1,0:T(8,128)(2,1)}, u32[]{:S(2)}, u32[]{:S(2)}) collective-permute-start(bf16[128,1024]{1,0:T(8,128)(2,1)} %get-tuple-element.224), channel_id=1, source_target_pairs={{0,4},{4,0},{8,12},{12,8},{16,20},{20,16},{24,28},{28,24},{1,5},{5... | collective-permute-start | bytes 786440 | tf_op jit(solution)/shard_map/ppermute | solution.py:841
  402.1 45.8 %collective-permute-start.26 = (bf16[512,1024]{1,0:T(8,128)(2,1)}, bf16[512,1024]{1,0:T(8,128)(2,1)}, u32[]{:S(2)}, u32[]{:S(2)}) collective-permute-start(bf16[512,1024]{1,0:T(8,128)(2,1)} %all-reduce.6.cloned.1.call-done), channel_id=1, source_target_pairs={{0,4},{4,0},{8,12},{12,8},{16,20},{20,16},{24,28},{28,24},{1,5},{5... | collective-permute-start | bytes 3145736 | tf_op jit(solution)/shard_map/ppermute | solution.py:857
  408.1 109.0 %all-reduce.10.cloned.1.call-start = ((), (), s32[]{:S(2)}) async-start(), calls=%async_computation.2 | async-start | bytes 1572864 | tf_op jit(solution)/shard_map/psum | solution.py:853
  459.4 30.4 %collective-permute-start.28 = (bf16[1024,1024]{1,0:T(8,128)(2,1)}, bf16[1024,1024]{1,0:T(8,128)(2,1)}, u32[]{:S(2)}, u32[]{:S(2)}) collective-permute-start(bf16[1024,1024]{1,0:T(8,128)(2,1)} %sum_products.12), channel_id=1, source_target_pairs={{1,0},{0,1},{3,2},{2,3},{5,4},{4,5},{7,6},{6,7},{9,8},{8,9},{11,10... | collective-permute-start | bytes 6291464 | tf_op jit(solution)/shard_map/ppermute | solution.py:723
  473.2 22.1 %collective-permute-start.29 = (bf16[1024,1024]{1,0:T(8,128)(2,1)}, bf16[1024,1024]{1,0:T(8,128)(2,1)}, u32[]{:S(2)}, u32[]{:S(2)}) collective-permute-start(bf16[1024,1024]{1,0:T(8,128)(2,1)} %sum_products.13), channel_id=1, source_target_pairs={{1,0},{0,1},{3,2},{2,3},{5,4},{4,5},{7,6},{6,7},{9,8},{8,9},{11,10... | collective-permute-start | bytes 6291464 | tf_op jit(solution)/shard_map/ppermute | solution.py:723
  473.3 45.8 %collective-permute-start.32 = (bf16[512,1024]{1,0:T(8,128)(2,1)S(1)}, bf16[512,1024]{1,0:T(8,128)(2,1)}, u32[]{:S(2)}, u32[]{:S(2)}) collective-permute-start(bf16[512,1024]{1,0:T(8,128)(2,1)S(1)} %copy-done.35), channel_id=1, source_target_pairs={{0,4},{4,0},{8,12},{12,8},{16,20},{20,16},{24,28},{28,24},{1,5},{5... | collective-permute-start | bytes 3145736 | tf_op jit(solution)/shard_map/ppermute | solution.py:857
  518.5 25.1 %collective-permute-start.30 = (bf16[512,768]{1,0:T(8,128)(2,1)}, bf16[512,768]{1,0:T(8,128)(2,1)S(1)}, u32[]{:S(2)}, u32[]{:S(2)}) collective-permute-start(bf16[512,768]{1,0:T(8,128)(2,1)} %all-reduce.10.cloned.1.call-done), channel_id=1, source_target_pairs={{0,4},{4,0},{8,12},{12,8},{16,20},{20,16},{24,28},{28,24},{1,5},{5... | collective-permute-start | bytes 2359304 | tf_op jit(solution)/shard_map/ppermute | solution.py:857
  (64 other events, 581.3 us)
Sparse Core Ops, SparseCore 0:
  33.3 99.3 all-gather.2
  276.0 52.1 all-reduce.7
  330.7 51.0 all-reduce.5
  408.2 58.4 all-reduce.11
  474.6 42.4 all-reduce.9

commit v4 on v3

--- a/solution.py
+++ b/solution.py
@@ -17,7 +17,7 @@
 BF16 = jnp.bfloat16
 F32 = jnp.float32
 MIB = 1 << 20
-COST_SHARE = 0.1
+COST_SHARE = 0.01
 PIECES = 2
 
 
@@ -915,26 +915,24 @@
     def up_sum(last):
         value = add_half(sums["up"], *last)
         sums["up"] = sum_half(value, 1)
-        sums["gate"], waits = swap_half(gate_pieces, value)
-        return [value] + waits
+        return [value]
+
+    def gate_swap(last):
+        sums["gate"], waits = swap_half(gate_pieces, *last)
+        sums["out"], more = swap_half(out_pieces, *last)
+        sums["down"] = after(down_sum, *waits, *more)
+        return waits + more + [sums["down"]]
 
     def gate_sum(last):
-        sums["gate"] = value = add_half(sums["gate"], *last)
-        sums["out"], waits = swap_half(out_pieces, *last)
-        sums["down"] = swap_sum(down_sum, *last)
-        return [value, sums["down"][0]] + waits
-
-    def down_whole(last):
-        sums["down"] = whole_sum(sums["down"], *last)
-        value = add_half(sums["out"], *last)
-        sums["gate"], sums["out"] = sum_half((sums["gate"], value), 2)
+        values = add_half(sums["gate"], *last), add_half(sums["out"], *last)
+        sums["gate"], sums["out"] = sum_half(values, 2)
         sums["up"] = swap_sum(sums["up"], *last)
-        return [sums["down"], value, sums["up"][0]]
+        return [*values, sums["up"][0]]
 
     across, along = (exchanges(axis, size) for axis, size in (("tensor", tensor_size), ("dp", dp_size)))
     norm_steps = across + along[1:]
     sums = {}
-    moves = [up_swap, up_sum, gate_sum, down_whole]
+    moves = [up_swap, up_sum, gate_swap, gate_sum]
     last = list(grad_mixed)
     grad_qkv, qkv_grads = [], {}
     for index, group in enumerate(members):
@@ -982,7 +980,8 @@
 
     qkv_half, marks = swap_half(send_to_owner(qkv_grads) + [qkv_grads[0]])
     grad_up = whole_sum(sums["up"], *marks)
-    feed_terms[0] = (after(feed_terms[0][0], grad_up), *feed_terms[0][1:])
+    down_halves = swap_sum(sums["down"], *marks)
+    feed_terms[0] = (after(feed_terms[0][0], grad_up, down_halves[0]), *feed_terms[0][1:])
     one_terms = [
         (grad_qkv[index], part, weight, part, 1)
         for index, weight in enumerate(qkv_weights)
@@ -1008,7 +1007,6 @@
     (input_grad,), _, norm_one = norm_back(tokens, grad_hidden, gain_first, one_parts, True, 1)
     for step in norm_steps:
         norm_two = step(norm_two)
-    grad_down = sums["down"]
     window = [input_grad, output]
     qkv_halves = swap_sum(qkv_sum, *window)
     norm_one = after(norm_one, qkv_halves[0])
@@ -1016,6 +1014,7 @@
         norm_one = step(norm_one)
     norms = along[0](jnp.concatenate([norm_one, norm_two], axis=0))
     norm_one, norm_two = norms[:2], norms[2:]
+    grad_down = whole_sum(down_halves, qkv_halves[0])
     grad_gate = whole_sum(gate_halves, qkv_halves[0])
     out_grad = whole_sum(out_halves, qkv_halves[0])
     qkv_grad = whole_sum(qkv_halves)

time: 558 us -> 561 us (level)
    ppermute x8, waiting for transfers between devices: 19 us -> 10 us  [from_window(): return lax.ppermute(value, 'tensor', pairs)]
    ppermute x9, waiting for transfers between devices: 11.8 us -> 19.1 us  [exchanges(): lax.ppermute(value, axis, pairs)]
  transfers between devices with their start and end apart: 43 -> 43, of which waited for: 14 -> 16; matrix products, arithmetic and copies ran while one was open for 9% -> 9% of each run, Pallas kernels for 60% -> 60%
where the time goes in v4:
time: 561 us; the launch traced here: 556 us
  Pallas kernels  371 us (66%)
  waiting for transfers between devices  62.6 us (11%)
  other arithmetic  51 us (9%)
  starting transfers between devices  37.2 us (7%)
  local copies, waits for them, and re-layouts  19.2 us (3%)
  between operations  14.8 us (3%)
    pallas_call x4, Pallas kernels, attend_back(): pl.pallas_call(functools.partial(attend_back_kernel, chunk=chunk), grid_s...  109 us
    pallas_call x2, Pallas kernels, feed(): pl.pallas_call(functools.partial(feed_kernel, counts=(len(rows), len(targ...  73.7 us
    pallas_call x8, Pallas kernels, sum_products(): pl.pallas_call(functools.partial(sum_kernel, places=places, dims=tuple(di...  63.4 us
    pallas_call x2, Pallas kernels, attend(): pl.pallas_call(functools.partial(attend_kernel, chunk=chunk), grid_spec=p...  56.9 us
    psum x4, waiting for transfers between devices, sum_half(): return lax.psum(value, 'dp', axis_index_groups=groups)  20 us
    ppermute x9, waiting for transfers between devices, exchanges(): lax.ppermute(value, axis, pairs)  19.1 us
    pallas_call x3, Pallas kernels, norm_back(): pl.pallas_call(lambda *refs, held=len(held): norm_back_kernel(*refs[:3 +...  17.7 us
    convert_element_type x5, other arithmetic, total(): sum((half(piece, which).astype(F32) for piece in pieces)).astype(BF16)  15.7 us
  transfers between devices with their start and end apart: 43, of which 16 were waited for; matrix products, arithmetic and copies ran while one was open for 9% of the time, Pallas kernels for 60%

profile of v4, /device:TPU:0, one launch (start us, length us, event | category | flops | bytes accessed | tf_op | source)
XLA Modules:
  0.0 555.8 jit_solution(17816470237447196633)
XLA Ops:
  23.7 6.5 %project_rope.2 = (bf16[2048,256]{1,0:T(8,128)(2,1)S(1)}, bf16[2048,256]{1,0:T(8,128)(2,1)S(1)}, bf16[2048,256]{1,0:T(8,128)(2,1)S(1)}) custom-call(bf16[512,1024]{1,0:T(8,128)(2,1)S(1)} %copy-done.5, bf16[512,1024]{1,0:T(8,128)(2,1)S(1)} %copy-done.6, bf16[512,1024]{1,0:T(8,128)(2,1)} %collective-permute-done.refs_2_, ...), custom_call_target="tpu_custom_call" | custom-call | flops 32212254 | bytes 89128 | tf_op jit(solution)/shard_map/project_rope/pallas_call | solution.py:105
  35.8 28.4 %attention_forward.2 = (bf16[2048,256]{1,0:T(8,128)(2,1)}, f32[2,8,2048]{2,1,0:T(8,128)}) custom-call(s32[2]{0:T(128)} %pad_add_fusion.place_ref, bf16[2048,256]{1,0:T(8,128)(2,1)} %copy-done.9, bf16[2048,256]{1,0:T(8,128)(2,1)} %copy-done.10, bf16[2048,256]{1,0:T(8,128)(2,1)} %copy-done.11), custom_call_target="tpu_custom_call" | custom-call | flops 171798688 | bytes 41943 | tf_op jit(solution)/shard_map/attention_forward/pallas_call | solution.py:184
  71.5 7.9 %project_rope.3 = (bf16[2048,256]{1,0:T(8,128)(2,1)S(1)}, bf16[2048,256]{1,0:T(8,128)(2,1)S(1)}, bf16[2048,256]{1,0:T(8,128)(2,1)S(1)}) custom-call(bf16[512,1024]{1,0:T(8,128)(2,1)S(1)} %copy-done.5, bf16[512,1024]{1,0:T(8,128)(2,1)S(1)} %copy-done.7, bf16[512,1024]{1,0:T(8,128)(2,1)} %collective-permute-done.refs_2_, ...), custom_call_target="tpu_custom_call" | custom-call | flops 32212254 | bytes 89128 | tf_op jit(solution)/shard_map/project_rope/pallas_call | solution.py:105
  82.3 28.5 %attention_forward.3 = (bf16[2048,256]{1,0:T(8,128)(2,1)}, f32[2,8,2048]{2,1,0:T(8,128)}) custom-call(s32[2]{0:T(128)} %pad_add_fusion.place_ref, bf16[2048,256]{1,0:T(8,128)(2,1)} %copy-done.12, bf16[2048,256]{1,0:T(8,128)(2,1)} %copy-done.13, bf16[2048,256]{1,0:T(8,128)(2,1)} %copy-done.14), custom_call_target="tpu_custom_call" | custom-call | flops 171798688 | bytes 41943 | tf_op jit(solution)/shard_map/attention_forward/pallas_call | solution.py:184
  135.0 36.7 %feed_forward.2 = (bf16[2048,1024]{1,0:T(8,128)(2,1)}, bf16[2048,1024]{1,0:T(8,128)(2,1)}, bf16[2048,1024]{1,0:T(8,128)(2,1)}, bf16[1024,1024]{1,0:T(8,128)(2,1)...) custom-call(bf16[512,1024]{1,0:T(8,128)(2,1)} %get-tuple-element.135.refs_0_, ...), custom_call_target="tpu_custom_call" | custom-call | flops 257698032 | bytes 335544 | tf_op jit(solution)/shard_map/feed_forward/pallas_call | solution.py:371
  171.8 37.0 %feed_forward.3 = (bf16[2048,1024]{1,0:T(8,128)(2,1)}, bf16[2048,1024]{1,0:T(8,128)(2,1)}, bf16[2048,1024]{1,0:T(8,128)(2,1)}, bf16[1024,1024]{1,0:T(8,128)(2,1)...) custom-call(bf16[512,1024]{1,0:T(8,128)(2,1)} %get-tuple-element.135.refs_0_, ...), custom_call_target="tpu_custom_call" | custom-call | flops 257698032 | bytes 335544 | tf_op jit(solution)/shard_map/feed_forward/pallas_call | solution.py:371
  208.8 12.5 %sum_products.10 = bf16[1024,1024]{1,0:T(8,128)(2,1)} custom-call(bf16[2048,1024]{1,0:T(8,128)(2,1)} %get-tuple-element.141.refs_0_, bf16[8,384,1024]{2,1,0:T(8,128)(2,1)} %bitcast.13, bf16[2048,1024]{1,0:T(8,128)(2,1)} %get-tuple-element.134.refs_2_, bf16[8,384,1024]{2,1,0:T(8,128)(2,1)} %bitcast.14, bf16[2048,1024]{1,0:T(8,128)(2,1)} %get-tuple-element.136.refs_4_, ...), custom_call_target="tpu_custom_call" | custom-call | flops 85899344 | bytes 209715 | tf_op jit(solution)/shard_map/sum_products/pallas_call | solution.py:450
  229.5 12.9 %sum_products.11.refs_3_ = f32[1024,1024]{1,0:T(8,128)} custom-call(bf16[2048,1024]{1,0:T(8,128)(2,1)} %get-tuple-element.141.refs_0_, bf16[8,384,1024]{2,1,0:T(8,128)(2,1)} %bitcast.15, bf16[2048,1024]{1,0:T(8,128)(2,1)} %get-tuple-element.134.refs_2_, bf16[8,384,1024]{2,1,0:T(8,128)(2,1)} %bitcast.16, bf16[2048,1024]{1,0:T(8,128)(2,1)} %get-tuple-element.136.refs_4_, ...), custom_call_target="tpu_custom_call" | custom-call | flops 85899344 | bytes 209715 | tf_op jit(solution)/shard_map/sum_products/pallas_call | solution.py:450
  257.6 8.2 %branch_backward.1 = (bf16[2048,256]{1,0:T(8,128)(2,1)S(1)}, bf16[2048,256]{1,0:T(8,128)(2,1)S(1)}, bf16[256,1024]{1,0:T(8,128)(2,1)S(1)}, bf16[256,1024]{1,0:T(8,128)(2,1)S(1)}) custom-call(bf16[512,1024]{1,0:T(8,128)(2,1)S(1)} %copy-done.21, bf16[512,1024]{1,0:T(8,128)(2,1)} %get-tuple-element.144.refs_1_, ...), custom_call_target="tpu_custom_call" | custom-call | flops 42949672 | bytes 125829 | tf_op jit(solution)/shard_map/branch_backward/pallas_call | solution.py:522
  277.2 27.4 %attention_backward.4.rest_0_ = bf16[3,2048,256]{2,1,0:T(8,128)(2,1)} custom-call(s32[2]{0:T(128)} %pad_add_fusion.place_ref, bf16[2048,256]{1,0:T(8,128)(2,1)} %copy-done.12, bf16[2048,256]{1,0:T(8,128)(2,1)} %copy-done.13, bf16[2048,256]{1,0:T(8,128)(2,1)} %copy-done.14, bf16[2048,256]{1,0:T(8,128)(2,1)} %get-tuple-element.124.refs_2_.refs_6_.out_ref, ...), custom_call_target="tpu_custom_call" | custom-call | flops 150323856 | bytes 41943 | tf_op jit(solution)/shard_map/attention_backward/pallas_call | solution.py:283
  306.1 8.9 %collective-permute-done.18 = f32[2,1024]{1,0:T(2,128)S(1)} collective-permute-done((f32[2,1024]{1,0:T(2,128)S(1)}, f32[2,1024]{1,0:T(2,128)S(1)}, u32[]{:S(2)}, u32[]{:S(2)}) %collective-permute-start.18) | collective-permute-done | bytes 8224 | tf_op jit(solution)/shard_map/ppermute | solution.py:686
  319.6 27.1 %attention_backward.5.refs_4_.refs_0_.refs_2_ = bf16[3,2048,256]{2,1,0:T(8,128)(2,1)} custom-call(s32[2]{0:T(128)} %pad_add_fusion.place_ref, bf16[2048,256]{1,0:T(8,128)(2,1)} %copy-done.12, bf16[2048,256]{1,0:T(8,128)(2,1)} %copy-done.13, bf16[2048,256]{1,0:T(8,128)(2,1)} %copy-done.14, ...), custom_call_target="tpu_custom_call", output_to_operand_aliasing={{}: (11, {})} | custom-call | flops 150323856 | bytes 41943 | tf_op jit(solution)/shard_map/attention_backward/pallas_call | solution.py:283
  348.6 7.6 %outer_product.2 = bf16[1024,768]{1,0:T(8,128)(2,1)} custom-call(bf16[512,1024]{1,0:T(8,128)(2,1)S(1)} %copy-done.5, bf16[512,1024]{1,0:T(8,128)(2,1)S(1)} %copy-done.8, bf16[512,1024]{1,0:T(8,128)(2,1)} %collective-permute-done.refs_2_, bf16[512,1024]{1,0:T(8,128)(2,1)} %collective-permute-done.1.refs_3_, bf16[3,2048,256]{2,1,0:T(8,128)(2,1)S(1)} %copy-done.1), custom_call_target="tpu_custom_call" | custom-call | flops 32212254 | bytes 89128 | tf_op jit(solution)/shard_map/outer_product/pallas_call | solution.py:485
  368.9 27.3 %attention_backward.6.rest_0_ = bf16[3,2048,256]{2,1,0:T(8,128)(2,1)} custom-call(s32[2]{0:T(128)} %pad_add_fusion.place_ref, bf16[2048,256]{1,0:T(8,128)(2,1)} %copy-done.9, bf16[2048,256]{1,0:T(8,128)(2,1)} %copy-done.10, bf16[2048,256]{1,0:T(8,128)(2,1)} %copy-done.11, bf16[2048,256]{1,0:T(8,128)(2,1)} %get-tuple-element.117.refs_0_.refs_7_.out_ref, ...), custom_call_target="tpu_custom_call" | custom-call | flops 150323856 | bytes 41943 | tf_op jit(solution)/shard_map/attention_backward/pallas_call | solution.py:283
  406.9 27.4 %attention_backward.7.refs_4_.refs_6_.refs_8_.refs_10_ = bf16[3,2048,256]{2,1,0:T(8,128)(2,1)} custom-call(s32[2]{0:T(128)} %pad_add_fusion.place_ref, bf16[2048,256]{1,0:T(8,128)(2,1)} %copy-done.9, bf16[2048,256]{1,0:T(8,128)(2,1)} %copy-done.10, bf16[2048,256]{1,0:T(8,128)(2,1)} %copy-done.11, ...), custom_call_target="tpu_custom_call", output_to_operand_aliasing={{}: (11, {})} | custom-call | flops 150323856 | bytes 41943 | tf_op jit(solution)/shard_map/attention_backward/pallas_call | solution.py:283
  436.2 7.0 %outer_product.3 = bf16[1024,768]{1,0:T(8,128)(2,1)S(1)} custom-call(bf16[512,1024]{1,0:T(8,128)(2,1)S(1)} %copy-done.5, bf16[512,1024]{1,0:T(8,128)(2,1)S(1)} %copy-done.8, bf16[512,1024]{1,0:T(8,128)(2,1)} %collective-permute-done.refs_2_, bf16[512,1024]{1,0:T(8,128)(2,1)} %collective-permute-done.1.refs_3_, bf16[3,2048,256]{2,1,0:T(8,128)(2,1)S(1)} %copy-done), custom_call_target="tpu_custom_call" | custom-call | flops 32212254 | bytes 89128 | tf_op jit(solution)/shard_map/outer_product/pallas_call | solution.py:485
  449.4 7.6 %sum_products.12 = bf16[1024,1024]{1,0:T(8,128)(2,1)} custom-call(bf16[2048,1024]{1,0:T(8,128)(2,1)} %get-tuple-element.190.refs_0_, bf16[8,384,1024]{2,1,0:T(8,128)(2,1)} %bitcast.17, bf16[2048,1024]{1,0:T(8,128)(2,1)} %get-tuple-element.185.refs_2_, bf16[1024,1024]{1,0:T(8,128)(2,1)} %refs_3_.3), custom_call_target="tpu_custom_call" | custom-call | flops 42949672 | bytes 125829 | tf_op jit(solution)/shard_map/sum_products/pallas_call | solution.py:450
  460.7 6.9 %all-reduce.12.cloned.1.call-done = (bf16[512,1024]{1,0:T(8,128)(2,1)}, bf16[128,1024]{1,0:T(8,128)(2,1)}) async-done(((bf16[512,1024]{1,0:T(8,128)(2,1)}, bf16[128,1024]{1,0:T(8,128)(2,1)}), (bf16[512,1024]{1,0:T(8,128)(2,1)}, bf16[128,1024]{1,0:T(8,128)(2,1)})) %all-reduce.12.cloned.1.call-update) | async-done | bytes 1310736 | tf_op jit(solution)/shard_map/psum | solution.py:853
  468.6 6.6 %sum_products.13 = bf16[1024,1024]{1,0:T(8,128)(2,1)} custom-call(bf16[3,2048,256]{2,1,0:T(8,128)(2,1)} %attention_backward.5.refs_4_.refs_0_.refs_2_, bf16[1024,768]{1,0:T(8,128)(2,1)} %collective-permute-done.3.refs_4_.refs_1_.refs_3_.refs_5_, bf16[3,2048,256]{2,1,0:T(8,128)(2,1)} %attention_backward.5.refs_4_.refs_0_.refs_2_, ...), custom_call_target="tpu_custom_call" | custom-call | flops 32212254 | bytes 104857 | tf_op jit(solution)/shard_map/sum_products/pallas_call | solution.py:450
  478.9 7.8 %sum_products.14 = f32[1024,1024]{1,0:T(8,128)} custom-call(bf16[2048,1024]{1,0:T(8,128)(2,1)} %get-tuple-element.190.refs_0_, bf16[8,384,1024]{2,1,0:T(8,128)(2,1)} %bitcast.18, bf16[2048,1024]{1,0:T(8,128)(2,1)} %get-tuple-element.185.refs_2_, bf16[1024,1024]{1,0:T(8,128)(2,1)} %refs_3_.3), custom_call_target="tpu_custom_call" | custom-call | flops 42949672 | bytes 125829 | tf_op jit(solution)/shard_map/sum_products/pallas_call | solution.py:450
  486.8 7.6 %sum_products.15.refs_3_ = f32[1024,1024]{1,0:T(8,128)} custom-call(bf16[3,2048,256]{2,1,0:T(8,128)(2,1)} %attention_backward.5.refs_4_.refs_0_.refs_2_, bf16[1024,768]{1,0:T(8,128)(2,1)} %collective-permute-done.3.refs_4_.refs_1_.refs_3_.refs_5_, bf16[3,2048,256]{2,1,0:T(8,128)(2,1)} %attention_backward.5.refs_4_.refs_0_.refs_2_, ...), custom_call_target="tpu_custom_call" | custom-call | flops 32212254 | bytes 104857 | tf_op jit(solution)/shard_map/sum_products/pallas_call | solution.py:450
  494.4 5.5 add_convert_fusion
  499.8 8.0 %layer_norm_backward.5 = (bf16[1024,1024]{1,0:T(8,128)(2,1)}, f32[2,1024]{1,0:T(2,128)}) custom-call(bf16[1024,1024]{1,0:T(8,128)(2,1)} %refs_0_.7, f32[1024,1024]{1,0:T(8,128)} %get-tuple-element.191.refs_1_, f32[1,1024]{1,0:T(1,128)} %bitcast.25, f32[1024,1024]{1,0:T(8,128)} %sum_products.15.refs_3_, bf16[1024,1024]{1,0:T(8,128)(2,1)} %collective-permute-done.28.refs_4_), custom_call_target="tpu_custom_call" | custom-call | flops 314572 | bytes 167772 | tf_op jit(solution)/shard_map/layer_norm_backward/pallas_call | solution.py:637
  507.8 13.0 %all-reduce.10.cloned.1.call-done = bf16[512,768]{1,0:T(8,128)(2,1)} async-done(((bf16[512,768]{1,0:T(8,128)(2,1)}), bf16[512,768]{1,0:T(8,128)(2,1)}) %all-reduce.10.cloned.1.call-update) | async-done | bytes 786448 | tf_op jit(solution)/shard_map/psum | solution.py:853
  (233 shorter events, 166.8 us)
Async XLA Ops:
  7.2 126.8 %all-gather.3.cloned.1.call-start = ((), (), s32[]{:S(2)}) async-start(), calls=%async_computation.3 | async-start | bytes 7077888 | tf_op jit(solution)/shard_map/all_gather | solution.py:758
  33.2 333.2 %all-reduce.8.cloned.1.call-start = ((), (), s32[]{:S(2)}) async-start(), calls=%async_computation.1 | async-start | bytes 2097152 | tf_op jit(solution)/shard_map/psum | solution.py:853
  33.8 48.6 %collective-permute-start.4 = (bf16[1024,1024]{1,0:T(8,128)(2,1)}, bf16[1024,1024]{1,0:T(8,128)(2,1)}, u32[]{:S(2)}, u32[]{:S(2)}) collective-permute-start(bf16[1024,1024]{1,0:T(8,128)(2,1)} %refs_1_.7), channel_id=1, source_target_pairs={{1,0},{0,1},{3,2},{2,3},{5,4},{4,5},{7,6},{6,7},{9,8},{8,9},{11,10... | collective-permute-start | bytes 6291464 | tf_op jit(solution)/shard_map/ppermute | solution.py:723
  33.9 37.5 %collective-permute-start.3 = (bf16[1024,768]{1,0:T(8,128)(2,1)}, bf16[1024,768]{1,0:T(8,128)(2,1)}, u32[]{:S(2)}, u32[]{:S(2)}) collective-permute-start(bf16[1024,768]{1,0:T(8,128)(2,1)} %copy-done.4), channel_id=1, source_target_pairs={{2,0},{3,1},{0,2},{1,3},{6,4},{7,5},{4,6},{5,7},{10,8},{11,9},{8,1... | collective-permute-start | bytes 4718600 | tf_op jit(solution)/shard_map/ppermute | solution.py:730
  64.2 46.7 %collective-permute-start.5 = (bf16[256,1024]{1,0:T(8,128)(2,1)S(1)}, bf16[256,1024]{1,0:T(8,128)(2,1)S(1)}, u32[]{:S(2)}, u32[]{:S(2)}) collective-permute-start(bf16[256,1024]{1,0:T(8,128)(2,1)S(1)} %copy-done.15), channel_id=1, source_target_pairs={{2,0},{3,1},{0,2},{1,3},{6,4},{7,5},{4,6},{5,7},{10,8},{11,9},{8,1... | collective-permute-start | bytes 1572872 | tf_op jit(solution)/shard_map/ppermute | solution.py:730
  171.6 51.8 %collective-permute-start.10 = (bf16[1024,1024]{1,0:T(8,128)(2,1)}, bf16[1024,1024]{1,0:T(8,128)(2,1)}, u32[]{:S(2)}, u32[]{:S(2)}) collective-permute-start(bf16[1024,1024]{1,0:T(8,128)(2,1)} %get-tuple-element.133), channel_id=1, source_target_pairs={{2,0},{3,1},{0,2},{1,3},{6,4},{7,5},{4,6},{5,7},{10,8},{11,9},{8,1... | collective-permute-start | bytes 6291464 | tf_op jit(solution)/shard_map/ppermute | solution.py:730
  221.7 48.8 %collective-permute-start.9 = (bf16[1024,1024]{1,0:T(8,128)(2,1)}, bf16[1024,1024]{1,0:T(8,128)(2,1)}, u32[]{:S(2)}, u32[]{:S(2)}) collective-permute-start(bf16[1024,1024]{1,0:T(8,128)(2,1)} %get-tuple-element.131), channel_id=1, source_target_pairs={{2,0},{3,1},{0,2},{1,3},{6,4},{7,5},{4,6},{5,7},{10,8},{11,9},{8,1... | collective-permute-start | bytes 6291464 | tf_op jit(solution)/shard_map/ppermute | solution.py:730
  227.9 26.7 %collective-permute-start.12 = (bf16[512,1024]{1,0:T(8,128)(2,1)}, bf16[512,1024]{1,0:T(8,128)(2,1)}, u32[]{:S(2)}, u32[]{:S(2)}) collective-permute-start(bf16[512,1024]{1,0:T(8,128)(2,1)} %get-tuple-element.211), channel_id=1, source_target_pairs={{0,4},{4,0},{8,12},{12,8},{16,20},{20,16},{24,28},{28,24},{1,5},{5... | collective-permute-start | bytes 3145736 | tf_op jit(solution)/shard_map/ppermute | solution.py:841
  254.1 102.2 %collective-permute-start.17 = (bf16[1024,1024]{1,0:T(8,128)(2,1)}, bf16[1024,1024]{1,0:T(8,128)(2,1)}, u32[]{:S(2)}, u32[]{:S(2)}) collective-permute-start(bf16[1024,1024]{1,0:T(8,128)(2,1)} %get-tuple-element.160), channel_id=1, source_target_pairs={{2,0},{3,1},{0,2},{1,3},{6,4},{7,5},{4,6},{5,7},{10,8},{11,9},{8,1... | collective-permute-start | bytes 6291464 | tf_op jit(solution)/shard_map/ppermute | solution.py:730
  274.0 41.0 %collective-permute-start.16 = (bf16[512,1024]{1,0:T(8,128)(2,1)}, bf16[512,1024]{1,0:T(8,128)(2,1)}, u32[]{:S(2)}, u32[]{:S(2)}) collective-permute-start(bf16[512,1024]{1,0:T(8,128)(2,1)} %get-tuple-element.210), channel_id=1, source_target_pairs={{0,4},{4,0},{8,12},{12,8},{16,20},{20,16},{24,28},{28,24},{1,5},{5... | collective-permute-start | bytes 3145736 | tf_op jit(solution)/shard_map/ppermute | solution.py:841
  275.8 125.0 %all-reduce.6.cloned.1.call-start = ((), (), s32[]{:S(2)}) async-start(), calls=%async_computation | async-start | bytes 2097152 | tf_op jit(solution)/shard_map/psum | solution.py:853
  317.7 149.8 %all-reduce.12.cloned.1.call-start = ((), (), s32[]{:S(2)}) async-start(), calls=%async_computation.4 | async-start | bytes 2621440 | tf_op jit(solution)/shard_map/psum | solution.py:853
  317.8 44.5 %collective-permute-start.19 = (bf16[256,1024]{1,0:T(8,128)(2,1)S(1)}, bf16[256,1024]{1,0:T(8,128)(2,1)}, u32[]{:S(2)}, u32[]{:S(2)}) collective-permute-start(bf16[256,1024]{1,0:T(8,128)(2,1)S(1)} %copy-done.25), channel_id=1, source_target_pairs={{2,0},{3,1},{0,2},{1,3},{6,4},{7,5},{4,6},{5,7},{10,8},{11,9},{8,1... | collective-permute-start | bytes 1572872 | tf_op jit(solution)/shard_map/ppermute | solution.py:730
  360.2 44.0 %collective-permute-start.22 = (bf16[512,1024]{1,0:T(8,128)(2,1)}, bf16[512,1024]{1,0:T(8,128)(2,1)}, u32[]{:S(2)}, u32[]{:S(2)}) collective-permute-start(bf16[512,1024]{1,0:T(8,128)(2,1)} %get-tuple-element.207), channel_id=1, source_target_pairs={{0,4},{4,0},{8,12},{12,8},{16,20},{20,16},{24,28},{28,24},{1,5},{5... | collective-permute-start | bytes 3145736 | tf_op jit(solution)/shard_map/ppermute | solution.py:841
  361.9 81.3 %collective-permute-start.21 = (bf16[1024,768]{1,0:T(8,128)(2,1)}, bf16[1024,768]{1,0:T(8,128)(2,1)}, u32[]{:S(2)}, u32[]{:S(2)}) collective-permute-start(bf16[1024,768]{1,0:T(8,128)(2,1)} %outer_product.2), channel_id=1, source_target_pairs={{2,0},{3,1},{0,2},{1,3},{6,4},{7,5},{4,6},{5,7},{10,8},{11,9},{8,1... | collective-permute-start | bytes 4718600 | tf_op jit(solution)/shard_map/ppermute | solution.py:730
  364.3 36.5 %collective-permute-start.23 = (bf16[128,1024]{1,0:T(8,128)(2,1)}, bf16[128,1024]{1,0:T(8,128)(2,1)}, u32[]{:S(2)}, u32[]{:S(2)}) collective-permute-start(bf16[128,1024]{1,0:T(8,128)(2,1)} %get-tuple-element.226), channel_id=1, source_target_pairs={{0,4},{4,0},{8,12},{12,8},{16,20},{20,16},{24,28},{28,24},{1,5},{5... | collective-permute-start | bytes 786440 | tf_op jit(solution)/shard_map/ppermute | solution.py:841
  400.8 44.8 %collective-permute-start.25 = (bf16[512,1024]{1,0:T(8,128)(2,1)}, bf16[512,1024]{1,0:T(8,128)(2,1)}, u32[]{:S(2)}, u32[]{:S(2)}) collective-permute-start(bf16[512,1024]{1,0:T(8,128)(2,1)} %all-reduce.6.cloned.1.call-done), channel_id=1, source_target_pairs={{0,4},{4,0},{8,12},{12,8},{16,20},{20,16},{24,28},{28,24},{1,5},{5... | collective-permute-start | bytes 3145736 | tf_op jit(solution)/shard_map/ppermute | solution.py:857
  406.9 114.0 %all-reduce.10.cloned.1.call-start = ((), (), s32[]{:S(2)}) async-start(), calls=%async_computation.2 | async-start | bytes 1572864 | tf_op jit(solution)/shard_map/psum | solution.py:853
  457.1 37.3 %collective-permute-start.27 = (bf16[1024,1024]{1,0:T(8,128)(2,1)}, bf16[1024,1024]{1,0:T(8,128)(2,1)}, u32[]{:S(2)}, u32[]{:S(2)}) collective-permute-start(bf16[1024,1024]{1,0:T(8,128)(2,1)} %sum_products.12), channel_id=1, source_target_pairs={{1,0},{0,1},{3,2},{2,3},{5,4},{4,5},{7,6},{6,7},{9,8},{8,9},{11,10... | collective-permute-start | bytes 6291464 | tf_op jit(solution)/shard_map/ppermute | solution.py:723
  475.2 24.6 %collective-permute-start.28 = (bf16[1024,1024]{1,0:T(8,128)(2,1)}, bf16[1024,1024]{1,0:T(8,128)(2,1)}, u32[]{:S(2)}, u32[]{:S(2)}) collective-permute-start(bf16[1024,1024]{1,0:T(8,128)(2,1)} %sum_products.13), channel_id=1, source_target_pairs={{1,0},{0,1},{3,2},{2,3},{5,4},{4,5},{7,6},{6,7},{9,8},{8,9},{11,10... | collective-permute-start | bytes 6291464 | tf_op jit(solution)/shard_map/ppermute | solution.py:723
  475.3 47.0 %collective-permute-start.31 = (bf16[512,1024]{1,0:T(8,128)(2,1)}, bf16[512,1024]{1,0:T(8,128)(2,1)}, u32[]{:S(2)}, u32[]{:S(2)}) collective-permute-start(bf16[512,1024]{1,0:T(8,128)(2,1)} %get-tuple-element.199), channel_id=1, source_target_pairs={{0,4},{4,0},{8,12},{12,8},{16,20},{20,16},{24,28},{28,24},{1,5},{5... | collective-permute-start | bytes 3145736 | tf_op jit(solution)/shard_map/ppermute | solution.py:857
  476.8 47.3 %collective-permute-start.32 = (bf16[512,1024]{1,0:T(8,128)(2,1)S(1)}, bf16[512,1024]{1,0:T(8,128)(2,1)}, u32[]{:S(2)}, u32[]{:S(2)}) collective-permute-start(bf16[512,1024]{1,0:T(8,128)(2,1)S(1)} %copy-done.33), channel_id=1, source_target_pairs={{0,4},{4,0},{8,12},{12,8},{16,20},{20,16},{24,28},{28,24},{1,5},{5... | collective-permute-start | bytes 3145736 | tf_op jit(solution)/shard_map/ppermute | solution.py:857
  477.4 52.2 %collective-permute-start.30 = (bf16[128,1024]{1,0:T(8,128)(2,1)S(1)}, bf16[128,1024]{1,0:T(8,128)(2,1)S(1)}, u32[]{:S(2)}, u32[]{:S(2)}) collective-permute-start(bf16[128,1024]{1,0:T(8,128)(2,1)S(1)} %copy-done.40), channel_id=1, source_target_pairs={{0,4},{4,0},{8,12},{12,8},{16,20},{20,16},{24,28},{28,24},{1,5},{5... | collective-permute-start | bytes 786440 | tf_op jit(solution)/shard_map/ppermute | solution.py:857
  520.9 26.1 %collective-permute-start.29 = (bf16[512,768]{1,0:T(8,128)(2,1)}, bf16[512,768]{1,0:T(8,128)(2,1)S(1)}, u32[]{:S(2)}, u32[]{:S(2)}) collective-permute-start(bf16[512,768]{1,0:T(8,128)(2,1)} %all-reduce.10.cloned.1.call-done), channel_id=1, source_target_pairs={{0,4},{4,0},{8,12},{12,8},{16,20},{20,16},{24,28},{28,24},{1,5},{5... | collective-permute-start | bytes 2359304 | tf_op jit(solution)/shard_map/ppermute | solution.py:857
  (64 other events, 545.9 us)
Sparse Core Ops, SparseCore 0:
  33.3 99.3 all-gather.2
  276.0 52.1 all-reduce.7
  330.7 51.0 all-reduce.5
  407.0 60.5 all-reduce.11
  477.5 43.2 all-reduce.9

commit v5 on v4

--- a/solution.py
+++ b/solution.py
@@ -929,8 +929,7 @@
         sums["up"] = swap_sum(sums["up"], *last)
         return [*values, sums["up"][0]]
 
-    across, along = (exchanges(axis, size) for axis, size in (("tensor", tensor_size), ("dp", dp_size)))
-    norm_steps = across + along[1:]
+    exchange = exchanges("tensor", tensor_size) + exchanges("dp", dp_size)
     sums = {}
     moves = [up_swap, up_sum, gate_swap, gate_sum]
     last = list(grad_mixed)
@@ -941,9 +940,6 @@
         grads = None
         for pair in range(count // LANES):
             waits = moves.pop(0)(last) if moves else last
-            if norm_steps:
-                norm_two = norm_steps.pop(0)(after(norm_two, *last))
-                waits = waits + [norm_two]
             grads = attend_back(
                 place,
                 *qkv[index],
@@ -1005,15 +1001,11 @@
     one_parts += [to_seat(part, shift) for shift, part in zip(shifts, one_sent)]
     output = (hidden_one + sum(feed_parts)).astype(BF16)
     (input_grad,), _, norm_one = norm_back(tokens, grad_hidden, gain_first, one_parts, True, 1)
-    for step in norm_steps:
-        norm_two = step(norm_two)
     window = [input_grad, output]
     qkv_halves = swap_sum(qkv_sum, *window)
-    norm_one = after(norm_one, qkv_halves[0])
-    for step in across + along[1:]:
-        norm_one = step(norm_one)
-    norms = along[0](jnp.concatenate([norm_one, norm_two], axis=0))
-    norm_one, norm_two = norms[:2], norms[2:]
+    norms = jnp.concatenate([after(norm_one, qkv_halves[0]), norm_two], axis=0)
+    for step in exchange:
+        norms = step(norms)
     grad_down = whole_sum(down_halves, qkv_halves[0])
     grad_gate = whole_sum(gate_halves, qkv_halves[0])
     out_grad = whole_sum(out_halves, qkv_halves[0])
@@ -1026,10 +1018,10 @@
         grad_gate,
         grad_up,
         grad_down,
-        norm_one[0],
-        norm_one[1],
-        norm_two[0],
-        norm_two[1],
+        norms[0],
+        norms[1],
+        norms[2],
+        norms[3],
     )
 
 

time: 561 us -> 550 us (0.980)
  waiting for transfers between devices: 62.6 us -> 55.6 us
  starting transfers between devices: 37.2 us -> 31.5 us
    ppermute x9 -> x5, waiting for transfers between devices: 19.1 us -> 12.9 us  [exchanges(): lax.ppermute(value, axis, pairs)]
    ppermute x9 -> x5, starting transfers between devices: 12.1 us -> 6.46 us  [exchanges(): lax.ppermute(value, axis, pairs)]
    unnamed x92 -> x90, local copies, waits for them, and re-layouts: 14.2 us -> 14.1 us
  transfers between devices with their start and end apart: 43 -> 39, of which waited for: 16 -> 13; matrix products, arithmetic and copies ran while one was open for 9% -> 9% of each run, Pallas kernels for 60% -> 62%
where the time goes in v5:
time: 550 us; the launch traced here: 544 us
  Pallas kernels  371 us (67%)
  waiting for transfers between devices  55.6 us (10%)
  other arithmetic  51.6 us (9%)
  starting transfers between devices  31.5 us (6%)
  local copies, waits for them, and re-layouts  19.2 us (3%)
  between operations  14.8 us (3%)
    pallas_call x4, Pallas kernels, attend_back(): pl.pallas_call(functools.partial(attend_back_kernel, chunk=chunk), grid_s...  109 us
    pallas_call x2, Pallas kernels, feed(): pl.pallas_call(functools.partial(feed_kernel, counts=(len(rows), len(targ...  73.7 us
    pallas_call x8, Pallas kernels, sum_products(): pl.pallas_call(functools.partial(sum_kernel, places=places, dims=tuple(di...  63.4 us
    pallas_call x2, Pallas kernels, attend(): pl.pallas_call(functools.partial(attend_kernel, chunk=chunk), grid_spec=p...  56.9 us
    pallas_call x3, Pallas kernels, norm_back(): pl.pallas_call(lambda *refs, held=len(held): norm_back_kernel(*refs[:3 +...  17.8 us
    psum x4, waiting for transfers between devices, sum_half(): return lax.psum(value, 'dp', axis_index_groups=groups)  16.4 us
    convert_element_type x5, other arithmetic, total(): sum((half(piece, which).astype(F32) for piece in pieces)).astype(BF16)  15.7 us
    pallas_call x2, Pallas kernels, outer(): pl.pallas_call(functools.partial(outer_kernel, count=len(pieces)), grid=(...  14.6 us
  transfers between devices with their start and end apart: 39, of which 13 were waited for; matrix products, arithmetic and copies ran while one was open for 9% of the time, Pallas kernels for 62%

profile of v5, /device:TPU:0, one launch (start us, length us, event | category | flops | bytes accessed | tf_op | source)
XLA Modules:
  0.0 544.1 jit_solution(10661380783700613583)
XLA Ops:
  23.7 6.5 %project_rope.2 = (bf16[2048,256]{1,0:T(8,128)(2,1)S(1)}, bf16[2048,256]{1,0:T(8,128)(2,1)S(1)}, bf16[2048,256]{1,0:T(8,128)(2,1)S(1)}) custom-call(bf16[512,1024]{1,0:T(8,128)(2,1)S(1)} %copy-done.5, bf16[512,1024]{1,0:T(8,128)(2,1)S(1)} %copy-done.6, bf16[512,1024]{1,0:T(8,128)(2,1)} %collective-permute-done.refs_2_, ...), custom_call_target="tpu_custom_call" | custom-call | flops 32212254 | bytes 89128 | tf_op jit(solution)/shard_map/project_rope/pallas_call | solution.py:105
  35.8 28.3 %attention_forward.2 = (bf16[2048,256]{1,0:T(8,128)(2,1)}, f32[2,8,2048]{2,1,0:T(8,128)}) custom-call(s32[2]{0:T(128)} %pad_add_fusion.place_ref, bf16[2048,256]{1,0:T(8,128)(2,1)} %copy-done.9, bf16[2048,256]{1,0:T(8,128)(2,1)} %copy-done.10, bf16[2048,256]{1,0:T(8,128)(2,1)} %copy-done.11), custom_call_target="tpu_custom_call" | custom-call | flops 171798688 | bytes 41943 | tf_op jit(solution)/shard_map/attention_forward/pallas_call | solution.py:184
  71.5 7.9 %project_rope.3 = (bf16[2048,256]{1,0:T(8,128)(2,1)S(1)}, bf16[2048,256]{1,0:T(8,128)(2,1)S(1)}, bf16[2048,256]{1,0:T(8,128)(2,1)S(1)}) custom-call(bf16[512,1024]{1,0:T(8,128)(2,1)S(1)} %copy-done.5, bf16[512,1024]{1,0:T(8,128)(2,1)S(1)} %copy-done.7, bf16[512,1024]{1,0:T(8,128)(2,1)} %collective-permute-done.refs_2_, ...), custom_call_target="tpu_custom_call" | custom-call | flops 32212254 | bytes 89128 | tf_op jit(solution)/shard_map/project_rope/pallas_call | solution.py:105
  82.3 28.5 %attention_forward.3 = (bf16[2048,256]{1,0:T(8,128)(2,1)}, f32[2,8,2048]{2,1,0:T(8,128)}) custom-call(s32[2]{0:T(128)} %pad_add_fusion.place_ref, bf16[2048,256]{1,0:T(8,128)(2,1)} %copy-done.12, bf16[2048,256]{1,0:T(8,128)(2,1)} %copy-done.13, bf16[2048,256]{1,0:T(8,128)(2,1)} %copy-done.14), custom_call_target="tpu_custom_call" | custom-call | flops 171798688 | bytes 41943 | tf_op jit(solution)/shard_map/attention_forward/pallas_call | solution.py:184
  135.0 36.7 %feed_forward.2 = (bf16[2048,1024]{1,0:T(8,128)(2,1)}, bf16[2048,1024]{1,0:T(8,128)(2,1)}, bf16[2048,1024]{1,0:T(8,128)(2,1)}, bf16[1024,1024]{1,0:T(8,128)(2,1)...) custom-call(bf16[512,1024]{1,0:T(8,128)(2,1)} %get-tuple-element.131.refs_0_, ...), custom_call_target="tpu_custom_call" | custom-call | flops 257698032 | bytes 335544 | tf_op jit(solution)/shard_map/feed_forward/pallas_call | solution.py:371
  171.9 37.0 %feed_forward.3 = (bf16[2048,1024]{1,0:T(8,128)(2,1)}, bf16[2048,1024]{1,0:T(8,128)(2,1)}, bf16[2048,1024]{1,0:T(8,128)(2,1)}, bf16[1024,1024]{1,0:T(8,128)(2,1)...) custom-call(bf16[512,1024]{1,0:T(8,128)(2,1)} %get-tuple-element.131.refs_0_, ...), custom_call_target="tpu_custom_call" | custom-call | flops 257698032 | bytes 335544 | tf_op jit(solution)/shard_map/feed_forward/pallas_call | solution.py:371
  208.9 12.5 %sum_products.10 = bf16[1024,1024]{1,0:T(8,128)(2,1)} custom-call(bf16[2048,1024]{1,0:T(8,128)(2,1)} %get-tuple-element.137.refs_0_, bf16[8,384,1024]{2,1,0:T(8,128)(2,1)} %bitcast.13, bf16[2048,1024]{1,0:T(8,128)(2,1)} %get-tuple-element.130.refs_2_, bf16[8,384,1024]{2,1,0:T(8,128)(2,1)} %bitcast.14, bf16[2048,1024]{1,0:T(8,128)(2,1)} %get-tuple-element.132.refs_4_, ...), custom_call_target="tpu_custom_call" | custom-call | flops 85899344 | bytes 209715 | tf_op jit(solution)/shard_map/sum_products/pallas_call | solution.py:450
  229.6 12.9 %sum_products.11.refs_3_ = f32[1024,1024]{1,0:T(8,128)} custom-call(bf16[2048,1024]{1,0:T(8,128)(2,1)} %get-tuple-element.137.refs_0_, bf16[8,384,1024]{2,1,0:T(8,128)(2,1)} %bitcast.15, bf16[2048,1024]{1,0:T(8,128)(2,1)} %get-tuple-element.130.refs_2_, bf16[8,384,1024]{2,1,0:T(8,128)(2,1)} %bitcast.16, bf16[2048,1024]{1,0:T(8,128)(2,1)} %get-tuple-element.132.refs_4_, ...), custom_call_target="tpu_custom_call" | custom-call | flops 85899344 | bytes 209715 | tf_op jit(solution)/shard_map/sum_products/pallas_call | solution.py:450
  257.7 8.2 %branch_backward.1 = (bf16[2048,256]{1,0:T(8,128)(2,1)S(1)}, bf16[2048,256]{1,0:T(8,128)(2,1)S(1)}, bf16[256,1024]{1,0:T(8,128)(2,1)S(1)}, bf16[256,1024]{1,0:T(8,128)(2,1)S(1)}) custom-call(bf16[512,1024]{1,0:T(8,128)(2,1)S(1)} %copy-done.21, bf16[512,1024]{1,0:T(8,128)(2,1)} %get-tuple-element.140.refs_1_, ...), custom_call_target="tpu_custom_call" | custom-call | flops 42949672 | bytes 125829 | tf_op jit(solution)/shard_map/branch_backward/pallas_call | solution.py:522
  275.9 27.5 %attention_backward.4.rest_0_ = bf16[3,2048,256]{2,1,0:T(8,128)(2,1)} custom-call(s32[2]{0:T(128)} %pad_add_fusion.place_ref, bf16[2048,256]{1,0:T(8,128)(2,1)} %copy-done.12, bf16[2048,256]{1,0:T(8,128)(2,1)} %copy-done.13, bf16[2048,256]{1,0:T(8,128)(2,1)} %copy-done.14, bf16[2048,256]{1,0:T(8,128)(2,1)} %get-tuple-element.120.refs_2_.refs_6_.out_ref, ...), custom_call_target="tpu_custom_call" | custom-call | flops 150323856 | bytes 41943 | tf_op jit(solution)/shard_map/attention_backward/pallas_call | solution.py:283
  307.9 27.2 %attention_backward.5.refs_4_.refs_0_.refs_2_ = bf16[3,2048,256]{2,1,0:T(8,128)(2,1)} custom-call(s32[2]{0:T(128)} %pad_add_fusion.place_ref, bf16[2048,256]{1,0:T(8,128)(2,1)} %copy-done.12, bf16[2048,256]{1,0:T(8,128)(2,1)} %copy-done.13, bf16[2048,256]{1,0:T(8,128)(2,1)} %copy-done.14, ...), custom_call_target="tpu_custom_call", output_to_operand_aliasing={{}: (11, {})} | custom-call | flops 150323856 | bytes 41943 | tf_op jit(solution)/shard_map/attention_backward/pallas_call | solution.py:283
  337.0 7.6 %outer_product.2 = bf16[1024,768]{1,0:T(8,128)(2,1)} custom-call(bf16[512,1024]{1,0:T(8,128)(2,1)S(1)} %copy-done.5, bf16[512,1024]{1,0:T(8,128)(2,1)S(1)} %copy-done.8, bf16[512,1024]{1,0:T(8,128)(2,1)} %collective-permute-done.refs_2_, bf16[512,1024]{1,0:T(8,128)(2,1)} %collective-permute-done.1.refs_3_, bf16[3,2048,256]{2,1,0:T(8,128)(2,1)S(1)} %copy-done.1), custom_call_target="tpu_custom_call" | custom-call | flops 32212254 | bytes 89128 | tf_op jit(solution)/shard_map/outer_product/pallas_call | solution.py:485
  353.1 27.3 %attention_backward.6.rest_0_ = bf16[3,2048,256]{2,1,0:T(8,128)(2,1)} custom-call(s32[2]{0:T(128)} %pad_add_fusion.place_ref, bf16[2048,256]{1,0:T(8,128)(2,1)} %copy-done.9, bf16[2048,256]{1,0:T(8,128)(2,1)} %copy-done.10, bf16[2048,256]{1,0:T(8,128)(2,1)} %copy-done.11, bf16[2048,256]{1,0:T(8,128)(2,1)} %get-tuple-element.113.refs_0_.refs_7_.out_ref, ...), custom_call_target="tpu_custom_call" | custom-call | flops 150323856 | bytes 41943 | tf_op jit(solution)/shard_map/attention_backward/pallas_call | solution.py:283
  387.9 27.4 %attention_backward.7.refs_4_.refs_6_.refs_8_.refs_10_ = bf16[3,2048,256]{2,1,0:T(8,128)(2,1)} custom-call(s32[2]{0:T(128)} %pad_add_fusion.place_ref, bf16[2048,256]{1,0:T(8,128)(2,1)} %copy-done.9, bf16[2048,256]{1,0:T(8,128)(2,1)} %copy-done.10, bf16[2048,256]{1,0:T(8,128)(2,1)} %copy-done.11, ...), custom_call_target="tpu_custom_call", output_to_operand_aliasing={{}: (11, {})} | custom-call | flops 150323856 | bytes 41943 | tf_op jit(solution)/shard_map/attention_backward/pallas_call | solution.py:283
  417.2 7.0 %outer_product.3 = bf16[1024,768]{1,0:T(8,128)(2,1)S(1)} custom-call(bf16[512,1024]{1,0:T(8,128)(2,1)S(1)} %copy-done.5, bf16[512,1024]{1,0:T(8,128)(2,1)S(1)} %copy-done.8, bf16[512,1024]{1,0:T(8,128)(2,1)} %collective-permute-done.refs_2_, bf16[512,1024]{1,0:T(8,128)(2,1)} %collective-permute-done.1.refs_3_, bf16[3,2048,256]{2,1,0:T(8,128)(2,1)S(1)} %copy-done), custom_call_target="tpu_custom_call" | custom-call | flops 32212254 | bytes 89128 | tf_op jit(solution)/shard_map/outer_product/pallas_call | solution.py:485
  430.5 7.7 %sum_products.12 = bf16[1024,1024]{1,0:T(8,128)(2,1)} custom-call(bf16[2048,1024]{1,0:T(8,128)(2,1)} %get-tuple-element.180.refs_0_, bf16[8,384,1024]{2,1,0:T(8,128)(2,1)} %bitcast.17, bf16[2048,1024]{1,0:T(8,128)(2,1)} %get-tuple-element.175.refs_2_, bf16[1024,1024]{1,0:T(8,128)(2,1)} %refs_3_.3), custom_call_target="tpu_custom_call" | custom-call | flops 42949672 | bytes 125829 | tf_op jit(solution)/shard_map/sum_products/pallas_call | solution.py:450
  438.2 7.1 %collective-permute-done.22 = bf16[512,768]{1,0:T(8,128)(2,1)S(1)} collective-permute-done((bf16[512,768]{1,0:T(8,128)(2,1)S(1)}, bf16[512,768]{1,0:T(8,128)(2,1)S(1)}, u32[]{:S(2)}, u32[]{:S(2)}) %collective-permute-start.22) | collective-permute-done | bytes 786464 | tf_op jit(solution)/shard_map/ppermute | solution.py:841
  448.3 6.6 %sum_products.13 = bf16[1024,1024]{1,0:T(8,128)(2,1)} custom-call(bf16[3,2048,256]{2,1,0:T(8,128)(2,1)} %attention_backward.5.refs_4_.refs_0_.refs_2_, bf16[1024,768]{1,0:T(8,128)(2,1)} %collective-permute-done.3.refs_4_.refs_1_.refs_3_.refs_5_, bf16[3,2048,256]{2,1,0:T(8,128)(2,1)} %attention_backward.5.refs_4_.refs_0_.refs_2_, ...), custom_call_target="tpu_custom_call" | custom-call | flops 32212254 | bytes 104857 | tf_op jit(solution)/shard_map/sum_products/pallas_call | solution.py:450
  458.6 7.9 %sum_products.14 = f32[1024,1024]{1,0:T(8,128)} custom-call(bf16[2048,1024]{1,0:T(8,128)(2,1)} %get-tuple-element.180.refs_0_, bf16[8,384,1024]{2,1,0:T(8,128)(2,1)} %bitcast.18, bf16[2048,1024]{1,0:T(8,128)(2,1)} %get-tuple-element.175.refs_2_, bf16[1024,1024]{1,0:T(8,128)(2,1)} %refs_3_.3), custom_call_target="tpu_custom_call" | custom-call | flops 42949672 | bytes 125829 | tf_op jit(solution)/shard_map/sum_products/pallas_call | solution.py:450
  466.5 7.6 %sum_products.15.refs_3_ = f32[1024,1024]{1,0:T(8,128)} custom-call(bf16[3,2048,256]{2,1,0:T(8,128)(2,1)} %attention_backward.5.refs_4_.refs_0_.refs_2_, bf16[1024,768]{1,0:T(8,128)(2,1)} %collective-permute-done.3.refs_4_.refs_1_.refs_3_.refs_5_, bf16[3,2048,256]{2,1,0:T(8,128)(2,1)} %attention_backward.5.refs_4_.refs_0_.refs_2_, ...), custom_call_target="tpu_custom_call" | custom-call | flops 32212254 | bytes 104857 | tf_op jit(solution)/shard_map/sum_products/pallas_call | solution.py:450
  474.1 5.5 %add_convert_fusion = bf16[1024,1024]{1,0:T(8,128)(2,1)} fusion(f32[1024,1024]{1,0:T(8,128)S(1)} %copy-done.26, f32[1024,1024]{1,0:T(8,128)} %sum_products.14, bf16[1024,1024]{1,0:T(8,128)(2,1)} %collective-permute-done.23), kind=kLoop, calls=%fused_computation | loop fusion | flops 4194304 | bytes 12582912 | tf_op jit(solution)/shard_map/convert_element_type | solution.py:1002
  479.6 8.0 %layer_norm_backward.5 = (bf16[1024,1024]{1,0:T(8,128)(2,1)}, f32[2,1024]{1,0:T(2,128)}) custom-call(bf16[1024,1024]{1,0:T(8,128)(2,1)} %refs_0_.7, f32[1024,1024]{1,0:T(8,128)} %get-tuple-element.181.refs_1_, f32[1,1024]{1,0:T(1,128)} %bitcast.25, f32[1024,1024]{1,0:T(8,128)} %sum_products.15.refs_3_, bf16[1024,1024]{1,0:T(8,128)(2,1)} %collective-permute-done.24.refs_4_), custom_call_target="tpu_custom_call" | custom-call | flops 314572 | bytes 167772 | tf_op jit(solution)/shard_map/layer_norm_backward/pallas_call | solution.py:637
  487.6 13.0 %all-reduce.10.cloned.1.call-done = bf16[512,768]{1,0:T(8,128)(2,1)} async-done(((bf16[512,768]{1,0:T(8,128)(2,1)}), bf16[512,768]{1,0:T(8,128)(2,1)}) %all-reduce.10.cloned.1.call-update) | async-done | bytes 786448 | tf_op jit(solution)/shard_map/psum | solution.py:853
  517.0 9.0 %collective-permute-done.31 = f32[4,1024]{1,0:T(4,128)S(1)} collective-permute-done((f32[4,1024]{1,0:T(4,128)S(1)}, f32[4,1024]{1,0:T(4,128)S(1)}, u32[]{:S(2)}, u32[]{:S(2)}) %collective-permute-start.31) | collective-permute-done | bytes 16416 | tf_op jit(solution)/shard_map/ppermute | solution.py:686
  (219 shorter events, 154.5 us)
Async XLA Ops:
  7.2 126.9 %all-gather.3.cloned.1.call-start = ((), (), s32[]{:S(2)}) async-start(), calls=%async_computation.3 | async-start | bytes 7077888 | tf_op jit(solution)/shard_map/all_gather | solution.py:758
  33.2 319.9 %all-reduce.8.cloned.1.call-start = ((), (), s32[]{:S(2)}) async-start(), calls=%async_computation.1 | async-start | bytes 2097152 | tf_op jit(solution)/shard_map/psum | solution.py:853
  33.8 48.6 %collective-permute-start.4 = (bf16[1024,1024]{1,0:T(8,128)(2,1)}, bf16[1024,1024]{1,0:T(8,128)(2,1)}, u32[]{:S(2)}, u32[]{:S(2)}) collective-permute-start(bf16[1024,1024]{1,0:T(8,128)(2,1)} %refs_1_.7), channel_id=1, source_target_pairs={{1,0},{0,1},{3,2},{2,3},{5,4},{4,5},{7,6},{6,7},{9,8},{8,9},{11,10... | collective-permute-start | bytes 6291464 | tf_op jit(solution)/shard_map/ppermute | solution.py:723
  33.9 37.5 %collective-permute-start.3 = (bf16[1024,768]{1,0:T(8,128)(2,1)}, bf16[1024,768]{1,0:T(8,128)(2,1)}, u32[]{:S(2)}, u32[]{:S(2)}) collective-permute-start(bf16[1024,768]{1,0:T(8,128)(2,1)} %copy-done.4), channel_id=1, source_target_pairs={{2,0},{3,1},{0,2},{1,3},{6,4},{7,5},{4,6},{5,7},{10,8},{11,9},{8,1... | collective-permute-start | bytes 4718600 | tf_op jit(solution)/shard_map/ppermute | solution.py:730
  64.2 46.7 %collective-permute-start.5 = (bf16[256,1024]{1,0:T(8,128)(2,1)S(1)}, bf16[256,1024]{1,0:T(8,128)(2,1)S(1)}, u32[]{:S(2)}, u32[]{:S(2)}) collective-permute-start(bf16[256,1024]{1,0:T(8,128)(2,1)S(1)} %copy-done.15), channel_id=1, source_target_pairs={{2,0},{3,1},{0,2},{1,3},{6,4},{7,5},{4,6},{5,7},{10,8},{11,9},{8,1... | collective-permute-start | bytes 1572872 | tf_op jit(solution)/shard_map/ppermute | solution.py:730
  171.7 51.8 %collective-permute-start.10 = (bf16[1024,1024]{1,0:T(8,128)(2,1)}, bf16[1024,1024]{1,0:T(8,128)(2,1)}, u32[]{:S(2)}, u32[]{:S(2)}) collective-permute-start(bf16[1024,1024]{1,0:T(8,128)(2,1)} %get-tuple-element.129), channel_id=1, source_target_pairs={{2,0},{3,1},{0,2},{1,3},{6,4},{7,5},{4,6},{5,7},{10,8},{11,9},{8,1... | collective-permute-start | bytes 6291464 | tf_op jit(solution)/shard_map/ppermute | solution.py:730
  221.8 48.8 %collective-permute-start.9 = (bf16[1024,1024]{1,0:T(8,128)(2,1)}, bf16[1024,1024]{1,0:T(8,128)(2,1)}, u32[]{:S(2)}, u32[]{:S(2)}) collective-permute-start(bf16[1024,1024]{1,0:T(8,128)(2,1)} %get-tuple-element.127), channel_id=1, source_target_pairs={{2,0},{3,1},{0,2},{1,3},{6,4},{7,5},{4,6},{5,7},{10,8},{11,9},{8,1... | collective-permute-start | bytes 6291464 | tf_op jit(solution)/shard_map/ppermute | solution.py:730
  228.0 26.8 %collective-permute-start.12 = (bf16[512,1024]{1,0:T(8,128)(2,1)}, bf16[512,1024]{1,0:T(8,128)(2,1)}, u32[]{:S(2)}, u32[]{:S(2)}) collective-permute-start(bf16[512,1024]{1,0:T(8,128)(2,1)} %get-tuple-element.203), channel_id=1, source_target_pairs={{0,4},{4,0},{8,12},{12,8},{16,20},{20,16},{24,28},{28,24},{1,5},{5... | collective-permute-start | bytes 3145736 | tf_op jit(solution)/shard_map/ppermute | solution.py:841
  254.3 90.4 %collective-permute-start.16 = (bf16[1024,1024]{1,0:T(8,128)(2,1)}, bf16[1024,1024]{1,0:T(8,128)(2,1)}, u32[]{:S(2)}, u32[]{:S(2)}) collective-permute-start(bf16[1024,1024]{1,0:T(8,128)(2,1)} %get-tuple-element.153), channel_id=1, source_target_pairs={{2,0},{3,1},{0,2},{1,3},{6,4},{7,5},{4,6},{5,7},{10,8},{11,9},{8,1... | collective-permute-start | bytes 6291464 | tf_op jit(solution)/shard_map/ppermute | solution.py:730
  274.1 29.4 %collective-permute-start.15 = (bf16[512,1024]{1,0:T(8,128)(2,1)}, bf16[512,1024]{1,0:T(8,128)(2,1)}, u32[]{:S(2)}, u32[]{:S(2)}) collective-permute-start(bf16[512,1024]{1,0:T(8,128)(2,1)} %get-tuple-element.202), channel_id=1, source_target_pairs={{0,4},{4,0},{8,12},{12,8},{16,20},{20,16},{24,28},{28,24},{1,5},{5... | collective-permute-start | bytes 3145736 | tf_op jit(solution)/shard_map/ppermute | solution.py:841
  275.9 106.1 %all-reduce.6.cloned.1.call-start = ((), (), s32[]{:S(2)}) async-start(), calls=%async_computation | async-start | bytes 2097152 | tf_op jit(solution)/shard_map/psum | solution.py:853
  306.2 141.0 %all-reduce.12.cloned.1.call-start = ((), (), s32[]{:S(2)}) async-start(), calls=%async_computation.4 | async-start | bytes 2621440 | tf_op jit(solution)/shard_map/psum | solution.py:853
  306.2 43.2 %collective-permute-start.17 = (bf16[256,1024]{1,0:T(8,128)(2,1)S(1)}, bf16[256,1024]{1,0:T(8,128)(2,1)}, u32[]{:S(2)}, u32[]{:S(2)}) collective-permute-start(bf16[256,1024]{1,0:T(8,128)(2,1)S(1)} %copy-done.25), channel_id=1, source_target_pairs={{2,0},{3,1},{0,2},{1,3},{6,4},{7,5},{4,6},{5,7},{10,8},{11,9},{8,1... | collective-permute-start | bytes 1572872 | tf_op jit(solution)/shard_map/ppermute | solution.py:730
  348.6 36.6 %collective-permute-start.19 = (bf16[512,1024]{1,0:T(8,128)(2,1)}, bf16[512,1024]{1,0:T(8,128)(2,1)}, u32[]{:S(2)}, u32[]{:S(2)}) collective-permute-start(bf16[512,1024]{1,0:T(8,128)(2,1)} %get-tuple-element.199), channel_id=1, source_target_pairs={{0,4},{4,0},{8,12},{12,8},{16,20},{20,16},{24,28},{28,24},{1,5},{5... | collective-permute-start | bytes 3145736 | tf_op jit(solution)/shard_map/ppermute | solution.py:841
  349.0 75.1 %collective-permute-start.18 = (bf16[1024,768]{1,0:T(8,128)(2,1)}, bf16[1024,768]{1,0:T(8,128)(2,1)}, u32[]{:S(2)}, u32[]{:S(2)}) collective-permute-start(bf16[1024,768]{1,0:T(8,128)(2,1)} %outer_product.2), channel_id=1, source_target_pairs={{2,0},{3,1},{0,2},{1,3},{6,4},{7,5},{4,6},{5,7},{10,8},{11,9},{8,1... | collective-permute-start | bytes 4718600 | tf_op jit(solution)/shard_map/ppermute | solution.py:730
  351.4 29.0 %collective-permute-start.20 = (bf16[128,1024]{1,0:T(8,128)(2,1)}, bf16[128,1024]{1,0:T(8,128)(2,1)}, u32[]{:S(2)}, u32[]{:S(2)}) collective-permute-start(bf16[128,1024]{1,0:T(8,128)(2,1)} %get-tuple-element.218), channel_id=1, source_target_pairs={{0,4},{4,0},{8,12},{12,8},{16,20},{20,16},{24,28},{28,24},{1,5},{5... | collective-permute-start | bytes 786440 | tf_op jit(solution)/shard_map/ppermute | solution.py:841
  382.0 44.7 %collective-permute-start.21 = (bf16[512,1024]{1,0:T(8,128)(2,1)}, bf16[512,1024]{1,0:T(8,128)(2,1)}, u32[]{:S(2)}, u32[]{:S(2)}) collective-permute-start(bf16[512,1024]{1,0:T(8,128)(2,1)} %all-reduce.6.cloned.1.call-done), channel_id=1, source_target_pairs={{0,4},{4,0},{8,12},{12,8},{16,20},{20,16},{24,28},{28,24},{1,5},{5... | collective-permute-start | bytes 3145736 | tf_op jit(solution)/shard_map/ppermute | solution.py:857
  387.8 112.7 %all-reduce.10.cloned.1.call-start = ((), (), s32[]{:S(2)}) async-start(), calls=%async_computation.2 | async-start | bytes 1572864 | tf_op jit(solution)/shard_map/psum | solution.py:853
  438.2 35.9 %collective-permute-start.23 = (bf16[1024,1024]{1,0:T(8,128)(2,1)}, bf16[1024,1024]{1,0:T(8,128)(2,1)}, u32[]{:S(2)}, u32[]{:S(2)}) collective-permute-start(bf16[1024,1024]{1,0:T(8,128)(2,1)} %sum_products.12), channel_id=1, source_target_pairs={{1,0},{0,1},{3,2},{2,3},{5,4},{4,5},{7,6},{6,7},{9,8},{8,9},{11,10... | collective-permute-start | bytes 6291464 | tf_op jit(solution)/shard_map/ppermute | solution.py:723
  454.8 24.7 %collective-permute-start.24 = (bf16[1024,1024]{1,0:T(8,128)(2,1)}, bf16[1024,1024]{1,0:T(8,128)(2,1)}, u32[]{:S(2)}, u32[]{:S(2)}) collective-permute-start(bf16[1024,1024]{1,0:T(8,128)(2,1)} %sum_products.13), channel_id=1, source_target_pairs={{1,0},{0,1},{3,2},{2,3},{5,4},{4,5},{7,6},{6,7},{9,8},{8,9},{11,10... | collective-permute-start | bytes 6291464 | tf_op jit(solution)/shard_map/ppermute | solution.py:723
  454.9 47.1 %collective-permute-start.27 = (bf16[512,1024]{1,0:T(8,128)(2,1)}, bf16[512,1024]{1,0:T(8,128)(2,1)}, u32[]{:S(2)}, u32[]{:S(2)}) collective-permute-start(bf16[512,1024]{1,0:T(8,128)(2,1)} %get-tuple-element.189), channel_id=1, source_target_pairs={{0,4},{4,0},{8,12},{12,8},{16,20},{20,16},{24,28},{28,24},{1,5},{5... | collective-permute-start | bytes 3145736 | tf_op jit(solution)/shard_map/ppermute | solution.py:857
  456.5 47.3 %collective-permute-start.28 = (bf16[512,1024]{1,0:T(8,128)(2,1)S(1)}, bf16[512,1024]{1,0:T(8,128)(2,1)}, u32[]{:S(2)}, u32[]{:S(2)}) collective-permute-start(bf16[512,1024]{1,0:T(8,128)(2,1)S(1)} %copy-done.33), channel_id=1, source_target_pairs={{0,4},{4,0},{8,12},{12,8},{16,20},{20,16},{24,28},{28,24},{1,5},{5... | collective-permute-start | bytes 3145736 | tf_op jit(solution)/shard_map/ppermute | solution.py:857
  457.1 52.2 %collective-permute-start.26 = (bf16[128,1024]{1,0:T(8,128)(2,1)S(1)}, bf16[128,1024]{1,0:T(8,128)(2,1)S(1)}, u32[]{:S(2)}, u32[]{:S(2)}) collective-permute-start(bf16[128,1024]{1,0:T(8,128)(2,1)S(1)} %copy-done.39), channel_id=1, source_target_pairs={{0,4},{4,0},{8,12},{12,8},{16,20},{20,16},{24,28},{28,24},{1,5},{5... | collective-permute-start | bytes 786440 | tf_op jit(solution)/shard_map/ppermute | solution.py:857
  500.5 34.7 %collective-permute-start.25 = (bf16[512,768]{1,0:T(8,128)(2,1)}, bf16[512,768]{1,0:T(8,128)(2,1)S(1)}, u32[]{:S(2)}, u32[]{:S(2)}) collective-permute-start(bf16[512,768]{1,0:T(8,128)(2,1)} %all-reduce.10.cloned.1.call-done), channel_id=1, source_target_pairs={{0,4},{4,0},{8,12},{12,8},{16,20},{20,16},{24,28},{28,24},{1,5},{5... | collective-permute-start | bytes 2359304 | tf_op jit(solution)/shard_map/ppermute | solution.py:857
  (59 other events, 526.9 us)
Sparse Core Ops, SparseCore 0:
  33.3 99.3 all-gather.2
  276.0 52.1 all-reduce.7
  330.7 51.1 all-reduce.5
  387.9 59.2 all-reduce.11
  457.2 43.3 all-reduce.9

commit v6 on v5

--- a/solution.py
+++ b/solution.py
@@ -17,7 +17,7 @@
 BF16 = jnp.bfloat16
 F32 = jnp.float32
 MIB = 1 << 20
-COST_SHARE = 0.01
+COST_SHARE = 0.1
 PIECES = 2
 
 
@@ -927,9 +927,11 @@
         values = add_half(sums["gate"], *last), add_half(sums["out"], *last)
         sums["gate"], sums["out"] = sum_half(values, 2)
         sums["up"] = swap_sum(sums["up"], *last)
+        sums["down"] = swap_sum(sums["down"], *last)
         return [*values, sums["up"][0]]
 
-    exchange = exchanges("tensor", tensor_size) + exchanges("dp", dp_size)
+    along = exchanges("dp", dp_size)
+    exchange = exchanges("tensor", tensor_size) + along[1:] + along[:1]
     sums = {}
     moves = [up_swap, up_sum, gate_swap, gate_sum]
     last = list(grad_mixed)
@@ -976,8 +978,7 @@
 
     qkv_half, marks = swap_half(send_to_owner(qkv_grads) + [qkv_grads[0]])
     grad_up = whole_sum(sums["up"], *marks)
-    down_halves = swap_sum(sums["down"], *marks)
-    feed_terms[0] = (after(feed_terms[0][0], grad_up, down_halves[0]), *feed_terms[0][1:])
+    feed_terms[0] = (after(feed_terms[0][0], grad_up), *feed_terms[0][1:])
     one_terms = [
         (grad_qkv[index], part, weight, part, 1)
         for index, weight in enumerate(qkv_weights)
@@ -993,7 +994,8 @@
     gate_halves = swap_sum(sums["gate"], *feed_sent)
     out_halves = swap_sum(sums["out"], *feed_sent)
     qkv_sum = sum_half(after(qkv_half, gate_halves[0], out_halves[0]), 3)
-    one_terms = later(one_terms, qkv_half, gate_halves[0])
+    grad_down = whole_sum(sums["down"], *feed_sent)
+    one_terms = later(one_terms, qkv_half, gate_halves[0], grad_down)
     one_sent = [sum_products(one_terms, shift * held, held, BF16) for shift in shifts]
     feed_parts = [sum_products(later(feed_terms, *one_sent), 0, held)]
     one_parts = [sum_products(later(one_terms, feed_parts[0]), 0, held)]
@@ -1006,7 +1008,6 @@
     norms = jnp.concatenate([after(norm_one, qkv_halves[0]), norm_two], axis=0)
     for step in exchange:
         norms = step(norms)
-    grad_down = whole_sum(down_halves, qkv_halves[0])
     grad_gate = whole_sum(gate_halves, qkv_halves[0])
     out_grad = whole_sum(out_halves, qkv_halves[0])
     qkv_grad = whole_sum(qkv_halves)

time: 550 us -> 542 us (0.985)
  waiting for transfers between devices: 55.6 us -> 48.2 us
  transfers between devices with their start and end apart: 39 -> 39, of which waited for: 13 -> 12; matrix products, arithmetic and copies ran while one was open for 9% -> 10% of each run, Pallas kernels for 62% -> 62%
where the time goes in v6:
time: 542 us; the launch traced here: 536 us
  Pallas kernels  371 us (68%)
  other arithmetic  52 us (10%)
  waiting for transfers between devices  48.2 us (9%)
  starting transfers between devices  30.9 us (6%)
  local copies, waits for them, and re-layouts  19.2 us (4%)
  between operations  14.7 us (3%)
    pallas_call x4, Pallas kernels, attend_back(): pl.pallas_call(functools.partial(attend_back_kernel, chunk=chunk), grid_s...  109 us
    pallas_call x2, Pallas kernels, feed(): pl.pallas_call(functools.partial(feed_kernel, counts=(len(rows), len(targ...  73.7 us
    pallas_call x8, Pallas kernels, sum_products(): pl.pallas_call(functools.partial(sum_kernel, places=places, dims=tuple(di...  63.5 us
    pallas_call x2, Pallas kernels, attend(): pl.pallas_call(functools.partial(attend_kernel, chunk=chunk), grid_spec=p...  57 us
    pallas_call x3, Pallas kernels, norm_back(): pl.pallas_call(lambda *refs, held=len(held): norm_back_kernel(*refs[:3 +...  17.6 us
    psum x4, waiting for transfers between devices, sum_half(): return lax.psum(value, 'dp', axis_index_groups=groups)  16.9 us
    convert_element_type x5, other arithmetic, total(): sum((half(piece, which).astype(F32) for piece in pieces)).astype(BF16)  15.7 us
    pallas_call x2, Pallas kernels, outer(): pl.pallas_call(functools.partial(outer_kernel, count=len(pieces)), grid=(...  14.6 us
  transfers between devices with their start and end apart: 39, of which 12 were waited for; matrix products, arithmetic and copies ran while one was open for 10% of the time, Pallas kernels for 62%

profile of v6, /device:TPU:0, one launch (start us, length us, event | category | flops | bytes accessed | tf_op | source)
XLA Modules:
  0.0 536.3 jit_solution(16530625465245819180)
XLA Ops:
  23.7 6.5 %project_rope.2 = (bf16[2048,256]{1,0:T(8,128)(2,1)S(1)}, bf16[2048,256]{1,0:T(8,128)(2,1)S(1)}, bf16[2048,256]{1,0:T(8,128)(2,1)S(1)}) custom-call(bf16[512,1024]{1,0:T(8,128)(2,1)S(1)} %copy-done.5, bf16[512,1024]{1,0:T(8,128)(2,1)S(1)} %copy-done.6, bf16[512,1024]{1,0:T(8,128)(2,1)} %collective-permute-done.refs_2_, ...), custom_call_target="tpu_custom_call" | custom-call | flops 322122560 | bytes 891289 | tf_op jit(solution)/shard_map/project_rope/pallas_call | solution.py:105
  35.8 28.5 %attention_forward.2 = (bf16[2048,256]{1,0:T(8,128)(2,1)}, f32[2,8,2048]{2,1,0:T(8,128)}) custom-call(s32[2]{0:T(128)} %pad_add_fusion.place_ref, bf16[2048,256]{1,0:T(8,128)(2,1)} %copy-done.13, bf16[2048,256]{1,0:T(8,128)(2,1)} %copy-done.14, bf16[2048,256]{1,0:T(8,128)(2,1)} %copy-done.15), custom_call_target="tpu_custom_call" | custom-call | flops 1717986944 | bytes 419430 | tf_op jit(solution)/shard_map/attention_forward/pallas_call | solution.py:184
  66.3 5.2 collective-permute-done.3.refs_4_.refs_1_.refs_3_.refs_5_
  71.5 7.9 %project_rope.3 = (bf16[2048,256]{1,0:T(8,128)(2,1)S(1)}, bf16[2048,256]{1,0:T(8,128)(2,1)S(1)}, bf16[2048,256]{1,0:T(8,128)(2,1)S(1)}) custom-call(bf16[512,1024]{1,0:T(8,128)(2,1)S(1)} %copy-done.5, bf16[512,1024]{1,0:T(8,128)(2,1)S(1)} %copy-done.7, bf16[512,1024]{1,0:T(8,128)(2,1)} %collective-permute-done.refs_2_, ...), custom_call_target="tpu_custom_call" | custom-call | flops 322122560 | bytes 891289 | tf_op jit(solution)/shard_map/project_rope/pallas_call | solution.py:105
  82.3 28.5 %attention_forward.3 = (bf16[2048,256]{1,0:T(8,128)(2,1)}, f32[2,8,2048]{2,1,0:T(8,128)}) custom-call(s32[2]{0:T(128)} %pad_add_fusion.place_ref, bf16[2048,256]{1,0:T(8,128)(2,1)} %copy-done.16, bf16[2048,256]{1,0:T(8,128)(2,1)} %copy-done.17, bf16[2048,256]{1,0:T(8,128)(2,1)} %copy-done.18), custom_call_target="tpu_custom_call" | custom-call | flops 1717986944 | bytes 419430 | tf_op jit(solution)/shard_map/attention_forward/pallas_call | solution.py:184
  135.0 36.7 %feed_forward.2 = (bf16[2048,1024]{1,0:T(8,128)(2,1)}, bf16[2048,1024]{1,0:T(8,128)(2,1)}, bf16[2048,1024]{1,0:T(8,128)(2,1)}, bf16[1024,1024]{1,0:T(8,128)(2,1)...) custom-call(bf16[512,1024]{1,0:T(8,128)(2,1)} %get-tuple-element.131.refs_0_, ...), custom_call_target="tpu_custom_call" | custom-call | flops 2576980480 | bytes 3355443 | tf_op jit(solution)/shard_map/feed_forward/pallas_call | solution.py:371
  171.9 37.0 %feed_forward.3 = (bf16[2048,1024]{1,0:T(8,128)(2,1)}, bf16[2048,1024]{1,0:T(8,128)(2,1)}, bf16[2048,1024]{1,0:T(8,128)(2,1)}, bf16[1024,1024]{1,0:T(8,128)(2,1)...) custom-call(bf16[512,1024]{1,0:T(8,128)(2,1)} %get-tuple-element.131.refs_0_, ...), custom_call_target="tpu_custom_call" | custom-call | flops 2576980480 | bytes 3355443 | tf_op jit(solution)/shard_map/feed_forward/pallas_call | solution.py:371
  208.9 12.5 %sum_products.10 = bf16[1024,1024]{1,0:T(8,128)(2,1)} custom-call(bf16[2048,1024]{1,0:T(8,128)(2,1)} %get-tuple-element.137.refs_0_, bf16[8,384,1024]{2,1,0:T(8,128)(2,1)} %bitcast.13, bf16[2048,1024]{1,0:T(8,128)(2,1)} %get-tuple-element.130.refs_2_, bf16[8,384,1024]{2,1,0:T(8,128)(2,1)} %bitcast.14, bf16[2048,1024]{1,0:T(8,128)(2,1)} %get-tuple-element.132.refs_4_, ...), custom_call_target="tpu_custom_call" | custom-call | flops 858993472 | bytes 2097152 | tf_op jit(solution)/shard_map/sum_products/pallas_call | solution.py:450
  229.6 12.9 %sum_products.11.refs_3_ = f32[1024,1024]{1,0:T(8,128)} custom-call(bf16[2048,1024]{1,0:T(8,128)(2,1)} %get-tuple-element.137.refs_0_, bf16[8,384,1024]{2,1,0:T(8,128)(2,1)} %bitcast.15, bf16[2048,1024]{1,0:T(8,128)(2,1)} %get-tuple-element.130.refs_2_, bf16[8,384,1024]{2,1,0:T(8,128)(2,1)} %bitcast.16, bf16[2048,1024]{1,0:T(8,128)(2,1)} %get-tuple-element.132.refs_4_, ...), custom_call_target="tpu_custom_call" | custom-call | flops 858993472 | bytes 2097152 | tf_op jit(solution)/shard_map/sum_products/pallas_call | solution.py:450
  257.5 8.2 %branch_backward.1 = (bf16[2048,256]{1,0:T(8,128)(2,1)S(1)}, bf16[2048,256]{1,0:T(8,128)(2,1)S(1)}, bf16[256,1024]{1,0:T(8,128)(2,1)S(1)}, bf16[256,1024]{1,0:T(8,128)(2,1)S(1)}) custom-call(bf16[512,1024]{1,0:T(8,128)(2,1)S(1)} %copy-done.21, bf16[512,1024]{1,0:T(8,128)(2,1)} %get-tuple-element.140.refs_1_, ...), custom_call_target="tpu_custom_call" | custom-call | flops 429496736 | bytes 1258291 | tf_op jit(solution)/shard_map/branch_backward/pallas_call | solution.py:522
  275.9 27.4 %attention_backward.4.rest_0_ = bf16[3,2048,256]{2,1,0:T(8,128)(2,1)} custom-call(s32[2]{0:T(128)} %pad_add_fusion.place_ref, bf16[2048,256]{1,0:T(8,128)(2,1)} %copy-done.16, bf16[2048,256]{1,0:T(8,128)(2,1)} %copy-done.17, bf16[2048,256]{1,0:T(8,128)(2,1)} %copy-done.18, bf16[2048,256]{1,0:T(8,128)(2,1)} %get-tuple-element.120.refs_2_.refs_6_.out_ref, ...), custom_call_target="tpu_custom_call" | custom-call | flops 1503238528 | bytes 419430 | tf_op jit(solution)/shard_map/attention_backward/pallas_call | solution.py:283
  307.8 27.2 %attention_backward.5.refs_4_.refs_0_.refs_2_ = bf16[3,2048,256]{2,1,0:T(8,128)(2,1)} custom-call(s32[2]{0:T(128)} %pad_add_fusion.place_ref, bf16[2048,256]{1,0:T(8,128)(2,1)} %copy-done.16, bf16[2048,256]{1,0:T(8,128)(2,1)} %copy-done.17, bf16[2048,256]{1,0:T(8,128)(2,1)} %copy-done.18, ...), custom_call_target="tpu_custom_call", output_to_operand_aliasing={{}: (11, {})} | custom-call | flops 1503238528 | bytes 419430 | tf_op jit(solution)/shard_map/attention_backward/pallas_call | solution.py:283
  337.0 7.6 %outer_product.2 = bf16[1024,768]{1,0:T(8,128)(2,1)} custom-call(bf16[512,1024]{1,0:T(8,128)(2,1)S(1)} %copy-done.5, bf16[512,1024]{1,0:T(8,128)(2,1)S(1)} %copy-done.8, bf16[512,1024]{1,0:T(8,128)(2,1)} %collective-permute-done.refs_2_, bf16[512,1024]{1,0:T(8,128)(2,1)} %collective-permute-done.1.refs_3_, bf16[3,2048,256]{2,1,0:T(8,128)(2,1)S(1)} %copy-done.1), custom_call_target="tpu_custom_call" | custom-call | flops 322122560 | bytes 891289 | tf_op jit(solution)/shard_map/outer_product/pallas_call | solution.py:485
  353.0 27.3 %attention_backward.6.rest_0_ = bf16[3,2048,256]{2,1,0:T(8,128)(2,1)} custom-call(s32[2]{0:T(128)} %pad_add_fusion.place_ref, bf16[2048,256]{1,0:T(8,128)(2,1)} %copy-done.13, bf16[2048,256]{1,0:T(8,128)(2,1)} %copy-done.14, bf16[2048,256]{1,0:T(8,128)(2,1)} %copy-done.15, bf16[2048,256]{1,0:T(8,128)(2,1)} %get-tuple-element.113.refs_0_.refs_7_.out_ref, ...), custom_call_target="tpu_custom_call" | custom-call | flops 1503238528 | bytes 419430 | tf_op jit(solution)/shard_map/attention_backward/pallas_call | solution.py:283
  388.4 27.4 %attention_backward.7.refs_4_.refs_6_.refs_8_.refs_10_ = bf16[3,2048,256]{2,1,0:T(8,128)(2,1)} custom-call(s32[2]{0:T(128)} %pad_add_fusion.place_ref, bf16[2048,256]{1,0:T(8,128)(2,1)} %copy-done.13, bf16[2048,256]{1,0:T(8,128)(2,1)} %copy-done.14, bf16[2048,256]{1,0:T(8,128)(2,1)} %copy-done.15, ...), custom_call_target="tpu_custom_call", output_to_operand_aliasing={{}: (11, {})} | custom-call | flops 1503238528 | bytes 419430 | tf_op jit(solution)/shard_map/attention_backward/pallas_call | solution.py:283
  417.7 7.0 %outer_product.3 = bf16[1024,768]{1,0:T(8,128)(2,1)S(1)} custom-call(bf16[512,1024]{1,0:T(8,128)(2,1)S(1)} %copy-done.5, bf16[512,1024]{1,0:T(8,128)(2,1)S(1)} %copy-done.8, bf16[512,1024]{1,0:T(8,128)(2,1)} %collective-permute-done.refs_2_, bf16[512,1024]{1,0:T(8,128)(2,1)} %collective-permute-done.1.refs_3_, bf16[3,2048,256]{2,1,0:T(8,128)(2,1)S(1)} %copy-done), custom_call_target="tpu_custom_call" | custom-call | flops 322122560 | bytes 891289 | tf_op jit(solution)/shard_map/outer_product/pallas_call | solution.py:485
  432.0 7.8 %sum_products.12 = bf16[1024,1024]{1,0:T(8,128)(2,1)} custom-call(bf16[2048,1024]{1,0:T(8,128)(2,1)} %get-tuple-element.182.refs_0_, bf16[8,384,1024]{2,1,0:T(8,128)(2,1)} %bitcast.17, bf16[2048,1024]{1,0:T(8,128)(2,1)} %get-tuple-element.174.refs_2_, bf16[1024,1024]{1,0:T(8,128)(2,1)} %refs_3_.3), custom_call_target="tpu_custom_call" | custom-call | flops 429496736 | bytes 1258291 | tf_op jit(solution)/shard_map/sum_products/pallas_call | solution.py:450
  449.3 6.6 %sum_products.13 = bf16[1024,1024]{1,0:T(8,128)(2,1)} custom-call(bf16[3,2048,256]{2,1,0:T(8,128)(2,1)} %attention_backward.5.refs_4_.refs_0_.refs_2_, bf16[1024,768]{1,0:T(8,128)(2,1)} %collective-permute-done.3.refs_4_.refs_1_.refs_3_.refs_5_, bf16[3,2048,256]{2,1,0:T(8,128)(2,1)} %attention_backward.5.refs_4_.refs_0_.refs_2_, ...), custom_call_target="tpu_custom_call" | custom-call | flops 322122560 | bytes 1048576 | tf_op jit(solution)/shard_map/sum_products/pallas_call | solution.py:450
  457.6 8.0 %sum_products.14 = f32[1024,1024]{1,0:T(8,128)} custom-call(bf16[2048,1024]{1,0:T(8,128)(2,1)} %get-tuple-element.182.refs_0_, bf16[8,384,1024]{2,1,0:T(8,128)(2,1)} %bitcast.18, bf16[2048,1024]{1,0:T(8,128)(2,1)} %get-tuple-element.174.refs_2_, bf16[1024,1024]{1,0:T(8,128)(2,1)} %refs_3_.3), custom_call_target="tpu_custom_call" | custom-call | flops 429496736 | bytes 1258291 | tf_op jit(solution)/shard_map/sum_products/pallas_call | solution.py:450
  465.6 7.4 %sum_products.15.refs_3_ = f32[1024,1024]{1,0:T(8,128)} custom-call(bf16[3,2048,256]{2,1,0:T(8,128)(2,1)} %attention_backward.5.refs_4_.refs_0_.refs_2_, bf16[1024,768]{1,0:T(8,128)(2,1)} %collective-permute-done.3.refs_4_.refs_1_.refs_3_.refs_5_, bf16[3,2048,256]{2,1,0:T(8,128)(2,1)} %attention_backward.5.refs_4_.refs_0_.refs_2_, ...), custom_call_target="tpu_custom_call" | custom-call | flops 322122560 | bytes 1048576 | tf_op jit(solution)/shard_map/sum_products/pallas_call | solution.py:450
  473.0 5.5 %add_convert_fusion = bf16[1024,1024]{1,0:T(8,128)(2,1)} fusion(f32[1024,1024]{1,0:T(8,128)S(1)} %copy-done.26, f32[1024,1024]{1,0:T(8,128)} %sum_products.14, bf16[1024,1024]{1,0:T(8,128)(2,1)} %collective-permute-done.24), kind=kLoop, calls=%fused_computation | loop fusion | flops 4194304 | bytes 12582912 | tf_op jit(solution)/shard_map/convert_element_type | solution.py:1004
  478.5 7.9 %layer_norm_backward.5 = (bf16[1024,1024]{1,0:T(8,128)(2,1)}, f32[2,1024]{1,0:T(2,128)}) custom-call(bf16[1024,1024]{1,0:T(8,128)(2,1)} %refs_0_.7, f32[1024,1024]{1,0:T(8,128)} %get-tuple-element.183.refs_1_, f32[1,1024]{1,0:T(1,128)} %bitcast.25, f32[1024,1024]{1,0:T(8,128)} %sum_products.15.refs_3_, bf16[1024,1024]{1,0:T(8,128)(2,1)} %collective-permute-done.25.refs_4_), custom_call_target="tpu_custom_call" | custom-call | flops 3145728 | bytes 1677721 | tf_op jit(solution)/shard_map/layer_norm_backward/pallas_call | solution.py:637
  486.4 13.7 %all-reduce.10.cloned.1.call-done = bf16[512,768]{1,0:T(8,128)(2,1)} async-done(((bf16[512,768]{1,0:T(8,128)(2,1)}), bf16[512,768]{1,0:T(8,128)(2,1)}) %all-reduce.10.cloned.1.call-update) | async-done | bytes 786448 | tf_op jit(solution)/shard_map/psum | solution.py:853
  521.1 5.7 %collective-permute-done.33 = f32[4,1024]{1,0:T(4,128)S(1)} collective-permute-done((f32[4,1024]{1,0:T(4,128)S(1)}, f32[4,1024]{1,0:T(4,128)S(1)}, u32[]{:S(2)}, u32[]{:S(2)}) %collective-permute-start.33) | collective-permute-done | bytes 16416 | tf_op jit(solution)/shard_map/ppermute | solution.py:686
  (219 shorter events, 151.2 us)
Async XLA Ops:
  7.2 126.9 %all-gather.3.cloned.1.call-start = ((), (), s32[]{:S(2)}) async-start(), calls=%async_computation.3 | async-start | bytes 7077888 | tf_op jit(solution)/shard_map/all_gather | solution.py:758
  10.2 23.0 %collective-permute-start.2 = (bf16[384,1024]{1,0:T(8,128)(2,1)}, bf16[384,1024]{1,0:T(8,128)(2,1)}, u32[]{:S(2)}, u32[]{:S(2)}) collective-permute-start(bf16[384,1024]{1,0:T(8,128)(2,1)} %pad_maximum_fusion), channel_id=1, source_target_pairs={{2,0},{3,1},{0,2},{1,3},{6,4},{7,5},{4,6},{5,7},{10,8},{11,9},{8,1... | collective-permute-start | bytes 2359304 | tf_op jit(solution)/shard_map/ppermute | solution.py:730
  33.2 319.8 %all-reduce.8.cloned.1.call-start = ((), (), s32[]{:S(2)}) async-start(), calls=%async_computation.1 | async-start | bytes 2097152 | tf_op jit(solution)/shard_map/psum | solution.py:853
  33.8 48.6 %collective-permute-start.4 = (bf16[1024,1024]{1,0:T(8,128)(2,1)}, bf16[1024,1024]{1,0:T(8,128)(2,1)}, u32[]{:S(2)}, u32[]{:S(2)}) collective-permute-start(bf16[1024,1024]{1,0:T(8,128)(2,1)} %refs_1_.7), channel_id=1, source_target_pairs={{1,0},{0,1},{3,2},{2,3},{5,4},{4,5},{7,6},{6,7},{9,8},{8,9},{11,10... | collective-permute-start | bytes 6291464 | tf_op jit(solution)/shard_map/ppermute | solution.py:723
  33.9 37.5 %collective-permute-start.3 = (bf16[1024,768]{1,0:T(8,128)(2,1)}, bf16[1024,768]{1,0:T(8,128)(2,1)}, u32[]{:S(2)}, u32[]{:S(2)}) collective-permute-start(bf16[1024,768]{1,0:T(8,128)(2,1)} %copy-done.4), channel_id=1, source_target_pairs={{2,0},{3,1},{0,2},{1,3},{6,4},{7,5},{4,6},{5,7},{10,8},{11,9},{8,1... | collective-permute-start | bytes 4718600 | tf_op jit(solution)/shard_map/ppermute | solution.py:730
  64.3 46.6 %collective-permute-start.5 = (bf16[256,1024]{1,0:T(8,128)(2,1)S(1)}, bf16[256,1024]{1,0:T(8,128)(2,1)S(1)}, u32[]{:S(2)}, u32[]{:S(2)}) collective-permute-start(bf16[256,1024]{1,0:T(8,128)(2,1)S(1)} %copy-done.9), channel_id=1, source_target_pairs={{2,0},{3,1},{0,2},{1,3},{6,4},{7,5},{4,6},{5,7},{10,8},{11,9},{8,1... | collective-permute-start | bytes 1572872 | tf_op jit(solution)/shard_map/ppermute | solution.py:730
  171.7 51.8 %collective-permute-start.10 = (bf16[1024,1024]{1,0:T(8,128)(2,1)}, bf16[1024,1024]{1,0:T(8,128)(2,1)}, u32[]{:S(2)}, u32[]{:S(2)}) collective-permute-start(bf16[1024,1024]{1,0:T(8,128)(2,1)} %get-tuple-element.129), channel_id=1, source_target_pairs={{2,0},{3,1},{0,2},{1,3},{6,4},{7,5},{4,6},{5,7},{10,8},{11,9},{8,1... | collective-permute-start | bytes 6291464 | tf_op jit(solution)/shard_map/ppermute | solution.py:730
  221.8 48.8 %collective-permute-start.9 = (bf16[1024,1024]{1,0:T(8,128)(2,1)}, bf16[1024,1024]{1,0:T(8,128)(2,1)}, u32[]{:S(2)}, u32[]{:S(2)}) collective-permute-start(bf16[1024,1024]{1,0:T(8,128)(2,1)} %get-tuple-element.127), channel_id=1, source_target_pairs={{2,0},{3,1},{0,2},{1,3},{6,4},{7,5},{4,6},{5,7},{10,8},{11,9},{8,1... | collective-permute-start | bytes 6291464 | tf_op jit(solution)/shard_map/ppermute | solution.py:730
  228.0 26.6 %collective-permute-start.12 = (bf16[512,1024]{1,0:T(8,128)(2,1)}, bf16[512,1024]{1,0:T(8,128)(2,1)}, u32[]{:S(2)}, u32[]{:S(2)}) collective-permute-start(bf16[512,1024]{1,0:T(8,128)(2,1)} %get-tuple-element.203), channel_id=1, source_target_pairs={{0,4},{4,0},{8,12},{12,8},{16,20},{20,16},{24,28},{28,24},{1,5},{5... | collective-permute-start | bytes 3145736 | tf_op jit(solution)/shard_map/ppermute | solution.py:841
  254.1 91.0 %collective-permute-start.16 = (bf16[1024,1024]{1,0:T(8,128)(2,1)}, bf16[1024,1024]{1,0:T(8,128)(2,1)}, u32[]{:S(2)}, u32[]{:S(2)}) collective-permute-start(bf16[1024,1024]{1,0:T(8,128)(2,1)} %get-tuple-element.153), channel_id=1, source_target_pairs={{2,0},{3,1},{0,2},{1,3},{6,4},{7,5},{4,6},{5,7},{10,8},{11,9},{8,1... | collective-permute-start | bytes 6291464 | tf_op jit(solution)/shard_map/ppermute | solution.py:730
  274.0 29.3 %collective-permute-start.15 = (bf16[512,1024]{1,0:T(8,128)(2,1)}, bf16[512,1024]{1,0:T(8,128)(2,1)}, u32[]{:S(2)}, u32[]{:S(2)}) collective-permute-start(bf16[512,1024]{1,0:T(8,128)(2,1)} %get-tuple-element.202), channel_id=1, source_target_pairs={{0,4},{4,0},{8,12},{12,8},{16,20},{20,16},{24,28},{28,24},{1,5},{5... | collective-permute-start | bytes 3145736 | tf_op jit(solution)/shard_map/ppermute | solution.py:841
  275.9 106.1 %all-reduce.6.cloned.1.call-start = ((), (), s32[]{:S(2)}) async-start(), calls=%async_computation | async-start | bytes 2097152 | tf_op jit(solution)/shard_map/psum | solution.py:853
  306.0 142.2 %all-reduce.12.cloned.1.call-start = ((), (), s32[]{:S(2)}) async-start(), calls=%async_computation.4 | async-start | bytes 2621440 | tf_op jit(solution)/shard_map/psum | solution.py:853
  306.1 43.3 %collective-permute-start.17 = (bf16[256,1024]{1,0:T(8,128)(2,1)S(1)}, bf16[256,1024]{1,0:T(8,128)(2,1)}, u32[]{:S(2)}, u32[]{:S(2)}) collective-permute-start(bf16[256,1024]{1,0:T(8,128)(2,1)S(1)} %copy-done.25), channel_id=1, source_target_pairs={{2,0},{3,1},{0,2},{1,3},{6,4},{7,5},{4,6},{5,7},{10,8},{11,9},{8,1... | collective-permute-start | bytes 1572872 | tf_op jit(solution)/shard_map/ppermute | solution.py:730
  344.6 80.1 %collective-permute-start.18 = (bf16[1024,768]{1,0:T(8,128)(2,1)}, bf16[1024,768]{1,0:T(8,128)(2,1)}, u32[]{:S(2)}, u32[]{:S(2)}) collective-permute-start(bf16[1024,768]{1,0:T(8,128)(2,1)} %outer_product.2), channel_id=1, source_target_pairs={{2,0},{3,1},{0,2},{1,3},{6,4},{7,5},{4,6},{5,7},{10,8},{11,9},{8,1... | collective-permute-start | bytes 4718600 | tf_op jit(solution)/shard_map/ppermute | solution.py:730
  349.1 36.6 %collective-permute-start.19 = (bf16[512,1024]{1,0:T(8,128)(2,1)}, bf16[512,1024]{1,0:T(8,128)(2,1)}, u32[]{:S(2)}, u32[]{:S(2)}) collective-permute-start(bf16[512,1024]{1,0:T(8,128)(2,1)} %get-tuple-element.199), channel_id=1, source_target_pairs={{0,4},{4,0},{8,12},{12,8},{16,20},{20,16},{24,28},{28,24},{1,5},{5... | collective-permute-start | bytes 3145736 | tf_op jit(solution)/shard_map/ppermute | solution.py:841
  351.4 32.6 %collective-permute-start.20 = (bf16[128,1024]{1,0:T(8,128)(2,1)}, bf16[128,1024]{1,0:T(8,128)(2,1)}, u32[]{:S(2)}, u32[]{:S(2)}) collective-permute-start(bf16[128,1024]{1,0:T(8,128)(2,1)} %get-tuple-element.218), channel_id=1, source_target_pairs={{0,4},{4,0},{8,12},{12,8},{16,20},{20,16},{24,28},{28,24},{1,5},{5... | collective-permute-start | bytes 786440 | tf_op jit(solution)/shard_map/ppermute | solution.py:841
  382.0 46.2 %collective-permute-start.21 = (bf16[512,1024]{1,0:T(8,128)(2,1)}, bf16[512,1024]{1,0:T(8,128)(2,1)}, u32[]{:S(2)}, u32[]{:S(2)}) collective-permute-start(bf16[512,1024]{1,0:T(8,128)(2,1)} %all-reduce.6.cloned.1.call-done), channel_id=1, source_target_pairs={{0,4},{4,0},{8,12},{12,8},{16,20},{20,16},{24,28},{28,24},{1,5},{5... | collective-permute-start | bytes 3145736 | tf_op jit(solution)/shard_map/ppermute | solution.py:857
  383.4 56.4 %collective-permute-start.23 = (bf16[512,1024]{1,0:T(8,128)(2,1)}, bf16[512,1024]{1,0:T(8,128)(2,1)}, u32[]{:S(2)}, u32[]{:S(2)}) collective-permute-start(bf16[512,1024]{1,0:T(8,128)(2,1)} %all-reduce.8.cloned.1.call-done), channel_id=1, source_target_pairs={{0,4},{4,0},{8,12},{12,8},{16,20},{20,16},{24,28},{28,24},{1,5},{5... | collective-permute-start | bytes 3145736 | tf_op jit(solution)/shard_map/ppermute | solution.py:857
  388.3 111.8 %all-reduce.10.cloned.1.call-start = ((), (), s32[]{:S(2)}) async-start(), calls=%async_computation.2 | async-start | bytes 1572864 | tf_op jit(solution)/shard_map/psum | solution.py:853
  439.7 33.3 %collective-permute-start.24 = (bf16[1024,1024]{1,0:T(8,128)(2,1)}, bf16[1024,1024]{1,0:T(8,128)(2,1)}, u32[]{:S(2)}, u32[]{:S(2)}) collective-permute-start(bf16[1024,1024]{1,0:T(8,128)(2,1)} %sum_products.12), channel_id=1, source_target_pairs={{1,0},{0,1},{3,2},{2,3},{5,4},{4,5},{7,6},{6,7},{9,8},{8,9},{11,10... | collective-permute-start | bytes 6291464 | tf_op jit(solution)/shard_map/ppermute | solution.py:723
  455.9 22.6 %collective-permute-start.25 = (bf16[1024,1024]{1,0:T(8,128)(2,1)}, bf16[1024,1024]{1,0:T(8,128)(2,1)}, u32[]{:S(2)}, u32[]{:S(2)}) collective-permute-start(bf16[1024,1024]{1,0:T(8,128)(2,1)} %sum_products.13), channel_id=1, source_target_pairs={{1,0},{0,1},{3,2},{2,3},{5,4},{4,5},{7,6},{6,7},{9,8},{8,9},{11,10... | collective-permute-start | bytes 6291464 | tf_op jit(solution)/shard_map/ppermute | solution.py:723
  456.0 47.0 %collective-permute-start.28 = (bf16[512,1024]{1,0:T(8,128)(2,1)S(1)}, bf16[512,1024]{1,0:T(8,128)(2,1)}, u32[]{:S(2)}, u32[]{:S(2)}) collective-permute-start(bf16[512,1024]{1,0:T(8,128)(2,1)S(1)} %copy-done.34), channel_id=1, source_target_pairs={{0,4},{4,0},{8,12},{12,8},{16,20},{20,16},{24,28},{28,24},{1,5},{5... | collective-permute-start | bytes 3145736 | tf_op jit(solution)/shard_map/ppermute | solution.py:857
  502.5 25.0 %collective-permute-start.26 = (bf16[512,768]{1,0:T(8,128)(2,1)}, bf16[512,768]{1,0:T(8,128)(2,1)S(1)}, u32[]{:S(2)}, u32[]{:S(2)}) collective-permute-start(bf16[512,768]{1,0:T(8,128)(2,1)} %all-reduce.10.cloned.1.call-done), channel_id=1, source_target_pairs={{0,4},{4,0},{8,12},{12,8},{16,20},{20,16},{24,28},{28,24},{1,5},{5... | collective-permute-start | bytes 2359304 | tf_op jit(solution)/shard_map/ppermute | solution.py:857
  (59 other events, 527.7 us)
Sparse Core Ops, SparseCore 0:
  33.3 99.3 all-gather.2
  276.0 52.1 all-reduce.7
  330.7 51.1 all-reduce.5
  388.4 59.7 all-reduce.11
  457.7 42.4 all-reduce.9

commit v7 on v6

--- a/solution.py
+++ b/solution.py
@@ -176,7 +176,7 @@
     log_ref[0] = jnp.concatenate(logs + [jnp.zeros((6, q_ref.shape[0]), F32)], axis=0)
 
 
-def attend(place, queries, keys, values, block=1024, chunk=512):
+def attend(place, queries, keys, values, block=1024, chunk=2048):
     count, columns = queries.shape
     pairs = columns // LANES
     whole = pl.BlockSpec((count, LANES), lambda p, i, _: (0, p))

time: 542 us -> 540 us (level)
  transfers between devices with their start and end apart: 39 -> 39, of which waited for: 12 -> 13; matrix products, arithmetic and copies ran while one was open for 10% -> 10% of each run, Pallas kernels for 62% -> 62%
where the time goes in v7:
time: 540 us; the launch traced here: 534 us
  Pallas kernels  368 us (68%)
  other arithmetic  52 us (10%)
  waiting for transfers between devices  51.3 us (10%)
  starting transfers between devices  30.2 us (6%)
  local copies, waits for them, and re-layouts  18.6 us (3%)
  between operations  14.7 us (3%)
    pallas_call x4, Pallas kernels, attend_back(): pl.pallas_call(functools.partial(attend_back_kernel, chunk=chunk), grid_s...  109 us
    pallas_call x2, Pallas kernels, feed(): pl.pallas_call(functools.partial(feed_kernel, counts=(len(rows), len(targ...  73.7 us
    pallas_call x8, Pallas kernels, sum_products(): pl.pallas_call(functools.partial(sum_kernel, places=places, dims=tuple(di...  63.5 us
    pallas_call x2, Pallas kernels, attend(): pl.pallas_call(functools.partial(attend_kernel, chunk=chunk), grid_spec=p...  53.1 us
    pallas_call x3, Pallas kernels, norm_back(): pl.pallas_call(lambda *refs, held=len(held): norm_back_kernel(*refs[:3 +...  17.6 us
    psum x4, waiting for transfers between devices, sum_half(): return lax.psum(value, 'dp', axis_index_groups=groups)  16.8 us
    convert_element_type x5, other arithmetic, total(): sum((half(piece, which).astype(F32) for piece in pieces)).astype(BF16)  15.7 us
    pallas_call x2, Pallas kernels, outer(): pl.pallas_call(functools.partial(outer_kernel, count=len(pieces)), grid=(...  14.6 us
  transfers between devices with their start and end apart: 39, of which 13 were waited for; matrix products, arithmetic and copies ran while one was open for 10% of the time, Pallas kernels for 62%

profile of v7, /device:TPU:0, one launch (start us, length us, event | category | flops | bytes accessed | tf_op | source)
XLA Modules:
  0.0 534.3 jit_solution(12188772201651179034)
XLA Ops:
  23.7 6.5 %project_rope.2 = (bf16[2048,256]{1,0:T(8,128)(2,1)S(1)}, bf16[2048,256]{1,0:T(8,128)(2,1)S(1)}, bf16[2048,256]{1,0:T(8,128)(2,1)S(1)}) custom-call(bf16[512,1024]{1,0:T(8,128)(2,1)S(1)} %copy-done.5, bf16[512,1024]{1,0:T(8,128)(2,1)S(1)} %copy-done.6, bf16[512,1024]{1,0:T(8,128)(2,1)} %collective-permute-done.refs_2_, ...), custom_call_target="tpu_custom_call" | custom-call | flops 322122560 | bytes 891289 | tf_op jit(solution)/shard_map/project_rope/pallas_call | solution.py:105
  35.8 26.6 %attention_forward.2 = (bf16[2048,256]{1,0:T(8,128)(2,1)}, f32[2,8,2048]{2,1,0:T(8,128)}) custom-call(s32[2]{0:T(128)} %pad_add_fusion.place_ref, bf16[2048,256]{1,0:T(8,128)(2,1)} %copy-done.13, bf16[2048,256]{1,0:T(8,128)(2,1)} %copy-done.14, bf16[2048,256]{1,0:T(8,128)(2,1)} %copy-done.15), custom_call_target="tpu_custom_call" | custom-call | flops 1717986944 | bytes 419430 | tf_op jit(solution)/shard_map/attention_forward/pallas_call | solution.py:184
  64.4 7.1 %collective-permute-done.3.refs_4_.refs_1_.refs_3_.refs_5_ = bf16[1024,768]{1,0:T(8,128)(2,1)} collective-permute-done((bf16[1024,768]{1,0:T(8,128)(2,1)}, bf16[1024,768]{1,0:T(8,128)(2,1)}, u32[]{:S(2)}, u32[]{:S(2)}) %collective-permute-start.3) | collective-permute-done | bytes 1572896 | tf_op jit(solution)/shard_map/ppermute | solution.py:730
  71.5 7.9 %project_rope.3 = (bf16[2048,256]{1,0:T(8,128)(2,1)S(1)}, bf16[2048,256]{1,0:T(8,128)(2,1)S(1)}, bf16[2048,256]{1,0:T(8,128)(2,1)S(1)}) custom-call(bf16[512,1024]{1,0:T(8,128)(2,1)S(1)} %copy-done.5, bf16[512,1024]{1,0:T(8,128)(2,1)S(1)} %copy-done.7, bf16[512,1024]{1,0:T(8,128)(2,1)} %collective-permute-done.refs_2_, ...), custom_call_target="tpu_custom_call" | custom-call | flops 322122560 | bytes 891289 | tf_op jit(solution)/shard_map/project_rope/pallas_call | solution.py:105
  82.3 26.6 %attention_forward.3 = (bf16[2048,256]{1,0:T(8,128)(2,1)}, f32[2,8,2048]{2,1,0:T(8,128)}) custom-call(s32[2]{0:T(128)} %pad_add_fusion.place_ref, bf16[2048,256]{1,0:T(8,128)(2,1)} %copy-done.16, bf16[2048,256]{1,0:T(8,128)(2,1)} %copy-done.17, bf16[2048,256]{1,0:T(8,128)(2,1)} %copy-done.18), custom_call_target="tpu_custom_call" | custom-call | flops 1717986944 | bytes 419430 | tf_op jit(solution)/shard_map/attention_forward/pallas_call | solution.py:184
  133.1 36.7 %feed_forward.2 = (bf16[2048,1024]{1,0:T(8,128)(2,1)}, bf16[2048,1024]{1,0:T(8,128)(2,1)}, bf16[2048,1024]{1,0:T(8,128)(2,1)}, bf16[1024,1024]{1,0:T(8,128)(2,1)...) custom-call(bf16[512,1024]{1,0:T(8,128)(2,1)} %get-tuple-element.131.refs_0_, ...), custom_call_target="tpu_custom_call" | custom-call | flops 2576980480 | bytes 3355443 | tf_op jit(solution)/shard_map/feed_forward/pallas_call | solution.py:371
  170.9 37.0 %feed_forward.3 = (bf16[2048,1024]{1,0:T(8,128)(2,1)}, bf16[2048,1024]{1,0:T(8,128)(2,1)}, bf16[2048,1024]{1,0:T(8,128)(2,1)}, bf16[1024,1024]{1,0:T(8,128)(2,1)...) custom-call(bf16[512,1024]{1,0:T(8,128)(2,1)} %get-tuple-element.131.refs_0_, ...), custom_call_target="tpu_custom_call" | custom-call | flops 2576980480 | bytes 3355443 | tf_op jit(solution)/shard_map/feed_forward/pallas_call | solution.py:371
  208.0 12.5 %sum_products.10 = bf16[1024,1024]{1,0:T(8,128)(2,1)} custom-call(bf16[2048,1024]{1,0:T(8,128)(2,1)} %get-tuple-element.137.refs_0_, bf16[8,384,1024]{2,1,0:T(8,128)(2,1)} %bitcast.13, bf16[2048,1024]{1,0:T(8,128)(2,1)} %get-tuple-element.130.refs_2_, bf16[8,384,1024]{2,1,0:T(8,128)(2,1)} %bitcast.14, bf16[2048,1024]{1,0:T(8,128)(2,1)} %get-tuple-element.132.refs_4_, ...), custom_call_target="tpu_custom_call" | custom-call | flops 858993472 | bytes 2097152 | tf_op jit(solution)/shard_map/sum_products/pallas_call | solution.py:450
  227.6 12.9 %sum_products.11.refs_3_ = f32[1024,1024]{1,0:T(8,128)} custom-call(bf16[2048,1024]{1,0:T(8,128)(2,1)} %get-tuple-element.137.refs_0_, bf16[8,384,1024]{2,1,0:T(8,128)(2,1)} %bitcast.15, bf16[2048,1024]{1,0:T(8,128)(2,1)} %get-tuple-element.130.refs_2_, bf16[8,384,1024]{2,1,0:T(8,128)(2,1)} %bitcast.16, bf16[2048,1024]{1,0:T(8,128)(2,1)} %get-tuple-element.132.refs_4_, ...), custom_call_target="tpu_custom_call" | custom-call | flops 858993472 | bytes 2097152 | tf_op jit(solution)/shard_map/sum_products/pallas_call | solution.py:450
  255.6 8.2 %branch_backward.1 = (bf16[2048,256]{1,0:T(8,128)(2,1)S(1)}, bf16[2048,256]{1,0:T(8,128)(2,1)S(1)}, bf16[256,1024]{1,0:T(8,128)(2,1)S(1)}, bf16[256,1024]{1,0:T(8,128)(2,1)S(1)}) custom-call(bf16[512,1024]{1,0:T(8,128)(2,1)S(1)} %copy-done.21, bf16[512,1024]{1,0:T(8,128)(2,1)} %get-tuple-element.140.refs_1_, ...), custom_call_target="tpu_custom_call" | custom-call | flops 429496736 | bytes 1258291 | tf_op jit(solution)/shard_map/branch_backward/pallas_call | solution.py:522
  263.8 5.5 %collective-permute-done.9 = bf16[1024,1024]{1,0:T(8,128)(2,1)} collective-permute-done((bf16[1024,1024]{1,0:T(8,128)(2,1)}, bf16[1024,1024]{1,0:T(8,128)(2,1)}, u32[]{:S(2)}, u32[]{:S(2)}) %collective-permute-start.9) | collective-permute-done | bytes 2097184 | tf_op jit(solution)/shard_map/ppermute | solution.py:730
  274.0 27.4 %attention_backward.4.rest_0_ = bf16[3,2048,256]{2,1,0:T(8,128)(2,1)} custom-call(s32[2]{0:T(128)} %pad_add_fusion.place_ref, bf16[2048,256]{1,0:T(8,128)(2,1)} %copy-done.16, bf16[2048,256]{1,0:T(8,128)(2,1)} %copy-done.17, bf16[2048,256]{1,0:T(8,128)(2,1)} %copy-done.18, bf16[2048,256]{1,0:T(8,128)(2,1)} %get-tuple-element.120.refs_2_.refs_6_.out_ref, ...), custom_call_target="tpu_custom_call" | custom-call | flops 1503238528 | bytes 419430 | tf_op jit(solution)/shard_map/attention_backward/pallas_call | solution.py:283
  305.8 27.2 %attention_backward.5.refs_4_.refs_0_.refs_2_ = bf16[3,2048,256]{2,1,0:T(8,128)(2,1)} custom-call(s32[2]{0:T(128)} %pad_add_fusion.place_ref, bf16[2048,256]{1,0:T(8,128)(2,1)} %copy-done.16, bf16[2048,256]{1,0:T(8,128)(2,1)} %copy-done.17, bf16[2048,256]{1,0:T(8,128)(2,1)} %copy-done.18, ...), custom_call_target="tpu_custom_call", output_to_operand_aliasing={{}: (11, {})} | custom-call | flops 1503238528 | bytes 419430 | tf_op jit(solution)/shard_map/attention_backward/pallas_call | solution.py:283
  334.9 7.6 %outer_product.2 = bf16[1024,768]{1,0:T(8,128)(2,1)} custom-call(bf16[512,1024]{1,0:T(8,128)(2,1)S(1)} %copy-done.5, bf16[512,1024]{1,0:T(8,128)(2,1)S(1)} %copy-done.8, bf16[512,1024]{1,0:T(8,128)(2,1)} %collective-permute-done.refs_2_, bf16[512,1024]{1,0:T(8,128)(2,1)} %collective-permute-done.1.refs_3_, bf16[3,2048,256]{2,1,0:T(8,128)(2,1)S(1)} %copy-done.1), custom_call_target="tpu_custom_call" | custom-call | flops 322122560 | bytes 891289 | tf_op jit(solution)/shard_map/outer_product/pallas_call | solution.py:485
  351.1 27.3 %attention_backward.6.rest_0_ = bf16[3,2048,256]{2,1,0:T(8,128)(2,1)} custom-call(s32[2]{0:T(128)} %pad_add_fusion.place_ref, bf16[2048,256]{1,0:T(8,128)(2,1)} %copy-done.13, bf16[2048,256]{1,0:T(8,128)(2,1)} %copy-done.14, bf16[2048,256]{1,0:T(8,128)(2,1)} %copy-done.15, bf16[2048,256]{1,0:T(8,128)(2,1)} %get-tuple-element.113.refs_0_.refs_7_.out_ref, ...), custom_call_target="tpu_custom_call" | custom-call | flops 1503238528 | bytes 419430 | tf_op jit(solution)/shard_map/attention_backward/pallas_call | solution.py:283
  386.4 27.4 %attention_backward.7.refs_4_.refs_6_.refs_8_.refs_10_ = bf16[3,2048,256]{2,1,0:T(8,128)(2,1)} custom-call(s32[2]{0:T(128)} %pad_add_fusion.place_ref, bf16[2048,256]{1,0:T(8,128)(2,1)} %copy-done.13, bf16[2048,256]{1,0:T(8,128)(2,1)} %copy-done.14, bf16[2048,256]{1,0:T(8,128)(2,1)} %copy-done.15, ...), custom_call_target="tpu_custom_call", output_to_operand_aliasing={{}: (11, {})} | custom-call | flops 1503238528 | bytes 419430 | tf_op jit(solution)/shard_map/attention_backward/pallas_call | solution.py:283
  415.7 7.0 %outer_product.3 = bf16[1024,768]{1,0:T(8,128)(2,1)S(1)} custom-call(bf16[512,1024]{1,0:T(8,128)(2,1)S(1)} %copy-done.5, bf16[512,1024]{1,0:T(8,128)(2,1)S(1)} %copy-done.8, bf16[512,1024]{1,0:T(8,128)(2,1)} %collective-permute-done.refs_2_, bf16[512,1024]{1,0:T(8,128)(2,1)} %collective-permute-done.1.refs_3_, bf16[3,2048,256]{2,1,0:T(8,128)(2,1)S(1)} %copy-done), custom_call_target="tpu_custom_call" | custom-call | flops 322122560 | bytes 891289 | tf_op jit(solution)/shard_map/outer_product/pallas_call | solution.py:485
  430.0 7.8 %sum_products.12 = bf16[1024,1024]{1,0:T(8,128)(2,1)} custom-call(bf16[2048,1024]{1,0:T(8,128)(2,1)} %get-tuple-element.182.refs_0_, bf16[8,384,1024]{2,1,0:T(8,128)(2,1)} %bitcast.17, bf16[2048,1024]{1,0:T(8,128)(2,1)} %get-tuple-element.174.refs_2_, bf16[1024,1024]{1,0:T(8,128)(2,1)} %refs_3_.3), custom_call_target="tpu_custom_call" | custom-call | flops 429496736 | bytes 1258291 | tf_op jit(solution)/shard_map/sum_products/pallas_call | solution.py:450
  447.3 6.6 %sum_products.13 = bf16[1024,1024]{1,0:T(8,128)(2,1)} custom-call(bf16[3,2048,256]{2,1,0:T(8,128)(2,1)} %attention_backward.5.refs_4_.refs_0_.refs_2_, bf16[1024,768]{1,0:T(8,128)(2,1)} %collective-permute-done.3.refs_4_.refs_1_.refs_3_.refs_5_, bf16[3,2048,256]{2,1,0:T(8,128)(2,1)} %attention_backward.5.refs_4_.refs_0_.refs_2_, ...), custom_call_target="tpu_custom_call" | custom-call | flops 322122560 | bytes 1048576 | tf_op jit(solution)/shard_map/sum_products/pallas_call | solution.py:450
  455.6 8.0 %sum_products.14 = f32[1024,1024]{1,0:T(8,128)} custom-call(bf16[2048,1024]{1,0:T(8,128)(2,1)} %get-tuple-element.182.refs_0_, bf16[8,384,1024]{2,1,0:T(8,128)(2,1)} %bitcast.18, bf16[2048,1024]{1,0:T(8,128)(2,1)} %get-tuple-element.174.refs_2_, bf16[1024,1024]{1,0:T(8,128)(2,1)} %refs_3_.3), custom_call_target="tpu_custom_call" | custom-call | flops 429496736 | bytes 1258291 | tf_op jit(solution)/shard_map/sum_products/pallas_call | solution.py:450
  463.6 7.4 %sum_products.15.refs_3_ = f32[1024,1024]{1,0:T(8,128)} custom-call(bf16[3,2048,256]{2,1,0:T(8,128)(2,1)} %attention_backward.5.refs_4_.refs_0_.refs_2_, bf16[1024,768]{1,0:T(8,128)(2,1)} %collective-permute-done.3.refs_4_.refs_1_.refs_3_.refs_5_, bf16[3,2048,256]{2,1,0:T(8,128)(2,1)} %attention_backward.5.refs_4_.refs_0_.refs_2_, ...), custom_call_target="tpu_custom_call" | custom-call | flops 322122560 | bytes 1048576 | tf_op jit(solution)/shard_map/sum_products/pallas_call | solution.py:450
  476.5 7.9 %layer_norm_backward.5 = (bf16[1024,1024]{1,0:T(8,128)(2,1)}, f32[2,1024]{1,0:T(2,128)}) custom-call(bf16[1024,1024]{1,0:T(8,128)(2,1)} %refs_0_.7, f32[1024,1024]{1,0:T(8,128)} %get-tuple-element.183.refs_1_, f32[1,1024]{1,0:T(1,128)} %bitcast.25, f32[1024,1024]{1,0:T(8,128)} %sum_products.15.refs_3_, bf16[1024,1024]{1,0:T(8,128)(2,1)} %collective-permute-done.25.refs_4_), custom_call_target="tpu_custom_call" | custom-call | flops 3145728 | bytes 1677721 | tf_op jit(solution)/shard_map/layer_norm_backward/pallas_call | solution.py:637
  484.4 13.7 %all-reduce.10.cloned.1.call-done = bf16[512,768]{1,0:T(8,128)(2,1)} async-done(((bf16[512,768]{1,0:T(8,128)(2,1)}), bf16[512,768]{1,0:T(8,128)(2,1)}) %all-reduce.10.cloned.1.call-update) | async-done | bytes 786448 | tf_op jit(solution)/shard_map/psum | solution.py:853
  519.1 5.7 %collective-permute-done.33 = f32[4,1024]{1,0:T(4,128)S(1)} collective-permute-done((f32[4,1024]{1,0:T(4,128)S(1)}, f32[4,1024]{1,0:T(4,128)S(1)}, u32[]{:S(2)}, u32[]{:S(2)}) %collective-permute-start.33) | collective-permute-done | bytes 16416 | tf_op jit(solution)/shard_map/ppermute | solution.py:686
  (219 shorter events, 151.0 us)
Async XLA Ops:
  7.2 125.5 %all-gather.3.cloned.1.call-start = ((), (), s32[]{:S(2)}) async-start(), calls=%async_computation.3 | async-start | bytes 7077888 | tf_op jit(solution)/shard_map/all_gather | solution.py:758
  10.2 23.0 %collective-permute-start.2 = (bf16[384,1024]{1,0:T(8,128)(2,1)}, bf16[384,1024]{1,0:T(8,128)(2,1)}, u32[]{:S(2)}, u32[]{:S(2)}) collective-permute-start(bf16[384,1024]{1,0:T(8,128)(2,1)} %pad_maximum_fusion), channel_id=1, source_target_pairs={{2,0},{3,1},{0,2},{1,3},{6,4},{7,5},{4,6},{5,7},{10,8},{11,9},{8,1... | collective-permute-start | bytes 2359304 | tf_op jit(solution)/shard_map/ppermute | solution.py:730
  33.2 317.9 %all-reduce.8.cloned.1.call-start = ((), (), s32[]{:S(2)}) async-start(), calls=%async_computation.1 | async-start | bytes 2097152 | tf_op jit(solution)/shard_map/psum | solution.py:853
  33.8 48.6 %collective-permute-start.4 = (bf16[1024,1024]{1,0:T(8,128)(2,1)}, bf16[1024,1024]{1,0:T(8,128)(2,1)}, u32[]{:S(2)}, u32[]{:S(2)}) collective-permute-start(bf16[1024,1024]{1,0:T(8,128)(2,1)} %refs_1_.7), channel_id=1, source_target_pairs={{1,0},{0,1},{3,2},{2,3},{5,4},{4,5},{7,6},{6,7},{9,8},{8,9},{11,10... | collective-permute-start | bytes 6291464 | tf_op jit(solution)/shard_map/ppermute | solution.py:723
  33.9 37.5 %collective-permute-start.3 = (bf16[1024,768]{1,0:T(8,128)(2,1)}, bf16[1024,768]{1,0:T(8,128)(2,1)}, u32[]{:S(2)}, u32[]{:S(2)}) collective-permute-start(bf16[1024,768]{1,0:T(8,128)(2,1)} %copy-done.4), channel_id=1, source_target_pairs={{2,0},{3,1},{0,2},{1,3},{6,4},{7,5},{4,6},{5,7},{10,8},{11,9},{8,1... | collective-permute-start | bytes 4718600 | tf_op jit(solution)/shard_map/ppermute | solution.py:730
  62.3 46.6 %collective-permute-start.5 = (bf16[256,1024]{1,0:T(8,128)(2,1)S(1)}, bf16[256,1024]{1,0:T(8,128)(2,1)S(1)}, u32[]{:S(2)}, u32[]{:S(2)}) collective-permute-start(bf16[256,1024]{1,0:T(8,128)(2,1)S(1)} %copy-done.9), channel_id=1, source_target_pairs={{2,0},{3,1},{0,2},{1,3},{6,4},{7,5},{4,6},{5,7},{10,8},{11,9},{8,1... | collective-permute-start | bytes 1572872 | tf_op jit(solution)/shard_map/ppermute | solution.py:730
  169.8 51.8 %collective-permute-start.10 = (bf16[1024,1024]{1,0:T(8,128)(2,1)}, bf16[1024,1024]{1,0:T(8,128)(2,1)}, u32[]{:S(2)}, u32[]{:S(2)}) collective-permute-start(bf16[1024,1024]{1,0:T(8,128)(2,1)} %get-tuple-element.129), channel_id=1, source_target_pairs={{2,0},{3,1},{0,2},{1,3},{6,4},{7,5},{4,6},{5,7},{10,8},{11,9},{8,1... | collective-permute-start | bytes 6291464 | tf_op jit(solution)/shard_map/ppermute | solution.py:730
  220.6 48.8 %collective-permute-start.9 = (bf16[1024,1024]{1,0:T(8,128)(2,1)}, bf16[1024,1024]{1,0:T(8,128)(2,1)}, u32[]{:S(2)}, u32[]{:S(2)}) collective-permute-start(bf16[1024,1024]{1,0:T(8,128)(2,1)} %get-tuple-element.127), channel_id=1, source_target_pairs={{2,0},{3,1},{0,2},{1,3},{6,4},{7,5},{4,6},{5,7},{10,8},{11,9},{8,1... | collective-permute-start | bytes 6291464 | tf_op jit(solution)/shard_map/ppermute | solution.py:730
  226.0 26.6 %collective-permute-start.12 = (bf16[512,1024]{1,0:T(8,128)(2,1)}, bf16[512,1024]{1,0:T(8,128)(2,1)}, u32[]{:S(2)}, u32[]{:S(2)}) collective-permute-start(bf16[512,1024]{1,0:T(8,128)(2,1)} %get-tuple-element.203), channel_id=1, source_target_pairs={{0,4},{4,0},{8,12},{12,8},{16,20},{20,16},{24,28},{28,24},{1,5},{5... | collective-permute-start | bytes 3145736 | tf_op jit(solution)/shard_map/ppermute | solution.py:841
  252.1 91.1 %collective-permute-start.16 = (bf16[1024,1024]{1,0:T(8,128)(2,1)}, bf16[1024,1024]{1,0:T(8,128)(2,1)}, u32[]{:S(2)}, u32[]{:S(2)}) collective-permute-start(bf16[1024,1024]{1,0:T(8,128)(2,1)} %get-tuple-element.153), channel_id=1, source_target_pairs={{2,0},{3,1},{0,2},{1,3},{6,4},{7,5},{4,6},{5,7},{10,8},{11,9},{8,1... | collective-permute-start | bytes 6291464 | tf_op jit(solution)/shard_map/ppermute | solution.py:730
  272.9 28.5 %collective-permute-start.15 = (bf16[512,1024]{1,0:T(8,128)(2,1)}, bf16[512,1024]{1,0:T(8,128)(2,1)}, u32[]{:S(2)}, u32[]{:S(2)}) collective-permute-start(bf16[512,1024]{1,0:T(8,128)(2,1)} %get-tuple-element.202), channel_id=1, source_target_pairs={{0,4},{4,0},{8,12},{12,8},{16,20},{20,16},{24,28},{28,24},{1,5},{5... | collective-permute-start | bytes 3145736 | tf_op jit(solution)/shard_map/ppermute | solution.py:841
  273.9 106.0 %all-reduce.6.cloned.1.call-start = ((), (), s32[]{:S(2)}) async-start(), calls=%async_computation | async-start | bytes 2097152 | tf_op jit(solution)/shard_map/psum | solution.py:853
  304.1 142.1 %all-reduce.12.cloned.1.call-start = ((), (), s32[]{:S(2)}) async-start(), calls=%async_computation.4 | async-start | bytes 2621440 | tf_op jit(solution)/shard_map/psum | solution.py:853
  304.2 44.0 %collective-permute-start.17 = (bf16[256,1024]{1,0:T(8,128)(2,1)S(1)}, bf16[256,1024]{1,0:T(8,128)(2,1)}, u32[]{:S(2)}, u32[]{:S(2)}) collective-permute-start(bf16[256,1024]{1,0:T(8,128)(2,1)S(1)} %copy-done.25), channel_id=1, source_target_pairs={{2,0},{3,1},{0,2},{1,3},{6,4},{7,5},{4,6},{5,7},{10,8},{11,9},{8,1... | collective-permute-start | bytes 1572872 | tf_op jit(solution)/shard_map/ppermute | solution.py:730
  342.6 80.1 %collective-permute-start.18 = (bf16[1024,768]{1,0:T(8,128)(2,1)}, bf16[1024,768]{1,0:T(8,128)(2,1)}, u32[]{:S(2)}, u32[]{:S(2)}) collective-permute-start(bf16[1024,768]{1,0:T(8,128)(2,1)} %outer_product.2), channel_id=1, source_target_pairs={{2,0},{3,1},{0,2},{1,3},{6,4},{7,5},{4,6},{5,7},{10,8},{11,9},{8,1... | collective-permute-start | bytes 4718600 | tf_op jit(solution)/shard_map/ppermute | solution.py:730
  347.2 36.5 %collective-permute-start.19 = (bf16[512,1024]{1,0:T(8,128)(2,1)}, bf16[512,1024]{1,0:T(8,128)(2,1)}, u32[]{:S(2)}, u32[]{:S(2)}) collective-permute-start(bf16[512,1024]{1,0:T(8,128)(2,1)} %get-tuple-element.199), channel_id=1, source_target_pairs={{0,4},{4,0},{8,12},{12,8},{16,20},{20,16},{24,28},{28,24},{1,5},{5... | collective-permute-start | bytes 3145736 | tf_op jit(solution)/shard_map/ppermute | solution.py:841
  350.1 31.9 %collective-permute-start.20 = (bf16[128,1024]{1,0:T(8,128)(2,1)}, bf16[128,1024]{1,0:T(8,128)(2,1)}, u32[]{:S(2)}, u32[]{:S(2)}) collective-permute-start(bf16[128,1024]{1,0:T(8,128)(2,1)} %get-tuple-element.218), channel_id=1, source_target_pairs={{0,4},{4,0},{8,12},{12,8},{16,20},{20,16},{24,28},{28,24},{1,5},{5... | collective-permute-start | bytes 786440 | tf_op jit(solution)/shard_map/ppermute | solution.py:841
  379.9 46.2 %collective-permute-start.21 = (bf16[512,1024]{1,0:T(8,128)(2,1)}, bf16[512,1024]{1,0:T(8,128)(2,1)}, u32[]{:S(2)}, u32[]{:S(2)}) collective-permute-start(bf16[512,1024]{1,0:T(8,128)(2,1)} %all-reduce.6.cloned.1.call-done), channel_id=1, source_target_pairs={{0,4},{4,0},{8,12},{12,8},{16,20},{20,16},{24,28},{28,24},{1,5},{5... | collective-permute-start | bytes 3145736 | tf_op jit(solution)/shard_map/ppermute | solution.py:857
  381.4 56.4 %collective-permute-start.23 = (bf16[512,1024]{1,0:T(8,128)(2,1)}, bf16[512,1024]{1,0:T(8,128)(2,1)}, u32[]{:S(2)}, u32[]{:S(2)}) collective-permute-start(bf16[512,1024]{1,0:T(8,128)(2,1)} %all-reduce.8.cloned.1.call-done), channel_id=1, source_target_pairs={{0,4},{4,0},{8,12},{12,8},{16,20},{20,16},{24,28},{28,24},{1,5},{5... | collective-permute-start | bytes 3145736 | tf_op jit(solution)/shard_map/ppermute | solution.py:857
  386.3 111.8 %all-reduce.10.cloned.1.call-start = ((), (), s32[]{:S(2)}) async-start(), calls=%async_computation.2 | async-start | bytes 1572864 | tf_op jit(solution)/shard_map/psum | solution.py:853
  437.7 33.3 %collective-permute-start.24 = (bf16[1024,1024]{1,0:T(8,128)(2,1)}, bf16[1024,1024]{1,0:T(8,128)(2,1)}, u32[]{:S(2)}, u32[]{:S(2)}) collective-permute-start(bf16[1024,1024]{1,0:T(8,128)(2,1)} %sum_products.12), channel_id=1, source_target_pairs={{1,0},{0,1},{3,2},{2,3},{5,4},{4,5},{7,6},{6,7},{9,8},{8,9},{11,10... | collective-permute-start | bytes 6291464 | tf_op jit(solution)/shard_map/ppermute | solution.py:723
  453.9 22.6 %collective-permute-start.25 = (bf16[1024,1024]{1,0:T(8,128)(2,1)}, bf16[1024,1024]{1,0:T(8,128)(2,1)}, u32[]{:S(2)}, u32[]{:S(2)}) collective-permute-start(bf16[1024,1024]{1,0:T(8,128)(2,1)} %sum_products.13), channel_id=1, source_target_pairs={{1,0},{0,1},{3,2},{2,3},{5,4},{4,5},{7,6},{6,7},{9,8},{8,9},{11,10... | collective-permute-start | bytes 6291464 | tf_op jit(solution)/shard_map/ppermute | solution.py:723
  454.0 47.0 %collective-permute-start.28 = (bf16[512,1024]{1,0:T(8,128)(2,1)S(1)}, bf16[512,1024]{1,0:T(8,128)(2,1)}, u32[]{:S(2)}, u32[]{:S(2)}) collective-permute-start(bf16[512,1024]{1,0:T(8,128)(2,1)S(1)} %copy-done.34), channel_id=1, source_target_pairs={{0,4},{4,0},{8,12},{12,8},{16,20},{20,16},{24,28},{28,24},{1,5},{5... | collective-permute-start | bytes 3145736 | tf_op jit(solution)/shard_map/ppermute | solution.py:857
  500.5 25.0 %collective-permute-start.26 = (bf16[512,768]{1,0:T(8,128)(2,1)}, bf16[512,768]{1,0:T(8,128)(2,1)S(1)}, u32[]{:S(2)}, u32[]{:S(2)}) collective-permute-start(bf16[512,768]{1,0:T(8,128)(2,1)} %all-reduce.10.cloned.1.call-done), channel_id=1, source_target_pairs={{0,4},{4,0},{8,12},{12,8},{16,20},{20,16},{24,28},{28,24},{1,5},{5... | collective-permute-start | bytes 2359304 | tf_op jit(solution)/shard_map/ppermute | solution.py:857
  (59 other events, 530.0 us)
Sparse Core Ops, SparseCore 0:
  33.3 99.3 all-gather.2
  274.1 52.1 all-reduce.7
  328.7 51.1 all-reduce.5
  386.4 59.7 all-reduce.11
  455.7 42.4 all-reduce.9

commit v8 on v7

--- a/solution.py
+++ b/solution.py
@@ -272,7 +272,7 @@
 
 
 def attend_back(
-    place, queries, keys, values, mixed, upstream, logs, cosines, sines, pair, grads, block=512, chunk=512
+    place, queries, keys, values, mixed, upstream, logs, cosines, sines, pair, grads, block=1024, chunk=512
 ):
     count, columns = queries.shape
     whole = pl.BlockSpec((count, LANES), lambda p, i, _: (0, pair))

time: 540 us -> 540 us (level)
  no operation moved by 1% of the time
where the time goes in v8:
time: 540 us; the launch traced here: 534 us
  Pallas kernels  368 us (68%)
  other arithmetic  52 us (10%)
  waiting for transfers between devices  51.4 us (10%)
  starting transfers between devices  29.5 us (5%)
  local copies, waits for them, and re-layouts  18.3 us (3%)
  between operations  14.7 us (3%)
    pallas_call x4, Pallas kernels, attend_back(): pl.pallas_call(functools.partial(attend_back_kernel, chunk=chunk), grid_s...  110 us
    pallas_call x2, Pallas kernels, feed(): pl.pallas_call(functools.partial(feed_kernel, counts=(len(rows), len(targ...  73.7 us
    pallas_call x8, Pallas kernels, sum_products(): pl.pallas_call(functools.partial(sum_kernel, places=places, dims=tuple(di...  63.7 us
    pallas_call x2, Pallas kernels, attend(): pl.pallas_call(functools.partial(attend_kernel, chunk=chunk), grid_spec=p...  53.2 us
    pallas_call x3, Pallas kernels, norm_back(): pl.pallas_call(lambda *refs, held=len(held): norm_back_kernel(*refs[:3 +...  17.6 us
    psum x4, waiting for transfers between devices, sum_half(): return lax.psum(value, 'dp', axis_index_groups=groups)  16.7 us
    convert_element_type x5, other arithmetic, total(): sum((half(piece, which).astype(F32) for piece in pieces)).astype(BF16)  15.7 us
    pallas_call x2, Pallas kernels, outer(): pl.pallas_call(functools.partial(outer_kernel, count=len(pieces)), grid=(...  14.6 us
  transfers between devices with their start and end apart: 39, of which 13 were waited for; matrix products, arithmetic and copies ran while one was open for 10% of the time, Pallas kernels for 62%

profile of v8, /device:TPU:0, one launch (start us, length us, event | category | flops | bytes accessed | tf_op | source)
XLA Modules:
  0.0 534.1 jit_solution(7763820809141875820)
XLA Ops:
  23.7 6.5 %project_rope.2 = (bf16[2048,256]{1,0:T(8,128)(2,1)S(1)}, bf16[2048,256]{1,0:T(8,128)(2,1)S(1)}, bf16[2048,256]{1,0:T(8,128)(2,1)S(1)}) custom-call(bf16[512,1024]{1,0:T(8,128)(2,1)S(1)} %copy-done.5, bf16[512,1024]{1,0:T(8,128)(2,1)S(1)} %copy-done.6, bf16[512,1024]{1,0:T(8,128)(2,1)} %collective-permute-done.refs_2_, ...), custom_call_target="tpu_custom_call" | custom-call | flops 322122560 | bytes 891289 | tf_op jit(solution)/shard_map/project_rope/pallas_call | solution.py:105
  35.5 26.6 %attention_forward.2 = (bf16[2048,256]{1,0:T(8,128)(2,1)}, f32[2,8,2048]{2,1,0:T(8,128)}) custom-call(s32[2]{0:T(128)} %pad_add_fusion.place_ref, bf16[2048,256]{1,0:T(8,128)(2,1)} %copy-done.13, bf16[2048,256]{1,0:T(8,128)(2,1)} %copy-done.14, bf16[2048,256]{1,0:T(8,128)(2,1)} %copy-done.15), custom_call_target="tpu_custom_call" | custom-call | flops 1717986944 | bytes 419430 | tf_op jit(solution)/shard_map/attention_forward/pallas_call | solution.py:184
  64.0 7.1 %collective-permute-done.3.refs_4_.refs_1_.refs_3_.refs_5_ = bf16[1024,768]{1,0:T(8,128)(2,1)} collective-permute-done((bf16[1024,768]{1,0:T(8,128)(2,1)}, bf16[1024,768]{1,0:T(8,128)(2,1)}, u32[]{:S(2)}, u32[]{:S(2)}) %collective-permute-start.3) | collective-permute-done | bytes 1572896 | tf_op jit(solution)/shard_map/ppermute | solution.py:730
  71.2 7.9 %project_rope.3 = (bf16[2048,256]{1,0:T(8,128)(2,1)S(1)}, bf16[2048,256]{1,0:T(8,128)(2,1)S(1)}, bf16[2048,256]{1,0:T(8,128)(2,1)S(1)}) custom-call(bf16[512,1024]{1,0:T(8,128)(2,1)S(1)} %copy-done.5, bf16[512,1024]{1,0:T(8,128)(2,1)S(1)} %copy-done.7, bf16[512,1024]{1,0:T(8,128)(2,1)} %collective-permute-done.refs_2_, ...), custom_call_target="tpu_custom_call" | custom-call | flops 322122560 | bytes 891289 | tf_op jit(solution)/shard_map/project_rope/pallas_call | solution.py:105
  82.0 26.7 %attention_forward.3 = (bf16[2048,256]{1,0:T(8,128)(2,1)}, f32[2,8,2048]{2,1,0:T(8,128)}) custom-call(s32[2]{0:T(128)} %pad_add_fusion.place_ref, bf16[2048,256]{1,0:T(8,128)(2,1)} %copy-done.16, bf16[2048,256]{1,0:T(8,128)(2,1)} %copy-done.17, bf16[2048,256]{1,0:T(8,128)(2,1)} %copy-done.18), custom_call_target="tpu_custom_call" | custom-call | flops 1717986944 | bytes 419430 | tf_op jit(solution)/shard_map/attention_forward/pallas_call | solution.py:184
  132.9 36.9 %feed_forward.2 = (bf16[2048,1024]{1,0:T(8,128)(2,1)}, bf16[2048,1024]{1,0:T(8,128)(2,1)}, bf16[2048,1024]{1,0:T(8,128)(2,1)}, bf16[1024,1024]{1,0:T(8,128)(2,1)...) custom-call(bf16[512,1024]{1,0:T(8,128)(2,1)} %get-tuple-element.131.refs_0_, ...), custom_call_target="tpu_custom_call" | custom-call | flops 2576980480 | bytes 3355443 | tf_op jit(solution)/shard_map/feed_forward/pallas_call | solution.py:371
  171.2 36.8 %feed_forward.3 = (bf16[2048,1024]{1,0:T(8,128)(2,1)}, bf16[2048,1024]{1,0:T(8,128)(2,1)}, bf16[2048,1024]{1,0:T(8,128)(2,1)}, bf16[1024,1024]{1,0:T(8,128)(2,1)...) custom-call(bf16[512,1024]{1,0:T(8,128)(2,1)} %get-tuple-element.131.refs_0_, ...), custom_call_target="tpu_custom_call" | custom-call | flops 2576980480 | bytes 3355443 | tf_op jit(solution)/shard_map/feed_forward/pallas_call | solution.py:371
  208.0 12.5 %sum_products.10 = bf16[1024,1024]{1,0:T(8,128)(2,1)} custom-call(bf16[2048,1024]{1,0:T(8,128)(2,1)} %get-tuple-element.137.refs_0_, bf16[8,384,1024]{2,1,0:T(8,128)(2,1)} %bitcast.13, bf16[2048,1024]{1,0:T(8,128)(2,1)} %get-tuple-element.130.refs_2_, bf16[8,384,1024]{2,1,0:T(8,128)(2,1)} %bitcast.14, bf16[2048,1024]{1,0:T(8,128)(2,1)} %get-tuple-element.132.refs_4_, ...), custom_call_target="tpu_custom_call" | custom-call | flops 858993472 | bytes 2097152 | tf_op jit(solution)/shard_map/sum_products/pallas_call | solution.py:450
  227.4 13.1 %sum_products.11.refs_3_ = f32[1024,1024]{1,0:T(8,128)} custom-call(bf16[2048,1024]{1,0:T(8,128)(2,1)} %get-tuple-element.137.refs_0_, bf16[8,384,1024]{2,1,0:T(8,128)(2,1)} %bitcast.15, bf16[2048,1024]{1,0:T(8,128)(2,1)} %get-tuple-element.130.refs_2_, bf16[8,384,1024]{2,1,0:T(8,128)(2,1)} %bitcast.16, bf16[2048,1024]{1,0:T(8,128)(2,1)} %get-tuple-element.132.refs_4_, ...), custom_call_target="tpu_custom_call" | custom-call | flops 858993472 | bytes 2097152 | tf_op jit(solution)/shard_map/sum_products/pallas_call | solution.py:450
  255.5 8.2 %branch_backward.1 = (bf16[2048,256]{1,0:T(8,128)(2,1)S(1)}, bf16[2048,256]{1,0:T(8,128)(2,1)S(1)}, bf16[256,1024]{1,0:T(8,128)(2,1)S(1)}, bf16[256,1024]{1,0:T(8,128)(2,1)S(1)}) custom-call(bf16[512,1024]{1,0:T(8,128)(2,1)S(1)} %copy-done.21, bf16[512,1024]{1,0:T(8,128)(2,1)} %get-tuple-element.140.refs_1_, ...), custom_call_target="tpu_custom_call" | custom-call | flops 429496736 | bytes 1258291 | tf_op jit(solution)/shard_map/branch_backward/pallas_call | solution.py:522
  263.8 5.6 %collective-permute-done.9 = bf16[1024,1024]{1,0:T(8,128)(2,1)} collective-permute-done((bf16[1024,1024]{1,0:T(8,128)(2,1)}, bf16[1024,1024]{1,0:T(8,128)(2,1)}, u32[]{:S(2)}, u32[]{:S(2)}) %collective-permute-start.9) | collective-permute-done | bytes 2097184 | tf_op jit(solution)/shard_map/ppermute | solution.py:730
  273.8 27.2 %attention_backward.4.rest_0_ = bf16[3,2048,256]{2,1,0:T(8,128)(2,1)} custom-call(s32[2]{0:T(128)} %pad_add_fusion.place_ref, bf16[2048,256]{1,0:T(8,128)(2,1)} %copy-done.16, bf16[2048,256]{1,0:T(8,128)(2,1)} %copy-done.17, bf16[2048,256]{1,0:T(8,128)(2,1)} %copy-done.18, bf16[2048,256]{1,0:T(8,128)(2,1)} %get-tuple-element.120.refs_2_.refs_6_.out_ref, ...), custom_call_target="tpu_custom_call" | custom-call | flops 1503238528 | bytes 419430 | tf_op jit(solution)/shard_map/attention_backward/pallas_call | solution.py:283
  305.4 27.5 %attention_backward.5.refs_4_.refs_0_.refs_2_ = bf16[3,2048,256]{2,1,0:T(8,128)(2,1)} custom-call(s32[2]{0:T(128)} %pad_add_fusion.place_ref, bf16[2048,256]{1,0:T(8,128)(2,1)} %copy-done.16, bf16[2048,256]{1,0:T(8,128)(2,1)} %copy-done.17, bf16[2048,256]{1,0:T(8,128)(2,1)} %copy-done.18, ...), custom_call_target="tpu_custom_call", output_to_operand_aliasing={{}: (11, {})} | custom-call | flops 1503238528 | bytes 419430 | tf_op jit(solution)/shard_map/attention_backward/pallas_call | solution.py:283
  334.8 7.6 %outer_product.2 = bf16[1024,768]{1,0:T(8,128)(2,1)} custom-call(bf16[512,1024]{1,0:T(8,128)(2,1)S(1)} %copy-done.5, bf16[512,1024]{1,0:T(8,128)(2,1)S(1)} %copy-done.8, bf16[512,1024]{1,0:T(8,128)(2,1)} %collective-permute-done.refs_2_, bf16[512,1024]{1,0:T(8,128)(2,1)} %collective-permute-done.1.refs_3_, bf16[3,2048,256]{2,1,0:T(8,128)(2,1)S(1)} %copy-done.1), custom_call_target="tpu_custom_call" | custom-call | flops 322122560 | bytes 891289 | tf_op jit(solution)/shard_map/outer_product/pallas_call | solution.py:485
  351.0 27.4 %attention_backward.6.rest_0_ = bf16[3,2048,256]{2,1,0:T(8,128)(2,1)} custom-call(s32[2]{0:T(128)} %pad_add_fusion.place_ref, bf16[2048,256]{1,0:T(8,128)(2,1)} %copy-done.13, bf16[2048,256]{1,0:T(8,128)(2,1)} %copy-done.14, bf16[2048,256]{1,0:T(8,128)(2,1)} %copy-done.15, bf16[2048,256]{1,0:T(8,128)(2,1)} %get-tuple-element.113.refs_0_.refs_7_.out_ref, ...), custom_call_target="tpu_custom_call" | custom-call | flops 1503238528 | bytes 419430 | tf_op jit(solution)/shard_map/attention_backward/pallas_call | solution.py:283
  386.2 27.6 %attention_backward.7.refs_4_.refs_6_.refs_8_.refs_10_ = bf16[3,2048,256]{2,1,0:T(8,128)(2,1)} custom-call(s32[2]{0:T(128)} %pad_add_fusion.place_ref, bf16[2048,256]{1,0:T(8,128)(2,1)} %copy-done.13, bf16[2048,256]{1,0:T(8,128)(2,1)} %copy-done.14, bf16[2048,256]{1,0:T(8,128)(2,1)} %copy-done.15, ...), custom_call_target="tpu_custom_call", output_to_operand_aliasing={{}: (11, {})} | custom-call | flops 1503238528 | bytes 419430 | tf_op jit(solution)/shard_map/attention_backward/pallas_call | solution.py:283
  415.7 7.0 %outer_product.3 = bf16[1024,768]{1,0:T(8,128)(2,1)S(1)} custom-call(bf16[512,1024]{1,0:T(8,128)(2,1)S(1)} %copy-done.5, bf16[512,1024]{1,0:T(8,128)(2,1)S(1)} %copy-done.8, bf16[512,1024]{1,0:T(8,128)(2,1)} %collective-permute-done.refs_2_, bf16[512,1024]{1,0:T(8,128)(2,1)} %collective-permute-done.1.refs_3_, bf16[3,2048,256]{2,1,0:T(8,128)(2,1)S(1)} %copy-done), custom_call_target="tpu_custom_call" | custom-call | flops 322122560 | bytes 891289 | tf_op jit(solution)/shard_map/outer_product/pallas_call | solution.py:485
  429.9 7.8 %sum_products.12 = bf16[1024,1024]{1,0:T(8,128)(2,1)} custom-call(bf16[2048,1024]{1,0:T(8,128)(2,1)} %get-tuple-element.182.refs_0_, bf16[8,384,1024]{2,1,0:T(8,128)(2,1)} %bitcast.17, bf16[2048,1024]{1,0:T(8,128)(2,1)} %get-tuple-element.174.refs_2_, bf16[1024,1024]{1,0:T(8,128)(2,1)} %refs_3_.3), custom_call_target="tpu_custom_call" | custom-call | flops 429496736 | bytes 1258291 | tf_op jit(solution)/shard_map/sum_products/pallas_call | solution.py:450
  447.1 6.6 %sum_products.13 = bf16[1024,1024]{1,0:T(8,128)(2,1)} custom-call(bf16[3,2048,256]{2,1,0:T(8,128)(2,1)} %attention_backward.5.refs_4_.refs_0_.refs_2_, bf16[1024,768]{1,0:T(8,128)(2,1)} %collective-permute-done.3.refs_4_.refs_1_.refs_3_.refs_5_, bf16[3,2048,256]{2,1,0:T(8,128)(2,1)} %attention_backward.5.refs_4_.refs_0_.refs_2_, ...), custom_call_target="tpu_custom_call" | custom-call | flops 322122560 | bytes 1048576 | tf_op jit(solution)/shard_map/sum_products/pallas_call | solution.py:450
  455.4 8.0 %sum_products.14 = f32[1024,1024]{1,0:T(8,128)} custom-call(bf16[2048,1024]{1,0:T(8,128)(2,1)} %get-tuple-element.182.refs_0_, bf16[8,384,1024]{2,1,0:T(8,128)(2,1)} %bitcast.18, bf16[2048,1024]{1,0:T(8,128)(2,1)} %get-tuple-element.174.refs_2_, bf16[1024,1024]{1,0:T(8,128)(2,1)} %refs_3_.3), custom_call_target="tpu_custom_call" | custom-call | flops 429496736 | bytes 1258291 | tf_op jit(solution)/shard_map/sum_products/pallas_call | solution.py:450
  463.4 7.4 %sum_products.15.refs_3_ = f32[1024,1024]{1,0:T(8,128)} custom-call(bf16[3,2048,256]{2,1,0:T(8,128)(2,1)} %attention_backward.5.refs_4_.refs_0_.refs_2_, bf16[1024,768]{1,0:T(8,128)(2,1)} %collective-permute-done.3.refs_4_.refs_1_.refs_3_.refs_5_, bf16[3,2048,256]{2,1,0:T(8,128)(2,1)} %attention_backward.5.refs_4_.refs_0_.refs_2_, ...), custom_call_target="tpu_custom_call" | custom-call | flops 322122560 | bytes 1048576 | tf_op jit(solution)/shard_map/sum_products/pallas_call | solution.py:450
  476.3 7.9 %layer_norm_backward.5 = (bf16[1024,1024]{1,0:T(8,128)(2,1)}, f32[2,1024]{1,0:T(2,128)}) custom-call(bf16[1024,1024]{1,0:T(8,128)(2,1)} %refs_0_.7, f32[1024,1024]{1,0:T(8,128)} %get-tuple-element.183.refs_1_, f32[1,1024]{1,0:T(1,128)} %bitcast.25, f32[1024,1024]{1,0:T(8,128)} %sum_products.15.refs_3_, bf16[1024,1024]{1,0:T(8,128)(2,1)} %collective-permute-done.25.refs_4_), custom_call_target="tpu_custom_call" | custom-call | flops 3145728 | bytes 1677721 | tf_op jit(solution)/shard_map/layer_norm_backward/pallas_call | solution.py:637
  484.2 13.7 %all-reduce.10.cloned.1.call-done = bf16[512,768]{1,0:T(8,128)(2,1)} async-done(((bf16[512,768]{1,0:T(8,128)(2,1)}), bf16[512,768]{1,0:T(8,128)(2,1)}) %all-reduce.10.cloned.1.call-update) | async-done | bytes 786448 | tf_op jit(solution)/shard_map/psum | solution.py:853
  518.9 5.7 %collective-permute-done.33 = f32[4,1024]{1,0:T(4,128)S(1)} collective-permute-done((f32[4,1024]{1,0:T(4,128)S(1)}, f32[4,1024]{1,0:T(4,128)S(1)}, u32[]{:S(2)}, u32[]{:S(2)}) %collective-permute-start.33) | collective-permute-done | bytes 16416 | tf_op jit(solution)/shard_map/ppermute | solution.py:686
  (219 shorter events, 150.2 us)
Async XLA Ops:
  7.2 125.5 %all-gather.3.cloned.1.call-start = ((), (), s32[]{:S(2)}) async-start(), calls=%async_computation.3 | async-start | bytes 7077888 | tf_op jit(solution)/shard_map/all_gather | solution.py:758
  10.2 23.0 %collective-permute-start.2 = (bf16[384,1024]{1,0:T(8,128)(2,1)}, bf16[384,1024]{1,0:T(8,128)(2,1)}, u32[]{:S(2)}, u32[]{:S(2)}) collective-permute-start(bf16[384,1024]{1,0:T(8,128)(2,1)} %pad_maximum_fusion), channel_id=1, source_target_pairs={{2,0},{3,1},{0,2},{1,3},{6,4},{7,5},{4,6},{5,7},{10,8},{11,9},{8,1... | collective-permute-start | bytes 2359304 | tf_op jit(solution)/shard_map/ppermute | solution.py:730
  33.2 317.8 %all-reduce.8.cloned.1.call-start = ((), (), s32[]{:S(2)}) async-start(), calls=%async_computation.1 | async-start | bytes 2097152 | tf_op jit(solution)/shard_map/psum | solution.py:853
  33.5 48.6 %collective-permute-start.4 = (bf16[1024,1024]{1,0:T(8,128)(2,1)}, bf16[1024,1024]{1,0:T(8,128)(2,1)}, u32[]{:S(2)}, u32[]{:S(2)}) collective-permute-start(bf16[1024,1024]{1,0:T(8,128)(2,1)} %refs_1_.7), channel_id=1, source_target_pairs={{1,0},{0,1},{3,2},{2,3},{5,4},{4,5},{7,6},{6,7},{9,8},{8,9},{11,10... | collective-permute-start | bytes 6291464 | tf_op jit(solution)/shard_map/ppermute | solution.py:723
  33.6 37.5 %collective-permute-start.3 = (bf16[1024,768]{1,0:T(8,128)(2,1)}, bf16[1024,768]{1,0:T(8,128)(2,1)}, u32[]{:S(2)}, u32[]{:S(2)}) collective-permute-start(bf16[1024,768]{1,0:T(8,128)(2,1)} %copy-done.4), channel_id=1, source_target_pairs={{2,0},{3,1},{0,2},{1,3},{6,4},{7,5},{4,6},{5,7},{10,8},{11,9},{8,1... | collective-permute-start | bytes 4718600 | tf_op jit(solution)/shard_map/ppermute | solution.py:730
  62.0 46.7 %collective-permute-start.5 = (bf16[256,1024]{1,0:T(8,128)(2,1)S(1)}, bf16[256,1024]{1,0:T(8,128)(2,1)S(1)}, u32[]{:S(2)}, u32[]{:S(2)}) collective-permute-start(bf16[256,1024]{1,0:T(8,128)(2,1)S(1)} %copy-done.9), channel_id=1, source_target_pairs={{2,0},{3,1},{0,2},{1,3},{6,4},{7,5},{4,6},{5,7},{10,8},{11,9},{8,1... | collective-permute-start | bytes 1572872 | tf_op jit(solution)/shard_map/ppermute | solution.py:730
  169.8 51.6 %collective-permute-start.10 = (bf16[1024,1024]{1,0:T(8,128)(2,1)}, bf16[1024,1024]{1,0:T(8,128)(2,1)}, u32[]{:S(2)}, u32[]{:S(2)}) collective-permute-start(bf16[1024,1024]{1,0:T(8,128)(2,1)} %get-tuple-element.129), channel_id=1, source_target_pairs={{2,0},{3,1},{0,2},{1,3},{6,4},{7,5},{4,6},{5,7},{10,8},{11,9},{8,1... | collective-permute-start | bytes 6291464 | tf_op jit(solution)/shard_map/ppermute | solution.py:730
  220.6 48.8 %collective-permute-start.9 = (bf16[1024,1024]{1,0:T(8,128)(2,1)}, bf16[1024,1024]{1,0:T(8,128)(2,1)}, u32[]{:S(2)}, u32[]{:S(2)}) collective-permute-start(bf16[1024,1024]{1,0:T(8,128)(2,1)} %get-tuple-element.127), channel_id=1, source_target_pairs={{2,0},{3,1},{0,2},{1,3},{6,4},{7,5},{4,6},{5,7},{10,8},{11,9},{8,1... | collective-permute-start | bytes 6291464 | tf_op jit(solution)/shard_map/ppermute | solution.py:730
  225.9 26.7 %collective-permute-start.12 = (bf16[512,1024]{1,0:T(8,128)(2,1)}, bf16[512,1024]{1,0:T(8,128)(2,1)}, u32[]{:S(2)}, u32[]{:S(2)}) collective-permute-start(bf16[512,1024]{1,0:T(8,128)(2,1)} %get-tuple-element.203), channel_id=1, source_target_pairs={{0,4},{4,0},{8,12},{12,8},{16,20},{20,16},{24,28},{28,24},{1,5},{5... | collective-permute-start | bytes 3145736 | tf_op jit(solution)/shard_map/ppermute | solution.py:841
  252.1 91.0 %collective-permute-start.16 = (bf16[1024,1024]{1,0:T(8,128)(2,1)}, bf16[1024,1024]{1,0:T(8,128)(2,1)}, u32[]{:S(2)}, u32[]{:S(2)}) collective-permute-start(bf16[1024,1024]{1,0:T(8,128)(2,1)} %get-tuple-element.153), channel_id=1, source_target_pairs={{2,0},{3,1},{0,2},{1,3},{6,4},{7,5},{4,6},{5,7},{10,8},{11,9},{8,1... | collective-permute-start | bytes 6291464 | tf_op jit(solution)/shard_map/ppermute | solution.py:730
  272.9 28.1 %collective-permute-start.15 = (bf16[512,1024]{1,0:T(8,128)(2,1)}, bf16[512,1024]{1,0:T(8,128)(2,1)}, u32[]{:S(2)}, u32[]{:S(2)}) collective-permute-start(bf16[512,1024]{1,0:T(8,128)(2,1)} %get-tuple-element.202), channel_id=1, source_target_pairs={{0,4},{4,0},{8,12},{12,8},{16,20},{20,16},{24,28},{28,24},{1,5},{5... | collective-permute-start | bytes 3145736 | tf_op jit(solution)/shard_map/ppermute | solution.py:841
  273.8 106.0 %all-reduce.6.cloned.1.call-start = ((), (), s32[]{:S(2)}) async-start(), calls=%async_computation | async-start | bytes 2097152 | tf_op jit(solution)/shard_map/psum | solution.py:853
  303.8 142.3 %all-reduce.12.cloned.1.call-start = ((), (), s32[]{:S(2)}) async-start(), calls=%async_computation.4 | async-start | bytes 2621440 | tf_op jit(solution)/shard_map/psum | solution.py:853
  303.8 44.4 %collective-permute-start.17 = (bf16[256,1024]{1,0:T(8,128)(2,1)S(1)}, bf16[256,1024]{1,0:T(8,128)(2,1)}, u32[]{:S(2)}, u32[]{:S(2)}) collective-permute-start(bf16[256,1024]{1,0:T(8,128)(2,1)S(1)} %copy-done.25), channel_id=1, source_target_pairs={{2,0},{3,1},{0,2},{1,3},{6,4},{7,5},{4,6},{5,7},{10,8},{11,9},{8,1... | collective-permute-start | bytes 1572872 | tf_op jit(solution)/shard_map/ppermute | solution.py:730
  342.4 80.2 %collective-permute-start.18 = (bf16[1024,768]{1,0:T(8,128)(2,1)}, bf16[1024,768]{1,0:T(8,128)(2,1)}, u32[]{:S(2)}, u32[]{:S(2)}) collective-permute-start(bf16[1024,768]{1,0:T(8,128)(2,1)} %outer_product.2), channel_id=1, source_target_pairs={{2,0},{3,1},{0,2},{1,3},{6,4},{7,5},{4,6},{5,7},{10,8},{11,9},{8,1... | collective-permute-start | bytes 4718600 | tf_op jit(solution)/shard_map/ppermute | solution.py:730
  347.0 36.5 %collective-permute-start.19 = (bf16[512,1024]{1,0:T(8,128)(2,1)}, bf16[512,1024]{1,0:T(8,128)(2,1)}, u32[]{:S(2)}, u32[]{:S(2)}) collective-permute-start(bf16[512,1024]{1,0:T(8,128)(2,1)} %get-tuple-element.199), channel_id=1, source_target_pairs={{0,4},{4,0},{8,12},{12,8},{16,20},{20,16},{24,28},{28,24},{1,5},{5... | collective-permute-start | bytes 3145736 | tf_op jit(solution)/shard_map/ppermute | solution.py:841
  350.2 31.6 %collective-permute-start.20 = (bf16[128,1024]{1,0:T(8,128)(2,1)}, bf16[128,1024]{1,0:T(8,128)(2,1)}, u32[]{:S(2)}, u32[]{:S(2)}) collective-permute-start(bf16[128,1024]{1,0:T(8,128)(2,1)} %get-tuple-element.218), channel_id=1, source_target_pairs={{0,4},{4,0},{8,12},{12,8},{16,20},{20,16},{24,28},{28,24},{1,5},{5... | collective-permute-start | bytes 786440 | tf_op jit(solution)/shard_map/ppermute | solution.py:841
  379.8 46.3 %collective-permute-start.21 = (bf16[512,1024]{1,0:T(8,128)(2,1)}, bf16[512,1024]{1,0:T(8,128)(2,1)}, u32[]{:S(2)}, u32[]{:S(2)}) collective-permute-start(bf16[512,1024]{1,0:T(8,128)(2,1)} %all-reduce.6.cloned.1.call-done), channel_id=1, source_target_pairs={{0,4},{4,0},{8,12},{12,8},{16,20},{20,16},{24,28},{28,24},{1,5},{5... | collective-permute-start | bytes 3145736 | tf_op jit(solution)/shard_map/ppermute | solution.py:857
  381.2 56.5 %collective-permute-start.23 = (bf16[512,1024]{1,0:T(8,128)(2,1)}, bf16[512,1024]{1,0:T(8,128)(2,1)}, u32[]{:S(2)}, u32[]{:S(2)}) collective-permute-start(bf16[512,1024]{1,0:T(8,128)(2,1)} %all-reduce.8.cloned.1.call-done), channel_id=1, source_target_pairs={{0,4},{4,0},{8,12},{12,8},{16,20},{20,16},{24,28},{28,24},{1,5},{5... | collective-permute-start | bytes 3145736 | tf_op jit(solution)/shard_map/ppermute | solution.py:857
  386.1 111.8 %all-reduce.10.cloned.1.call-start = ((), (), s32[]{:S(2)}) async-start(), calls=%async_computation.2 | async-start | bytes 1572864 | tf_op jit(solution)/shard_map/psum | solution.py:853
  437.7 33.1 %collective-permute-start.24 = (bf16[1024,1024]{1,0:T(8,128)(2,1)}, bf16[1024,1024]{1,0:T(8,128)(2,1)}, u32[]{:S(2)}, u32[]{:S(2)}) collective-permute-start(bf16[1024,1024]{1,0:T(8,128)(2,1)} %sum_products.12), channel_id=1, source_target_pairs={{1,0},{0,1},{3,2},{2,3},{5,4},{4,5},{7,6},{6,7},{9,8},{8,9},{11,10... | collective-permute-start | bytes 6291464 | tf_op jit(solution)/shard_map/ppermute | solution.py:723
  453.7 22.6 %collective-permute-start.25 = (bf16[1024,1024]{1,0:T(8,128)(2,1)}, bf16[1024,1024]{1,0:T(8,128)(2,1)}, u32[]{:S(2)}, u32[]{:S(2)}) collective-permute-start(bf16[1024,1024]{1,0:T(8,128)(2,1)} %sum_products.13), channel_id=1, source_target_pairs={{1,0},{0,1},{3,2},{2,3},{5,4},{4,5},{7,6},{6,7},{9,8},{8,9},{11,10... | collective-permute-start | bytes 6291464 | tf_op jit(solution)/shard_map/ppermute | solution.py:723
  453.8 47.0 %collective-permute-start.28 = (bf16[512,1024]{1,0:T(8,128)(2,1)S(1)}, bf16[512,1024]{1,0:T(8,128)(2,1)}, u32[]{:S(2)}, u32[]{:S(2)}) collective-permute-start(bf16[512,1024]{1,0:T(8,128)(2,1)S(1)} %copy-done.34), channel_id=1, source_target_pairs={{0,4},{4,0},{8,12},{12,8},{16,20},{20,16},{24,28},{28,24},{1,5},{5... | collective-permute-start | bytes 3145736 | tf_op jit(solution)/shard_map/ppermute | solution.py:857
  500.2 25.0 %collective-permute-start.26 = (bf16[512,768]{1,0:T(8,128)(2,1)}, bf16[512,768]{1,0:T(8,128)(2,1)S(1)}, u32[]{:S(2)}, u32[]{:S(2)}) collective-permute-start(bf16[512,768]{1,0:T(8,128)(2,1)} %all-reduce.10.cloned.1.call-done), channel_id=1, source_target_pairs={{0,4},{4,0},{8,12},{12,8},{16,20},{20,16},{24,28},{28,24},{1,5},{5... | collective-permute-start | bytes 2359304 | tf_op jit(solution)/shard_map/ppermute | solution.py:857
  (59 other events, 529.9 us)
Sparse Core Ops, SparseCore 0:
  33.3 99.3 all-gather.2
  273.9 52.1 all-reduce.7
  328.5 51.1 all-reduce.5
  386.3 59.7 all-reduce.11
  455.5 42.4 all-reduce.9
